TPU v7x, 256 devices: a whole 4x4x8 slice. The times are simulated.
256 devices in a mesh: band: 32 (over z_hi, y, x), strip: 8 (over z_lo, core).
Axes of the slice: x: 4, y: 4, z: 8 (z_hi: 2, z_lo: 4; z = z_hi * 4 + z_lo), core: 2. Of those that a mesh axis runs over, the one named last changes fastest.
Arguments:
- coeffs: bfloat16 [512, 128, 4096], P('strip', None, 'band'), may hold values from -4.1875 to 4.1875
- hamiltonian: bfloat16 [512, 5, 128, 128], P('strip'), may hold values from -0.15625 to 0.15625
- adjacency: int32 [512, 5], P('strip'), may hold values from 0 to 511, as said below
- occupation: float32 [4096], P('band'), may hold values from 0.1 to 2
Outputs:
- density: float32 [512, 128, 128], P(('strip', 'band'))
Inputs may be any that keep to these rules, and one draw needn't show every extreme that they name: `adjacency`: row e lists element e itself and its four neighbours on the periodic 32 x 16 sheet of elements, numbered row * 16 + column, in an order drawn for each element.
All inputs are finite; a program needn't handle non-finite values.
Results may differ from a plain program's by a relative error of at most 0.019.
Values may be sent and summed in bfloat16 or wider, within the bound.
No kernel may reach another device: no remote copies, remote signals or barrier semaphores. Data moves between devices by JAX's collectives and lax.ppermute only.
A program may use at most 128 MiB of HBM per device.

v0:
```python
import jax
import jax.numpy as jnp
from jax import lax
from jax.sharding import PartitionSpec as P

EY = 16
EXS = 4


def with_halo(block, sides, width):
    for axis, dim in sides:
        count = lax.axis_size(axis)
        forward = [(i, i + 1) for i in range(count - 1)]
        forward.append((count - 1, 0))
        backward = [(target, source) for source, target in forward]
        low = lax.ppermute(
            lax.slice_in_dim(block, block.shape[dim] - width, None, axis=dim), axis, forward
        )
        high = lax.ppermute(lax.slice_in_dim(block, 0, width, axis=dim), axis, backward)
        block = jnp.concatenate([low, block, high], axis=dim)
    return block


def sent_to_all(x, axis):
    copies = jnp.broadcast_to(x, (lax.axis_size(axis), *x.shape))
    return lax.all_to_all(copies, axis, split_axis=0, concat_axis=0, tiled=True)


def joined_along(parts, dim):
    parts = jnp.moveaxis(parts, 0, dim)
    shape = parts.shape
    return parts.reshape(*shape[:dim], shape[dim] * shape[dim + 1], *shape[dim + 2 :])


def gathered_copies(x, axis, dim):
    parts = sent_to_all(x, axis)
    return joined_along(parts, dim)


def items_in_groups(x, axis, split_dim, concat_dim, work, item_dim, out_dim):
    items = jax.tree.leaves(x)[0].shape[item_dim]
    count = 2 if items % 2 == 0 else 1
    done = []
    for k in range(count):
        group = jax.tree.map(
            lambda a: lax.slice_in_dim(
                a, k * (items // count), (k + 1) * (items // count), axis=item_dim
            ),
            x,
        )
        done.append(
            work(
                lax.all_to_all(
                    group, axis, split_axis=split_dim, concat_axis=concat_dim, tiled=True
                )
            )
        )
    return jax.tree.map(lambda *parts: jnp.concatenate(parts, axis=out_dim), *done)


def apply_operator(field_block, hamiltonian, local_index):
    basis = field_block.shape[1]
    columns = field_block.shape[2]
    blocked = field_block.reshape(EXS, EY, basis, columns)
    padded = with_halo(blocked, (("strip", 0),), 1)
    padded = padded.reshape((EXS + 2) * EY, basis, columns)
    picked = jnp.take(padded, local_index, axis=0)
    return jnp.einsum("ejik,ejkb->eib", hamiltonian, picked, preferred_element_type=jnp.float32)


def local(coeffs, hamiltonian, adjacency, occupation):
    strip_index = lax.axis_index("strip")
    ex_total = EXS * lax.axis_size("strip")
    band_count = lax.axis_size("band")
    rel_row = (adjacency // EY - strip_index * EXS + 1) % ex_total
    local_index = rel_row * EY + adjacency % EY
    degree_one = apply_operator(coeffs, hamiltonian, local_index).astype(jnp.bfloat16)
    degree_two = (
        2.0 * apply_operator(degree_one, hamiltonian, local_index) - coeffs.astype(jnp.float32)
    ).astype(jnp.bfloat16)
    filtered = (
        2.0 * apply_operator(degree_two, hamiltonian, local_index) - degree_one.astype(jnp.float32)
    ).astype(jnp.bfloat16)
    elem_count = filtered.shape[0]
    basis = filtered.shape[1]
    local_bands = filtered.shape[2]
    total_bands = local_bands * band_count
    owned_count = elem_count // band_count
    occ_full = gathered_copies(occupation, "band", 0)
    grouped = filtered.reshape(band_count, owned_count, basis, local_bands)

    def gram_items(item_block):
        scaled = (item_block.astype(jnp.float32) * occ_full).astype(jnp.bfloat16)
        return jnp.einsum("zmib,zmjb->mij", scaled, item_block, preferred_element_type=jnp.float32)

    summed = items_in_groups(grouped, "band", 0, 3, gram_items, 1, 0)
    return summed / total_bands


def solution(mesh):
    return jax.shard_map(
        local,
        mesh=mesh,
        in_specs=(
            P("strip", None, "band"),
            P("strip", None, None, None),
            P("strip", None),
            P("band"),
        ),
        out_specs=P(("strip", "band"), None, None),
        check_vma=False,
    )
```

profile of v0, /device:TPU:2, one launch (start us, length us, event | category | flops | bytes accessed | tf_op | source)
XLA Modules:
  0.0 205.8 jit_solution(1472161391297654026)
XLA Ops:
  0.0 1.3 slice_bitcast_fusion.5
  1.3 0.1 collective-permute-start
  1.4 4.1 %collective-permute-start.1 = (bf16[1,16,128,128]{3,2,1,0:T(8,128)(2,1)S(1)}, bf16[1,16,128,128]{3,2,1,0:T(8,128)(2,1)S(1)}, u32[]{:S(2)}, u32[]{:S(2)}) collective-permute-start(bf16[1,16,128,128]{3,2,1,0:T(8,128)(2,1)S(1)} %get-tuple-element.15), channel_id=1, source_target_pairs={{1,0},{2,1},{3,2},{4,3},{5,4},{6,5},{7,6},{0,7},{9,8},{10,9},{11,1... | collective-permute-start | bytes 1572872 | tf_op jit(solution)/shard_map/ppermute | solution.py:19
  5.5 0.7 compare_and_fusion
  6.2 0.1 copy.24
  6.3 0.1 reshape.147
  6.5 0.1 copy.21
  6.6 8.8 %collective-permute-done = bf16[1,16,128,128]{3,2,1,0:T(8,128)(2,1)S(1)} collective-permute-done((bf16[1,16,128,128]{3,2,1,0:T(8,128)(2,1)S(1)}, bf16[1,16,128,128]{3,2,1,0:T(8,128)(2,1)S(1)}, u32[]{:S(2)}, u32[]{:S(2)}) %collective-permute-start) | collective-permute-done | bytes 524320 | tf_op jit(solution)/shard_map/ppermute | solution.py:16
  15.4 0.0 copy-start.3
  15.4 0.0 collective-permute-done.1
  15.4 0.8 copy-done.3
  16.2 0.0 copy-start.4
  16.2 0.8 copy-done.4
  17.0 2.2 %pad_maximum_fusion = bf16[6,16,128,128]{3,2,1,0:T(8,128)(2,1)S(1)} fusion(bf16[1,16,128,128]{3,2,1,0:T(8,128)(2,1)} %copy-done.4, bf16[4,16,128,128]{3,2,1,0:T(8,128)(2,1)} %bitcast.88, bf16[1,16,128,128]{3,2,1,0:T(8,128)(2,1)} %copy-done.3), kind=kLoop, calls=%fused_computation.22 | loop fusion | flops 3145728 | bytes 6291456 | tf_op jit(solution)/shard_map/concatenate | solution.py:20
  19.2 10.7 %gather_fusion = bf16[320,128,128]{2,1,0:T(8,128)(2,1)} fusion(bf16[96,128,128]{2,1,0:T(8,128)(2,1)S(1)} %bitcast.85, s32[1024]{0:T(1024)S(1)} %pad_clamp_fusion), kind=kCustom, calls=%fused_computation.clone | custom fusion | bytes 20972800 | tf_op jit(solution)/shard_map/jit(_take)/gather | solution.py:67
  29.9 14.5 %copy.25 = bf16[64,5,128,128]{2,3,1,0:T(8,128)(2,1)} copy(bf16[64,5,128,128]{3,2,1,0:T(8,128)(2,1)} %bitcast.87) | data formatting | bytes 20971520 | tf_op jit(solution)/shard_map/jit(_take)/gather | solution.py:67
  44.4 0.0 copy-start
  44.4 9.1 %bitcast_convert_fusion = bf16[64,128,128]{2,1,0:T(8,128)(2,1)S(1)} fusion(bf16[64,5,128,128]{3,2,1,0:T(8,128)(2,1)} %param.7, bf16[64,5,128,128]{2,3,1,0:T(8,128)(2,1)} %copy.25, pred[64,5]{1,0:T(8,128)(4,1)S(1)} %copy.21), kind=kOutput, calls=%fused_computation.21 | convolution fusion | flops 1348468736 | bytes 23068992 | tf_op jit(solution)/shard_map/ejik,ejkb->eib/dot_general | solution.py:68
  53.6 0.0 copy-start.1
  53.6 1.3 copy-done.1
  54.9 1.1 slice_bitcast_fusion.3
  56.0 1.4 collective-permute-start.2
  57.4 2.1 %collective-permute-start.3 = (bf16[1,16,128,128]{2,3,1,0:T(8,128)(2,1)}, bf16[1,16,128,128]{2,3,1,0:T(8,128)(2,1)S(1)}, u32[]{:S(2)}, u32[]{:S(2)}) collective-permute-start(bf16[1,16,128,128]{2,3,1,0:T(8,128)(2,1)} %get-tuple-element.13), channel_id=1, source_target_pairs={{1,0},{2,1},{3,2},{4,3},{5,4},{6,5},{7,6},{0,7},{9,8},{10,9},{11,1... | collective-permute-start | bytes 1572872 | tf_op jit(solution)/shard_map/ppermute | solution.py:19
  59.5 0.0 copy-done
  59.5 3.0 %copy.27 = bf16[64,128,128]{1,2,0:T(8,128)(2,1)} copy(bf16[64,128,128]{2,1,0:T(8,128)(2,1)S(1)} %copy-done) | data formatting | bytes 4194304 | tf_op args[0]
  62.5 6.5 %collective-permute-done.2 = bf16[1,16,128,128]{2,3,1,0:T(8,128)(2,1)S(1)} collective-permute-done((bf16[1,16,128,128]{2,3,1,0:T(8,128)(2,1)}, bf16[1,16,128,128]{2,3,1,0:T(8,128)(2,1)S(1)}, u32[]{:S(2)}, u32[]{:S(2)}) %collective-permute-start.2) | collective-permute-done | bytes 524320 | tf_op jit(solution)/shard_map/ppermute | solution.py:16
  69.0 0.0 copy-start.7
  69.0 0.4 collective-permute-done.3
  69.4 0.4 copy-done.7
  69.8 0.0 copy-start.8
  69.8 0.8 copy-done.8
  70.6 2.2 %pad_maximum_fusion.1 = bf16[6,16,128,128]{2,3,1,0:T(8,128)(2,1)S(1)} fusion(bf16[1,16,128,128]{2,3,1,0:T(8,128)(2,1)} %copy-done.8, bf16[4,16,128,128]{2,3,1,0:T(8,128)(2,1)} %bitcast.92, bf16[1,16,128,128]{2,3,1,0:T(8,128)(2,1)} %copy-done.7), kind=kLoop, calls=%fused_computation.23 | loop fusion | flops 3145728 | bytes 6291456 | tf_op jit(solution)/shard_map/concatenate | solution.py:20
  72.8 10.7 %gather_fusion.1 = bf16[320,128,128]{1,2,0:T(8,128)(2,1)} fusion(bf16[96,128,128]{1,2,0:T(8,128)(2,1)S(1)} %bitcast.86, s32[1024]{0:T(1024)S(1)} %pad_clamp_fusion), kind=kCustom, calls=%fused_computation.1.clone | custom fusion | bytes 20972800 | tf_op jit(solution)/shard_map/jit(_take)/gather | solution.py:67
  83.5 0.0 copy-start.9
  83.5 9.5 %fusion.13 = bf16[64,128,128]{1,2,0:T(8,128)(2,1)S(1)} fusion(bf16[64,128,128]{1,2,0:T(8,128)(2,1)} %copy.27, bf16[64,5,128,128]{3,2,1,0:T(8,128)(2,1)} %param.7, bf16[64,5,128,128]{2,3,1,0:T(8,128)(2,1)} %bitcast.90, pred[64,5]{1,0:T(8,128)(4,1)S(1)} %copy.21), kind=kOutput, calls=%fused_computation.19 | convolution fusion | flops 1351614464 | bytes 25166144 | tf_op jit(solution)/shard_map/ejik,ejkb->eib/dot_general | solution.py:68
  93.0 0.0 copy-start.2
  93.1 1.1 slice_bitcast_fusion.1
  94.2 2.1 %collective-permute-start.4 = (bf16[1,16,128,128]{2,3,1,0:T(8,128)(2,1)}, bf16[1,16,128,128]{2,3,1,0:T(8,128)(2,1)S(1)}, u32[]{:S(2)}, u32[]{:S(2)}) collective-permute-start(bf16[1,16,128,128]{2,3,1,0:T(8,128)(2,1)} %get-tuple-element.10), channel_id=1, source_target_pairs={{0,1},{1,2},{2,3},{3,4},{4,5},{5,6},{6,7},{7,0},{8,9},{9,10},{10,1... | collective-permute-start | bytes 1572872 | tf_op jit(solution)/shard_map/ppermute | solution.py:16
  96.3 1.5 collective-permute-start.5
  97.7 0.0 copy-done.9
  97.7 0.6 broadcast_in_dim.12
  98.3 16.9 %all-to-all-start.1 = ((f32[32,1,128]{2,1,0:T(1,128)}), f32[32,1,128]{2,1,0:T(1,128)S(1)}, u32[]{:S(2)}, u32[]{:S(2)}) async-start(f32[32,1,128]{2,1,0:T(1,128)} %broadcast_in_dim.12), calls=%async_computation.1 | async-start | bytes 32768 | tf_op jit(solution)/shard_map/all_to_all | solution.py:26
  115.2 0.0 collective-permute-done.4
  115.3 0.0 copy-start.5
  115.3 0.0 collective-permute-done.5
  115.3 0.0 copy-done.2
  115.3 0.8 copy-done.5
  116.1 0.0 copy-start.6
  116.1 0.8 copy-done.6
  116.9 2.2 %pad_maximum_fusion.2 = bf16[6,16,128,128]{2,3,1,0:T(8,128)(2,1)S(1)} fusion(bf16[1,16,128,128]{2,3,1,0:T(8,128)(2,1)} %copy-done.6, bf16[4,16,128,128]{2,3,1,0:T(8,128)(2,1)} %bitcast.93, bf16[1,16,128,128]{2,3,1,0:T(8,128)(2,1)} %copy-done.5), kind=kLoop, calls=%fused_computation.24 | loop fusion | flops 3145728 | bytes 6291456 | tf_op jit(solution)/shard_map/concatenate | solution.py:20
  119.1 10.7 %gather_fusion.2 = bf16[320,128,128]{1,2,0:T(8,128)(2,1)} fusion(bf16[96,128,128]{1,2,0:T(8,128)(2,1)S(1)} %bitcast.84, s32[1024]{0:T(1024)S(1)} %pad_clamp_fusion), kind=kCustom, calls=%fused_computation.2.clone | custom fusion | bytes 20972800 | tf_op jit(solution)/shard_map/jit(_take)/gather | solution.py:67
  129.8 9.5 %fusion.12 = bf16[64,128,128]{1,2,0:T(8,128)(2,1)S(1)} fusion(bf16[64,5,128,128]{3,2,1,0:T(8,128)(2,1)} %param.7, bf16[64,5,128,128]{2,3,1,0:T(8,128)(2,1)} %bitcast.89, pred[64,5]{1,0:T(8,128)(4,1)S(1)} %copy.21, bf16[64,128,128]{2,1,0:T(8,128)(2,1)} %copy-done.1), kind=kOutput, calls=%fused_computation.16 | convolution fusion | flops 1351614464 | bytes 25166144 | tf_op jit(solution)/shard_map/ejik,ejkb->eib/dot_general | solution.py:68
  139.3 0.1 fusion.39
  139.5 1.3 copy.35
  140.8 0.0 all-to-all-done.1
  140.8 12.2 %all-to-all-start.2 = ((bf16[32,1,128,128]{3,2,1,0:T(8,128)(2,1)}), bf16[32,1,128,128]{3,2,1,0:T(8,128)(2,1)S(1)}, u32[]{:S(2)}, u32[]{:S(2)}) async-start(bf16[32,1,128,128]{3,2,1,0:T(8,128)(2,1)} %copy.35), calls=%async_computation.2 | async-start | bytes 2097152 | tf_op jit(solution)/shard_map/all_to_all | solution.py:53
  153.0 1.3 copy.34
  154.4 20.9 %all-to-all-done.2 = bf16[32,1,128,128]{3,2,1,0:T(8,128)(2,1)S(1)} async-done(((bf16[32,1,128,128]{3,2,1,0:T(8,128)(2,1)}), bf16[32,1,128,128]{3,2,1,0:T(8,128)(2,1)S(1)}, u32[]{:S(2)}, u32[]{:S(2)}) %all-to-all-start.2) | async-done | bytes 1048608 | tf_op jit(solution)/shard_map/all_to_all | solution.py:53
  175.2 9.8 %all-to-all-start = ((bf16[32,1,128,128]{3,2,1,0:T(8,128)(2,1)}), bf16[32,1,128,128]{3,2,1,0:T(8,128)(2,1)S(1)}, u32[]{:S(2)}, u32[]{:S(2)}) async-start(bf16[32,1,128,128]{3,2,1,0:T(8,128)(2,1)} %copy.34), calls=%async_computation | async-start | bytes 2097152 | tf_op jit(solution)/shard_map/all_to_all | solution.py:53
  185.1 0.4 convolution_bitcast_fusion
  185.5 19.2 %all-to-all-done = bf16[32,1,128,128]{3,2,1,0:T(8,128)(2,1)S(1)} async-done(((bf16[32,1,128,128]{3,2,1,0:T(8,128)(2,1)}), bf16[32,1,128,128]{3,2,1,0:T(8,128)(2,1)S(1)}, u32[]{:S(2)}, u32[]{:S(2)}) %all-to-all-start) | async-done | bytes 1048608 | tf_op jit(solution)/shard_map/all_to_all | solution.py:53
  204.7 0.5 convolution_bitcast_fusion.1
  205.2 0.7 maximum_multiply_fusion
  (1 shorter events, 0.0 us)
Async XLA Ops:
  1.3 14.1 %collective-permute-start = (bf16[1,16,128,128]{3,2,1,0:T(8,128)(2,1)S(1)}, bf16[1,16,128,128]{3,2,1,0:T(8,128)(2,1)S(1)}, u32[]{:S(2)}, u32[]{:S(2)}) collective-permute-start(bf16[1,16,128,128]{3,2,1,0:T(8,128)(2,1)S(1)} %get-tuple-element.14), channel_id=1, source_target_pairs={{0,1},{1,2},{2,3},{3,4},{4,5},{5,6},{6,7},{7,0},{8,9},{9,10},{10,1... | collective-permute-start | bytes 1572872 | tf_op jit(solution)/shard_map/ppermute | solution.py:16
  1.4 14.0 %collective-permute-start.1 = (bf16[1,16,128,128]{3,2,1,0:T(8,128)(2,1)S(1)}, bf16[1,16,128,128]{3,2,1,0:T(8,128)(2,1)S(1)}, u32[]{:S(2)}, u32[]{:S(2)}) collective-permute-start(bf16[1,16,128,128]{3,2,1,0:T(8,128)(2,1)S(1)} %get-tuple-element.15), channel_id=1, source_target_pairs={{1,0},{2,1},{3,2},{4,3},{5,4},{6,5},{7,6},{0,7},{9,8},{10,9},{11,1... | collective-permute-start | bytes 1572872 | tf_op jit(solution)/shard_map/ppermute | solution.py:19
  15.4 0.8 copy-start.3
  16.2 0.8 copy-start.4
  44.4 15.1 %copy-start = (bf16[64,128,128]{2,1,0:T(8,128)(2,1)S(1)}, bf16[64,128,128]{2,1,0:T(8,128)(2,1)}, u32[]{:S(2)}) copy-start(bf16[64,128,128]{2,1,0:T(8,128)(2,1)} %param.6) | copy-start | bytes 6291460
  53.6 1.3 copy-start.1
  56.0 13.0 %collective-permute-start.2 = (bf16[1,16,128,128]{2,3,1,0:T(8,128)(2,1)}, bf16[1,16,128,128]{2,3,1,0:T(8,128)(2,1)S(1)}, u32[]{:S(2)}, u32[]{:S(2)}) collective-permute-start(bf16[1,16,128,128]{2,3,1,0:T(8,128)(2,1)} %get-tuple-element.12), channel_id=1, source_target_pairs={{0,1},{1,2},{2,3},{3,4},{4,5},{5,6},{6,7},{7,0},{8,9},{9,10},{10,1... | collective-permute-start | bytes 1572872 | tf_op jit(solution)/shard_map/ppermute | solution.py:16
  57.4 12.0 %collective-permute-start.3 = (bf16[1,16,128,128]{2,3,1,0:T(8,128)(2,1)}, bf16[1,16,128,128]{2,3,1,0:T(8,128)(2,1)S(1)}, u32[]{:S(2)}, u32[]{:S(2)}) collective-permute-start(bf16[1,16,128,128]{2,3,1,0:T(8,128)(2,1)} %get-tuple-element.13), channel_id=1, source_target_pairs={{1,0},{2,1},{3,2},{4,3},{5,4},{6,5},{7,6},{0,7},{9,8},{10,9},{11,1... | collective-permute-start | bytes 1572872 | tf_op jit(solution)/shard_map/ppermute | solution.py:19
  69.0 0.8 copy-start.7
  69.8 0.8 copy-start.8
  83.5 14.2 %copy-start.9 = (f32[128]{0:T(128)S(1)}, f32[128]{0:T(128)}, u32[]{:S(2)}) copy-start(f32[128]{0:T(128)} %param.9) | copy-start | bytes 1540
  93.0 22.2 %copy-start.2 = (bf16[64,128,128]{1,2,0:T(8,128)(2,1)}, bf16[64,128,128]{1,2,0:T(8,128)(2,1)S(1)}, u32[]{:S(2)}) copy-start(bf16[64,128,128]{1,2,0:T(8,128)(2,1)S(1)} %fusion.13) | copy-start | bytes 6291460
  94.2 21.1 %collective-permute-start.4 = (bf16[1,16,128,128]{2,3,1,0:T(8,128)(2,1)}, bf16[1,16,128,128]{2,3,1,0:T(8,128)(2,1)S(1)}, u32[]{:S(2)}, u32[]{:S(2)}) collective-permute-start(bf16[1,16,128,128]{2,3,1,0:T(8,128)(2,1)} %get-tuple-element.10), channel_id=1, source_target_pairs={{0,1},{1,2},{2,3},{3,4},{4,5},{5,6},{6,7},{7,0},{8,9},{9,10},{10,1... | collective-permute-start | bytes 1572872 | tf_op jit(solution)/shard_map/ppermute | solution.py:16
  96.3 19.0 %collective-permute-start.5 = (bf16[1,16,128,128]{2,3,1,0:T(8,128)(2,1)}, bf16[1,16,128,128]{2,3,1,0:T(8,128)(2,1)S(1)}, u32[]{:S(2)}, u32[]{:S(2)}) collective-permute-start(bf16[1,16,128,128]{2,3,1,0:T(8,128)(2,1)} %get-tuple-element.11), channel_id=1, source_target_pairs={{1,0},{2,1},{3,2},{4,3},{5,4},{6,5},{7,6},{0,7},{9,8},{10,9},{11,1... | collective-permute-start | bytes 1572872 | tf_op jit(solution)/shard_map/ppermute | solution.py:19
  98.3 42.5 %all-to-all-start.1 = ((f32[32,1,128]{2,1,0:T(1,128)}), f32[32,1,128]{2,1,0:T(1,128)S(1)}, u32[]{:S(2)}, u32[]{:S(2)}) async-start(f32[32,1,128]{2,1,0:T(1,128)} %broadcast_in_dim.12), calls=%async_computation.1 | async-start | bytes 32768 | tf_op jit(solution)/shard_map/all_to_all | solution.py:26
  115.3 0.8 copy-start.5
  116.1 0.8 copy-start.6
  140.8 34.4 %all-to-all-start.2 = ((bf16[32,1,128,128]{3,2,1,0:T(8,128)(2,1)}), bf16[32,1,128,128]{3,2,1,0:T(8,128)(2,1)S(1)}, u32[]{:S(2)}, u32[]{:S(2)}) async-start(bf16[32,1,128,128]{3,2,1,0:T(8,128)(2,1)} %copy.35), calls=%async_computation.2 | async-start | bytes 2097152 | tf_op jit(solution)/shard_map/all_to_all | solution.py:53
  175.2 29.5 %all-to-all-start = ((bf16[32,1,128,128]{3,2,1,0:T(8,128)(2,1)}), bf16[32,1,128,128]{3,2,1,0:T(8,128)(2,1)S(1)}, u32[]{:S(2)}, u32[]{:S(2)}) async-start(bf16[32,1,128,128]{3,2,1,0:T(8,128)(2,1)} %copy.34), calls=%async_computation | async-start | bytes 2097152 | tf_op jit(solution)/shard_map/all_to_all | solution.py:53
where the time goes:
time: 207 us; the launch traced here: 206 us
  local copies, waits for them, and re-layouts  62.5 us (30%)
  waiting for transfers between devices  55.8 us (27%)
  starting transfers between devices  50.3 us (24%)
  matrix products  29.1 us (14%)
  other arithmetic  7.99 us (4%)
    gather x4, local copies, waits for them, and re-layouts, apply_operator(): picked = jnp.take(padded, local_index, axis=0)  46.7 us
    all_to_all x2, waiting for transfers between devices, items_in_groups(): lax.all_to_all(group, axis, split_axis=split_dim, concat_axis=concat_dim,...  40.1 us
    dot_general x3, matrix products, apply_operator(): jnp.einsum('ejik,ejkb->eib', hamiltonian, picked, preferred_element_type=...  28.2 us
    all_to_all x2, starting transfers between devices, items_in_groups(): lax.all_to_all(group, axis, split_axis=split_dim, concat_axis=concat_dim,...  22 us
    all_to_all x1, starting transfers between devices, sent_to_all(): return lax.all_to_all(copies, axis, split_axis=0, concat_axis=0, tiled=True)  16.9 us
    ppermute x3, waiting for transfers between devices, with_halo(): lax.ppermute(lax.slice_in_dim(block, block.shape[dim] - width, None, axis...  15.3 us
    unnamed x23, local copies, waits for them, and re-layouts  11.3 us
    ppermute x3, starting transfers between devices, with_halo(): lax.ppermute(lax.slice_in_dim(block, 0, width, axis=dim), axis, backward)  7.71 us
  transfers between devices with their start and end apart: 9, of which 5 were waited for; matrix products, arithmetic and copies ran while one was open for 15% of the time, Pallas kernels for 0%

commit v1 on v0

v1 whole, which is shorter than its diff:
```python
import functools

import jax
import jax.numpy as jnp
from jax import lax
from jax.experimental import pallas as pl
from jax.experimental.pallas import tpu as pltpu
from jax.sharding import PartitionSpec as P

EY = 16
EXS = 4
EX = 32
NB = 128
NBAND = 4096
XS = 4
YS = 4

BF = jnp.bfloat16
F32 = jnp.float32
VMEM = pltpu.VMEM


def struct(shape, dtype):
    return jax.ShapeDtypeStruct(shape, dtype)


def vmem_specs(count):
    return [pl.BlockSpec(memory_space=VMEM)] * count


def dot(a, b):
    return jnp.dot(a, b, preferred_element_type=F32)


def gram(a, b):
    return lax.dot_general(a, b, (((1,), (1,)), ((), ())), preferred_element_type=F32)


def block_indices(adjacency, strip_index):
    local = jnp.arange(EXS * EY, dtype=jnp.int32)
    row = strip_index * EXS + local // EY
    col = local % EY
    wanted = jnp.stack(
        [
            row * EY + col,
            (row + 1) % EX * EY + col,
            (row + EX - 1) % EX * EY + col,
            row * EY + (col + 1) % EY,
            row * EY + (col + EY - 1) % EY,
        ],
        axis=1,
    )
    hit = adjacency[:, None, :] == wanted[:, :, None]
    slot = jnp.sum(jnp.where(hit, jnp.arange(5, dtype=jnp.int32), 0), axis=2)
    return (local[:, None] * 5 + slot).reshape(-1)


def sweep_kernel(level, index_ref, *refs):
    if level == 1:
        v_ref, h_ref, mid_ref, part0, part3, far0, far3, h, sem = refs
        rows = [v_ref.at[pl.ds(r * EY, EY)] for r in range(EXS)]
        before = None
    else:
        v0, vm, v3, p0, pm, p3, h_ref, mid_ref, part0, part3, h, sem = refs
        rows = [v0, vm.at[pl.ds(0, EY)], vm.at[pl.ds(EY, EY)], v3]
        before = [p0, pm.at[pl.ds(0, EY)], pm.at[pl.ds(EY, EY)], p3]
    per_row = 5 * EY
    copies = [
        pltpu.make_async_copy(
            h_ref.at[pl.ds(r * per_row, per_row)], h.at[pl.ds(r * per_row, per_row)], sem.at[r]
        )
        for r in range(EXS)
    ]
    for copy in copies:
        copy.start()
    for r in range(EXS):
        copies[r].wait()

        def element(c, carry, r=r):
            at = (r * EY + c) * 5
            right = lax.rem(c + 1, EY)
            left = lax.rem(c + EY - 1, EY)
            terms = [(0, rows[r][c]), (3, rows[r][right]), (4, rows[r][left])]
            if r + 1 < EXS:
                terms.append((1, rows[r + 1][c]))
            if r > 0:
                terms.append((2, rows[r - 1][c]))
            a = jnp.concatenate([h[index_ref[at + k]] for k, _ in terms], axis=1)
            b = jnp.concatenate([v for _, v in terms], axis=0)
            total = dot(a, b)
            if before is not None:
                total = 2.0 * total - before[r][c].astype(F32)
            if r == 0:
                part0[c] = total
                if level == 1:
                    far0[c] = h[index_ref[at + 2]]
            elif r == EXS - 1:
                part3[c] = total
                if level == 1:
                    far3[c] = h[index_ref[at + 1]]
            else:
                mid_ref[(r - 1) * EY + c] = total.astype(BF)
            return carry

        lax.fori_loop(0, EY, element, 0, unroll=2)


def sweep(level, index, fields, blocks):
    row = (EY, NB, NB)
    outs = [struct((2 * EY, NB, NB), BF), struct(row, F32), struct(row, F32)]
    if level == 1:
        outs += [struct(row, BF), struct(row, BF)]
    count = 64 * 5
    return pl.pallas_call(
        functools.partial(sweep_kernel, level),
        out_shape=outs,
        in_specs=[pl.BlockSpec(memory_space=pltpu.SMEM)]
        + vmem_specs(len(fields))
        + [pl.BlockSpec(memory_space=pl.ANY)],
        out_specs=vmem_specs(len(outs)),
        scratch_shapes=[VMEM((count, NB, NB), BF), pltpu.SemaphoreType.DMA((EXS,))],
        compiler_params=pltpu.CompilerParams(vmem_limit_bytes=40 << 20),
        name=f"sweep{level}",
    )(index, *fields, blocks)


def edge_kernel(scale, part_ref, far_ref, halo_ref, out_ref):
    def element(c, carry):
        out_ref[c] = (part_ref[c] + scale * dot(far_ref[c], halo_ref[c])).astype(BF)
        return carry

    lax.fori_loop(0, EY, element, 0, unroll=4)


def edge(level, part, far, halo):
    return pl.pallas_call(
        functools.partial(edge_kernel, 1.0 if level == 1 else 2.0),
        out_shape=struct((EY, NB, NB), BF),
        in_specs=vmem_specs(3),
        out_specs=pl.BlockSpec(memory_space=VMEM),
        compiler_params=pltpu.CompilerParams(vmem_limit_bytes=16 << 20),
        name=f"edge{level}",
    )(part, far, halo)


def element_of(x, k):
    return (k // 2) * 8 + 2 * x + k % 2


def scaled_kernel(rows, me_ref, root_ref, *refs):
    srcs, outs = refs[: len(rows)], refs[len(rows) :]
    root = root_ref[...]
    for s in range(XS):
        x = lax.rem(me_ref[0] + s, XS)
        for n, offset in enumerate(rows):
            for k in range(4):
                value = srcs[n][offset + element_of(x, k)].astype(F32)
                outs[s][n * 4 + k] = (value * root).astype(BF)


def scaled(me, root, parts):
    n = len(parts)
    out = struct((4 * n, NB, NB), BF)
    return pl.pallas_call(
        functools.partial(scaled_kernel, [offset for _, offset in parts]),
        out_shape=[out] * XS,
        in_specs=[pl.BlockSpec(memory_space=pltpu.SMEM)] + vmem_specs(1 + n),
        out_specs=vmem_specs(XS),
        compiler_params=pltpu.CompilerParams(vmem_limit_bytes=16 << 20),
        name="scaled",
    )(me, root, *[array for array, _ in parts])


def grams(me, pieces):
    out = struct((2, NB, NB), BF)
    return pl.pallas_call(
        gram_sorted_kernel,
        out_shape=[struct((2, NB, NB), F32), out, out, out],
        in_specs=[pl.BlockSpec(memory_space=pltpu.SMEM)] + vmem_specs(len(pieces)),
        out_specs=vmem_specs(YS),
        compiler_params=pltpu.CompilerParams(vmem_limit_bytes=16 << 20),
        name="grams",
    )(me, *pieces)


def gram_sorted_kernel(me_ref, *refs):
    srcs, outs = refs[:XS], refs[XS:]
    for t in range(YS):
        y = lax.rem(me_ref[1] + t, YS)
        for k in range(2):
            a = jnp.concatenate([s[y * 2 + k] for s in srcs], axis=1)
            outs[t][k] = (gram(a, a) * (1.0 / NBAND)).astype(outs[t].dtype)


def shifted(array, along, shift):
    step, size = (1, XS) if along == "x" else (XS, YS)
    pairs = []
    for b in range(2 * XS * YS):
        at = b // step % size
        pairs.append((b, b + ((at + shift) % size - at) * step))
    return lax.ppermute(array, "band", pairs)


def exchanged(pieces, along):
    return [pieces[0]] + [shifted(pieces[s], along, s) for s in (1, 2, 3)]


def across(array, senders):
    half = XS * YS
    pairs = [(b, (b + half) % (2 * half)) for b in range(2 * half) if senders(b)]
    return lax.ppermute(array, "band", pairs)


def outer_owner(b):
    return (b // 16 == 0) == (b // 4 % 4 < 2)


def local(coeffs, hamiltonian, adjacency, occupation):
    strip_index = lax.axis_index("strip")
    band_index = lax.axis_index("band")
    count = lax.axis_size("strip")
    ahead = [(i, (i + 1) % count) for i in range(count)]
    back = [(j, i) for i, j in ahead]
    send_up = lambda a: lax.ppermute(a, "strip", ahead)
    send_down = lambda a: lax.ppermute(a, "strip", back)

    low = send_up(coeffs[3 * EY :])
    high = send_down(coeffs[:EY])
    index = block_indices(adjacency, strip_index)
    blocks = hamiltonian.reshape(-1, NB, NB)
    me = jnp.stack([band_index % XS, band_index // XS % YS]).astype(jnp.int32)
    root = jnp.sqrt(occupation).reshape(1, NB)
    c0, cm, c3 = coeffs[:EY], coeffs[EY : 3 * EY], coeffs[3 * EY :]

    m1, part0, part3, far0, far3 = sweep(1, index, [coeffs], blocks)
    u0 = edge(1, part0, far0, low)
    high1 = send_down(u0)
    u3 = edge(1, part3, far3, high)
    low1 = send_up(u3)
    m2, part0, part3 = sweep(2, index, [u0, m1, u3, c0, cm, c3], blocks)
    w3 = edge(2, part3, far3, high1)
    low2 = send_up(w3)
    w0 = edge(2, part0, far0, low1)
    high2 = send_down(w0)
    m3, part0, part3 = sweep(3, index, [w0, m2, w3, u0, m1, u3], blocks)

    inner = grams(me, exchanged(scaled(me, root, [(m3, EY), (m3, 0)]), "x"))
    inner = exchanged(inner, "y")
    inner = sum(a.astype(F32) for a in inner)
    inner_in = across(inner, outer_owner)
    f0 = edge(3, part0, far0, low2)
    f3 = edge(3, part3, far3, high2)
    outer = grams(me, exchanged(scaled(me, root, [(f0, 0), (f3, 0)]), "x"))
    outer = exchanged(outer, "y")
    outer = sum(a.astype(F32) for a in outer)
    outer_in = across(outer, lambda b: not outer_owner(b))
    mine = (band_index // 16 == 0) == (band_index // 4 % 4 < 2)
    return jnp.where(mine, outer + outer_in, inner + inner_in)


def solution(mesh):
    return jax.shard_map(
        local,
        mesh=mesh,
        in_specs=(
            P("strip", None, "band"),
            P("strip", None, None, None),
            P("strip", None),
            P("band"),
        ),
        out_specs=P(("strip", "band"), None, None),
        check_vma=False,
    )
```

time: 207 us -> 109 us (0.53)
  local copies, waits for them, and re-layouts: 62.5 us -> 6.23 us
  Pallas kernels: 0 us -> 44.9 us
  waiting for transfers between devices: 55.8 us -> 19.7 us
  matrix products: 29.1 us -> 0 us
  starting transfers between devices: 50.3 us -> 36.8 us
  other arithmetic: 7.99 us -> 0.89 us
    gather x4 -> x0, local copies, waits for them, and re-layouts: 46.7 us -> none  [apply_operator(): picked = jnp.take(padded, local_index, axis=0)]
    pallas_call x0 -> x13, Pallas kernels: none -> 44.9 us  [the longest x3 31.1 us: sweep(): pl.pallas_call(functools.partial(sweep_kernel, level), out_shape=outs, in...]
    all_to_all x3 -> x0, waiting for transfers between devices: 40.1 us -> none  [the longest x2 40.1 us: items_in_groups(): lax.all_to_all(group, axis, split_axis=split_dim, concat_axis=concat_dim,...]
    all_to_all x3 -> x0, starting transfers between devices: 38.9 us -> none  [the longest x2 22 us: items_in_groups(): lax.all_to_all(group, axis, split_axis=split_dim, concat_axis=concat_dim,...]
    dot_general x5 -> x0, matrix products: 29.1 us -> none  [the longest x3 28.2 us: apply_operator(): jnp.einsum('ejik,ejkb->eib', hamiltonian, picked, preferred_element_type=...]
    ppermute x6 -> x20, starting transfers between devices: 11.3 us -> 36.8 us  [the longest x12 19.6 us: shifted(): return lax.ppermute(array, 'band', pairs)]
    unnamed x23 -> x12, local copies, waits for them, and re-layouts: 11.3 us -> 2.47 us
    concatenate x3 -> x0, other arithmetic: 6.61 us -> none  [with_halo(): block = jnp.concatenate([low, block, high], axis=dim)]
  transfers between devices with their start and end apart: 9 -> 20, of which waited for: 5 -> 6; matrix products, arithmetic and copies ran while one was open for 15% -> 1% of each run, Pallas kernels for 0% -> 41%
where the time goes in v1:
time: 109 us
  Pallas kernels  44.9 us (41%)
  starting transfers between devices  36.8 us (34%)
  waiting for transfers between devices  19.7 us (18%)
  local copies, waits for them, and re-layouts  6.23 us (6%)
    pallas_call x3, Pallas kernels, sweep(): pl.pallas_call(functools.partial(sweep_kernel, level), out_shape=outs, in...  31.1 us
    ppermute x12, starting transfers between devices, shifted(): return lax.ppermute(array, 'band', pairs)  19.6 us
    pallas_call x6, Pallas kernels, edge(): pl.pallas_call(functools.partial(edge_kernel, 1.0 if level == 1 else 2.0)...  10.4 us
    ppermute x12, waiting for transfers between devices, shifted(): return lax.ppermute(array, 'band', pairs)  9.66 us
    ppermute x2, starting transfers between devices, across(): return lax.ppermute(array, 'band', pairs)  9.46 us
    ppermute x2, waiting for transfers between devices, across(): return lax.ppermute(array, 'band', pairs)  9.45 us
    ppermute x3, starting transfers between devices, local(): send_down = lambda a: lax.ppermute(a, 'strip', back)  7.63 us
    unnamed x12, local copies, waits for them, and re-layouts  2.47 us
  transfers between devices with their start and end apart: 20, of which 6 were waited for; matrix products, arithmetic and copies ran while one was open for 1% of the time, Pallas kernels for 41%

profile of v1, /device:TPU:2, one launch (start us, length us, event | category | flops | bytes accessed | tf_op | source)
XLA Modules:
  0.0 108.8 jit_solution(6360338987072857509)
XLA Ops:
  0.0 2.5 %fusion.12 = (bf16[16,128,128]{2,1,0:T(8,128)(2,1)}, bf16[16,128,128]{2,1,0:T(8,128)(2,1)}) fusion(bf16[64,128,128]{2,1,0:T(8,128)(2,1)} %refs_0_.1), kind=kLoop, calls=%fused_computation.38 | loop fusion | bytes 2097152 | tf_op jit(solution)/shard_map/slice | solution.py:228
  2.5 4.1 %collective-permute-start.1 = (bf16[16,128,128]{2,1,0:T(8,128)(2,1)}, bf16[16,128,128]{2,1,0:T(8,128)(2,1)}, u32[]{:S(2)}, u32[]{:S(2)}) collective-permute-start(bf16[16,128,128]{2,1,0:T(8,128)(2,1)} %get-tuple-element.59.refs_3_), channel_id=1, source_target_pairs={{1,0},{2,1},{3,2},{4,3},{5,4},{6,5},{7,6},{0,7},{9,8},{10,9},{11,1... | collective-permute-start | bytes 1572872 | tf_op jit(solution)/shard_map/ppermute | solution.py:225
  6.5 0.0 collective-permute-start
  6.7 0.1 copy.9
  6.8 0.1 add.293.index_ref
  6.9 0.0 copy-done
  6.9 9.8 %sweep1.1 = (bf16[32,128,128]{2,1,0:T(8,128)(2,1)S(1)}, f32[16,128,128]{2,1,0:T(8,128)S(1)}, f32[16,128,128]{2,1,0:T(8,128)S(1)}, bf16[16,128,128]{2,1,0:T(8,128)(2,1)S(1)}, bf16[16,128,128]{2,1,0:T(8,128)(2,1)S(1)}) custom-call(s32[320]{0:T(512)S(1)} %add.293.index_ref, bf16[64,128,128]{2,1,0:T(8,128)(2,1)S(1)} %copy-done, bf16[320,128,128]{2,1,0:T(8,128)(2,1)} %bitcast.5), custom_call_target="tpu_custom_call" | custom-call | tf_op jit(solution)/shard_map/sweep1/pallas_call | solution.py:114
  16.7 0.0 collective-permute-done.1.halo_ref
  16.7 2.9 %edge1.3.refs_2_.refs_5_ = bf16[16,128,128]{2,1,0:T(8,128)(2,1)} custom-call(f32[16,128,128]{2,1,0:T(8,128)S(1)} %get-tuple-element.35.part_ref, bf16[16,128,128]{2,1,0:T(8,128)(2,1)S(1)} %get-tuple-element.36.far_ref, bf16[16,128,128]{2,1,0:T(8,128)(2,1)} %collective-permute-done.1.halo_ref), custom_call_target="tpu_custom_call" | custom-call | tf_op jit(solution)/shard_map/edge1/pallas_call | solution.py:136
  19.6 0.0 collective-permute-start.2
  19.6 0.5 collective-permute-done.halo_ref
  20.2 2.5 %edge1.2.refs_0_.refs_3_ = bf16[16,128,128]{2,1,0:T(8,128)(2,1)} custom-call(f32[16,128,128]{2,1,0:T(8,128)S(1)} %get-tuple-element.32.part_ref, bf16[16,128,128]{2,1,0:T(8,128)(2,1)S(1)} %get-tuple-element.33.far_ref, bf16[16,128,128]{2,1,0:T(8,128)(2,1)} %collective-permute-done.halo_ref), custom_call_target="tpu_custom_call" | custom-call | tf_op jit(solution)/shard_map/edge1/pallas_call | solution.py:136
  22.7 3.0 %collective-permute-start.3 = (bf16[16,128,128]{2,1,0:T(8,128)(2,1)}, bf16[16,128,128]{2,1,0:T(8,128)(2,1)}, u32[]{:S(2)}, u32[]{:S(2)}) collective-permute-start(bf16[16,128,128]{2,1,0:T(8,128)(2,1)} %edge1.2.refs_0_.refs_3_), channel_id=1, source_target_pairs={{1,0},{2,1},{3,2},{4,3},{5,4},{6,5},{7,6},{0,7},{9,8},{10,9},{11,1... | collective-permute-start | bytes 1572872 | tf_op jit(solution)/shard_map/ppermute | solution.py:225
  25.7 1.0 slice.13.refs_4_
  26.8 1.2 %copy-done.1 = bf16[32,128,128]{2,1,0:T(8,128)(2,1)S(1)} copy-done((bf16[32,128,128]{2,1,0:T(8,128)(2,1)S(1)}, bf16[32,128,128]{2,1,0:T(8,128)(2,1)}, u32[]{:S(2)}) %copy-start.1) | copy-done | bytes 1048600
  28.0 1.2 %copy-done.3 = bf16[32,128,128]{2,1,0:T(8,128)(2,1)S(1)} copy-done((bf16[32,128,128]{2,1,0:T(8,128)(2,1)S(1)}, bf16[32,128,128]{2,1,0:T(8,128)(2,1)}, u32[]{:S(2)}) %copy-start.3) | copy-done | bytes 1048600
  29.2 10.8 %sweep2.1 = (bf16[32,128,128]{2,1,0:T(8,128)(2,1)S(1)}, f32[16,128,128]{2,1,0:T(8,128)S(1)}, f32[16,128,128]{2,1,0:T(8,128)S(1)}) custom-call(s32[320]{0:T(512)S(1)} %add.293.index_ref, bf16[16,128,128]{2,1,0:T(8,128)(2,1)} %edge1.2.refs_0_.refs_3_, bf16[32,128,128]{2,1,0:T(8,128)(2,1)S(1)} %copy-done.3, bf16[16,128,128]{2,1,0:T(8,128)(2,1)} %edge1.3.refs_2_.refs_5_, ...), custom_call_target="tpu_custom_call" | custom-call | tf_op jit(solution)/shard_map/sweep2/pallas_call | solution.py:114
  40.0 0.0 collective-permute-done.2.halo_ref
  40.0 0.0 copy-start.5
  40.1 1.8 %edge2.2.refs_0_ = bf16[16,128,128]{2,1,0:T(8,128)(2,1)S(1)} custom-call(f32[16,128,128]{2,1,0:T(8,128)S(1)} %get-tuple-element.37.part_ref, bf16[16,128,128]{2,1,0:T(8,128)(2,1)S(1)} %get-tuple-element.33.far_ref, bf16[16,128,128]{2,1,0:T(8,128)(2,1)} %collective-permute-done.2.halo_ref), custom_call_target="tpu_custom_call" | custom-call | tf_op jit(solution)/shard_map/edge2/pallas_call | solution.py:136
  41.8 0.6 collective-permute-start.5
  42.4 0.0 collective-permute-done.3.halo_ref
  42.4 1.7 %edge2.3.refs_2_ = bf16[16,128,128]{2,1,0:T(8,128)(2,1)S(1)} custom-call(f32[16,128,128]{2,1,0:T(8,128)S(1)} %get-tuple-element.39.part_ref, bf16[16,128,128]{2,1,0:T(8,128)(2,1)S(1)} %get-tuple-element.36.far_ref, bf16[16,128,128]{2,1,0:T(8,128)(2,1)} %collective-permute-done.3.halo_ref), custom_call_target="tpu_custom_call" | custom-call | tf_op jit(solution)/shard_map/edge2/pallas_call | solution.py:136
  44.1 0.1 collective-permute-start.4
  44.2 0.1 pad_add_fusion.me_ref
  44.3 0.0 copy-done.5
  44.3 10.5 %sweep3.1 = (bf16[32,128,128]{2,1,0:T(8,128)(2,1)S(1)}, f32[16,128,128]{2,1,0:T(8,128)S(1)}, f32[16,128,128]{2,1,0:T(8,128)S(1)}) custom-call(s32[320]{0:T(512)S(1)} %add.293.index_ref, bf16[16,128,128]{2,1,0:T(8,128)(2,1)S(1)} %edge2.2.refs_0_, bf16[32,128,128]{2,1,0:T(8,128)(2,1)S(1)} %get-tuple-element.38.refs_1_, ...), custom_call_target="tpu_custom_call" | custom-call | tf_op jit(solution)/shard_map/sweep3/pallas_call | solution.py:114
  54.9 0.7 scaled.3
  55.6 1.6 %collective-permute-start.13 = (bf16[8,128,128]{2,1,0:T(8,128)(2,1)S(1)}, bf16[8,128,128]{2,1,0:T(8,128)(2,1)S(1)}, u32[]{:S(2)}, u32[]{:S(2)}) collective-permute-start(bf16[8,128,128]{2,1,0:T(8,128)(2,1)S(1)} %get-tuple-element.52), channel_id=1, source_target_pairs={{0,8},{8,16},{16,24},{24,0},{32,40},{40,48},{48,56},{56,32},{64,72... | collective-permute-start | bytes 786440 | tf_op jit(solution)/shard_map/ppermute | solution.py:201
  57.2 1.1 %collective-permute-start.14 = (bf16[8,128,128]{2,1,0:T(8,128)(2,1)S(1)}, bf16[8,128,128]{2,1,0:T(8,128)(2,1)S(1)}, u32[]{:S(2)}, u32[]{:S(2)}) collective-permute-start(bf16[8,128,128]{2,1,0:T(8,128)(2,1)S(1)} %get-tuple-element.53), channel_id=1, source_target_pairs={{0,16},{8,24},{16,0},{24,8},{32,48},{40,56},{48,32},{56,40},{64,80... | collective-permute-start | bytes 786440 | tf_op jit(solution)/shard_map/ppermute | solution.py:201
  58.3 2.2 %collective-permute-start.15 = (bf16[8,128,128]{2,1,0:T(8,128)(2,1)S(1)}, bf16[8,128,128]{2,1,0:T(8,128)(2,1)S(1)}, u32[]{:S(2)}, u32[]{:S(2)}) collective-permute-start(bf16[8,128,128]{2,1,0:T(8,128)(2,1)S(1)} %get-tuple-element.54), channel_id=1, source_target_pairs={{0,24},{8,0},{16,8},{24,16},{32,56},{40,32},{48,40},{56,48},{64,88... | collective-permute-start | bytes 786440 | tf_op jit(solution)/shard_map/ppermute | solution.py:201
  60.4 0.0 collective-permute-done.5.halo_ref
  60.4 0.7 edge3.3.refs_1_
  61.2 0.0 collective-permute-done.4.halo_ref
  61.2 0.7 edge3.2.refs_0_
  61.9 0.7 scaled.2
  62.6 0.1 collective-permute-start.6
  62.7 3.5 %collective-permute-start.7 = (bf16[8,128,128]{2,1,0:T(8,128)(2,1)S(1)}, bf16[8,128,128]{2,1,0:T(8,128)(2,1)S(1)}, u32[]{:S(2)}, u32[]{:S(2)}) collective-permute-start(bf16[8,128,128]{2,1,0:T(8,128)(2,1)S(1)} %get-tuple-element.44), channel_id=1, source_target_pairs={{0,16},{8,24},{16,0},{24,8},{32,48},{40,56},{48,32},{56,40},{64,80... | collective-permute-start | bytes 786440 | tf_op jit(solution)/shard_map/ppermute | solution.py:201
  66.2 2.4 %collective-permute-done.13.refs_1_ = bf16[8,128,128]{2,1,0:T(8,128)(2,1)S(1)} collective-permute-done((bf16[8,128,128]{2,1,0:T(8,128)(2,1)S(1)}, bf16[8,128,128]{2,1,0:T(8,128)(2,1)S(1)}, u32[]{:S(2)}, u32[]{:S(2)}) %collective-permute-start.13) | collective-permute-done | bytes 262176 | tf_op jit(solution)/shard_map/ppermute | solution.py:201
  68.6 0.0 collective-permute-start.8
  68.6 0.0 collective-permute-done.14.refs_2_
  68.6 4.9 %collective-permute-done.15.refs_3_ = bf16[8,128,128]{2,1,0:T(8,128)(2,1)S(1)} collective-permute-done((bf16[8,128,128]{2,1,0:T(8,128)(2,1)S(1)}, bf16[8,128,128]{2,1,0:T(8,128)(2,1)S(1)}, u32[]{:S(2)}, u32[]{:S(2)}) %collective-permute-start.15) | collective-permute-done | bytes 262176 | tf_op jit(solution)/shard_map/ppermute | solution.py:201
  73.5 1.0 grams.3
  74.5 1.6 %collective-permute-start.16 = (bf16[2,128,128]{2,1,0:T(8,128)(2,1)S(1)}, bf16[2,128,128]{2,1,0:T(8,128)(2,1)S(1)}, u32[]{:S(2)}, u32[]{:S(2)}) collective-permute-start(bf16[2,128,128]{2,1,0:T(8,128)(2,1)S(1)} %get-tuple-element.56), channel_id=1, source_target_pairs={{0,32},{8,40},{16,48},{24,56},{32,64},{40,72},{48,80},{56,88},{64,... | collective-permute-start | bytes 196616 | tf_op jit(solution)/shard_map/ppermute | solution.py:201
  76.2 2.9 %collective-permute-start.17 = (bf16[2,128,128]{2,1,0:T(8,128)(2,1)S(1)}, bf16[2,128,128]{2,1,0:T(8,128)(2,1)S(1)}, u32[]{:S(2)}, u32[]{:S(2)}) collective-permute-start(bf16[2,128,128]{2,1,0:T(8,128)(2,1)S(1)} %get-tuple-element.57), channel_id=1, source_target_pairs={{0,64},{8,72},{16,80},{24,88},{32,96},{40,104},{48,112},{56,120},{... | collective-permute-start | bytes 196616 | tf_op jit(solution)/shard_map/ppermute | solution.py:201
  79.1 0.0 collective-permute-done.6.refs_1_
  79.1 1.3 %collective-permute-start.18 = (bf16[2,128,128]{2,1,0:T(8,128)(2,1)S(1)}, bf16[2,128,128]{2,1,0:T(8,128)(2,1)S(1)}, u32[]{:S(2)}, u32[]{:S(2)}) collective-permute-start(bf16[2,128,128]{2,1,0:T(8,128)(2,1)S(1)} %get-tuple-element.58), channel_id=1, source_target_pairs={{0,96},{8,104},{16,112},{24,120},{32,0},{40,8},{48,16},{56,24},{64... | collective-permute-start | bytes 196616 | tf_op jit(solution)/shard_map/ppermute | solution.py:201
  80.4 0.0 collective-permute-done.7.refs_2_
  80.4 2.4 %collective-permute-done.8.refs_3_ = bf16[8,128,128]{2,1,0:T(8,128)(2,1)S(1)} collective-permute-done((bf16[8,128,128]{2,1,0:T(8,128)(2,1)S(1)}, bf16[8,128,128]{2,1,0:T(8,128)(2,1)S(1)}, u32[]{:S(2)}, u32[]{:S(2)}) %collective-permute-start.8) | collective-permute-done | bytes 262176 | tf_op jit(solution)/shard_map/ppermute | solution.py:201
  82.8 1.0 grams.2
  83.8 3.3 %collective-permute-start.10 = (bf16[2,128,128]{2,1,0:T(8,128)(2,1)S(1)}, bf16[2,128,128]{2,1,0:T(8,128)(2,1)S(1)}, u32[]{:S(2)}, u32[]{:S(2)}) collective-permute-start(bf16[2,128,128]{2,1,0:T(8,128)(2,1)S(1)} %get-tuple-element.48), channel_id=1, source_target_pairs={{0,64},{8,72},{16,80},{24,88},{32,96},{40,104},{48,112},{56,120},{... | collective-permute-start | bytes 196616 | tf_op jit(solution)/shard_map/ppermute | solution.py:201
  87.1 1.0 collective-permute-start.11
  88.1 0.0 collective-permute-done.16
  88.1 1.0 collective-permute-start.9
  89.1 0.0 collective-permute-done.17
  89.1 0.0 collective-permute-done.18
  89.1 8.2 %collective-permute-start.19 = (f32[2,128,128]{2,1,0:T(8,128)S(1)}, f32[2,128,128]{2,1,0:T(8,128)S(1)}, u32[]{:S(2)}, u32[]{:S(2)}) collective-permute-start(f32[2,128,128]{2,1,0:T(8,128)S(1)} %convert_add_fusion), channel_id=1, source_target_pairs={{0,128},{8,136},{16,144},{24,152},{32,160},{40,168},{48,176},{56,1... | collective-permute-start | bytes 393224 | tf_op jit(solution)/shard_map/ppermute | solution.py:211
  97.3 0.0 collective-permute-done.10
  97.3 0.0 collective-permute-done.11
  97.3 0.0 collective-permute-done.9
  97.4 1.3 %collective-permute-start.12 = (f32[2,128,128]{2,1,0:T(8,128)S(1)}, f32[2,128,128]{2,1,0:T(8,128)S(1)}, u32[]{:S(2)}, u32[]{:S(2)}) collective-permute-start(f32[2,128,128]{2,1,0:T(8,128)S(1)} %convert_add_fusion.1), channel_id=1, source_target_pairs={{64,192},{72,200},{80,208},{88,216},{96,224},{104,232},{112,240},{... | collective-permute-start | bytes 393224 | tf_op jit(solution)/shard_map/ppermute | solution.py:211
  98.7 1.2 %collective-permute-done.19 = f32[2,128,128]{2,1,0:T(8,128)S(1)} collective-permute-done((f32[2,128,128]{2,1,0:T(8,128)S(1)}, f32[2,128,128]{2,1,0:T(8,128)S(1)}, u32[]{:S(2)}, u32[]{:S(2)}) %collective-permute-start.19) | collective-permute-done | bytes 131104 | tf_op jit(solution)/shard_map/ppermute | solution.py:211
  99.9 8.3 %collective-permute-done.12 = f32[2,128,128]{2,1,0:T(8,128)S(1)} collective-permute-done((f32[2,128,128]{2,1,0:T(8,128)S(1)}, f32[2,128,128]{2,1,0:T(8,128)S(1)}, u32[]{:S(2)}, u32[]{:S(2)}) %collective-permute-start.12) | collective-permute-done | bytes 131104 | tf_op jit(solution)/shard_map/ppermute | solution.py:211
  108.1 0.7 add_select_fusion
  (17 shorter events, 0.2 us)
Async XLA Ops:
  0.0 6.9 %copy-start = (bf16[64,128,128]{2,1,0:T(8,128)(2,1)S(1)}, bf16[64,128,128]{2,1,0:T(8,128)(2,1)}, u32[]{:S(2)}) copy-start(bf16[64,128,128]{2,1,0:T(8,128)(2,1)} %refs_0_.1) | copy-start | bytes 6291460
  0.0 6.6 %copy-start.4 = (s32[64,5]{0,1:T(8,128)S(1)}, s32[64,5]{0,1:T(8,128)}, u32[]{:S(2)}) copy-start(s32[64,5]{0,1:T(8,128)} %param.6) | copy-start | bytes 3844
  2.5 14.2 %collective-permute-start.1 = (bf16[16,128,128]{2,1,0:T(8,128)(2,1)}, bf16[16,128,128]{2,1,0:T(8,128)(2,1)}, u32[]{:S(2)}, u32[]{:S(2)}) collective-permute-start(bf16[16,128,128]{2,1,0:T(8,128)(2,1)} %get-tuple-element.59.refs_3_), channel_id=1, source_target_pairs={{1,0},{2,1},{3,2},{4,3},{5,4},{6,5},{7,6},{0,7},{9,8},{10,9},{11,1... | collective-permute-start | bytes 1572872 | tf_op jit(solution)/shard_map/ppermute | solution.py:225
  6.5 13.7 %collective-permute-start = (bf16[16,128,128]{2,1,0:T(8,128)(2,1)}, bf16[16,128,128]{2,1,0:T(8,128)(2,1)}, u32[]{:S(2)}, u32[]{:S(2)}) collective-permute-start(bf16[16,128,128]{2,1,0:T(8,128)(2,1)} %get-tuple-element.60.refs_5_), channel_id=1, source_target_pairs={{0,1},{1,2},{2,3},{3,4},{4,5},{5,6},{6,7},{7,0},{8,9},{9,10},{10,1... | collective-permute-start | bytes 1572872 | tf_op jit(solution)/shard_map/ppermute | solution.py:224
  16.7 6.0 %copy-start.2 = (bf16[32,128,128]{2,1,0:T(8,128)(2,1)}, bf16[32,128,128]{2,1,0:T(8,128)(2,1)S(1)}, u32[]{:S(2)}) copy-start(bf16[32,128,128]{2,1,0:T(8,128)(2,1)S(1)} %get-tuple-element.34.refs_1_.refs_4_) | copy-start | bytes 3145732
  19.6 20.4 %collective-permute-start.2 = (bf16[16,128,128]{2,1,0:T(8,128)(2,1)}, bf16[16,128,128]{2,1,0:T(8,128)(2,1)}, u32[]{:S(2)}, u32[]{:S(2)}) collective-permute-start(bf16[16,128,128]{2,1,0:T(8,128)(2,1)} %edge1.3.refs_2_.refs_5_), channel_id=1, source_target_pairs={{0,1},{1,2},{2,3},{3,4},{4,5},{5,6},{6,7},{7,0},{8,9},{9,10},{10,1... | collective-permute-start | bytes 1572872 | tf_op jit(solution)/shard_map/ppermute | solution.py:224
  22.7 19.7 %collective-permute-start.3 = (bf16[16,128,128]{2,1,0:T(8,128)(2,1)}, bf16[16,128,128]{2,1,0:T(8,128)(2,1)}, u32[]{:S(2)}, u32[]{:S(2)}) collective-permute-start(bf16[16,128,128]{2,1,0:T(8,128)(2,1)} %edge1.2.refs_0_.refs_3_), channel_id=1, source_target_pairs={{1,0},{2,1},{3,2},{4,3},{5,4},{6,5},{7,6},{0,7},{9,8},{10,9},{11,1... | collective-permute-start | bytes 1572872 | tf_op jit(solution)/shard_map/ppermute | solution.py:225
  26.8 1.2 %copy-start.1 = (bf16[32,128,128]{2,1,0:T(8,128)(2,1)S(1)}, bf16[32,128,128]{2,1,0:T(8,128)(2,1)}, u32[]{:S(2)}) copy-start(bf16[32,128,128]{2,1,0:T(8,128)(2,1)} %slice.13.refs_4_) | copy-start | bytes 3145732
  28.0 1.2 %copy-start.3 = (bf16[32,128,128]{2,1,0:T(8,128)(2,1)S(1)}, bf16[32,128,128]{2,1,0:T(8,128)(2,1)}, u32[]{:S(2)}) copy-start(bf16[32,128,128]{2,1,0:T(8,128)(2,1)} %copy-done.2) | copy-start | bytes 3145732
  40.0 4.3 %copy-start.5 = (f32[128]{0:T(128)S(1)}, f32[128]{0:T(128)}, u32[]{:S(2)}) copy-start(f32[128]{0:T(128)} %param.7) | copy-start | bytes 1540
  41.8 18.6 %collective-permute-start.5 = (bf16[16,128,128]{2,1,0:T(8,128)(2,1)S(1)}, bf16[16,128,128]{2,1,0:T(8,128)(2,1)S(1)}, u32[]{:S(2)}, u32[]{:S(2)}) collective-permute-start(bf16[16,128,128]{2,1,0:T(8,128)(2,1)S(1)} %edge2.2.refs_0_), channel_id=1, source_target_pairs={{1,0},{2,1},{3,2},{4,3},{5,4},{6,5},{7,6},{0,7},{9,8},{10,9},{11,1... | collective-permute-start | bytes 1572872 | tf_op jit(solution)/shard_map/ppermute | solution.py:225
  44.1 17.0 %collective-permute-start.4 = (bf16[16,128,128]{2,1,0:T(8,128)(2,1)S(1)}, bf16[16,128,128]{2,1,0:T(8,128)(2,1)S(1)}, u32[]{:S(2)}, u32[]{:S(2)}) collective-permute-start(bf16[16,128,128]{2,1,0:T(8,128)(2,1)S(1)} %edge2.3.refs_2_), channel_id=1, source_target_pairs={{0,1},{1,2},{2,3},{3,4},{4,5},{5,6},{6,7},{7,0},{8,9},{9,10},{10,1... | collective-permute-start | bytes 1572872 | tf_op jit(solution)/shard_map/ppermute | solution.py:224
  55.6 13.0 %collective-permute-start.13 = (bf16[8,128,128]{2,1,0:T(8,128)(2,1)S(1)}, bf16[8,128,128]{2,1,0:T(8,128)(2,1)S(1)}, u32[]{:S(2)}, u32[]{:S(2)}) collective-permute-start(bf16[8,128,128]{2,1,0:T(8,128)(2,1)S(1)} %get-tuple-element.52), channel_id=1, source_target_pairs={{0,8},{8,16},{16,24},{24,0},{32,40},{40,48},{48,56},{56,32},{64,72... | collective-permute-start | bytes 786440 | tf_op jit(solution)/shard_map/ppermute | solution.py:201
  57.2 11.5 %collective-permute-start.14 = (bf16[8,128,128]{2,1,0:T(8,128)(2,1)S(1)}, bf16[8,128,128]{2,1,0:T(8,128)(2,1)S(1)}, u32[]{:S(2)}, u32[]{:S(2)}) collective-permute-start(bf16[8,128,128]{2,1,0:T(8,128)(2,1)S(1)} %get-tuple-element.53), channel_id=1, source_target_pairs={{0,16},{8,24},{16,0},{24,8},{32,48},{40,56},{48,32},{56,40},{64,80... | collective-permute-start | bytes 786440 | tf_op jit(solution)/shard_map/ppermute | solution.py:201
  58.3 15.3 %collective-permute-start.15 = (bf16[8,128,128]{2,1,0:T(8,128)(2,1)S(1)}, bf16[8,128,128]{2,1,0:T(8,128)(2,1)S(1)}, u32[]{:S(2)}, u32[]{:S(2)}) collective-permute-start(bf16[8,128,128]{2,1,0:T(8,128)(2,1)S(1)} %get-tuple-element.54), channel_id=1, source_target_pairs={{0,24},{8,0},{16,8},{24,16},{32,56},{40,32},{48,40},{56,48},{64,88... | collective-permute-start | bytes 786440 | tf_op jit(solution)/shard_map/ppermute | solution.py:201
  62.6 16.4 %collective-permute-start.6 = (bf16[8,128,128]{2,1,0:T(8,128)(2,1)S(1)}, bf16[8,128,128]{2,1,0:T(8,128)(2,1)S(1)}, u32[]{:S(2)}, u32[]{:S(2)}) collective-permute-start(bf16[8,128,128]{2,1,0:T(8,128)(2,1)S(1)} %get-tuple-element.43), channel_id=1, source_target_pairs={{0,8},{8,16},{16,24},{24,0},{32,40},{40,48},{48,56},{56,32},{64,72... | collective-permute-start | bytes 786440 | tf_op jit(solution)/shard_map/ppermute | solution.py:201
  62.7 17.7 %collective-permute-start.7 = (bf16[8,128,128]{2,1,0:T(8,128)(2,1)S(1)}, bf16[8,128,128]{2,1,0:T(8,128)(2,1)S(1)}, u32[]{:S(2)}, u32[]{:S(2)}) collective-permute-start(bf16[8,128,128]{2,1,0:T(8,128)(2,1)S(1)} %get-tuple-element.44), channel_id=1, source_target_pairs={{0,16},{8,24},{16,0},{24,8},{32,48},{40,56},{48,32},{56,40},{64,80... | collective-permute-start | bytes 786440 | tf_op jit(solution)/shard_map/ppermute | solution.py:201
  68.6 14.2 %collective-permute-start.8 = (bf16[8,128,128]{2,1,0:T(8,128)(2,1)S(1)}, bf16[8,128,128]{2,1,0:T(8,128)(2,1)S(1)}, u32[]{:S(2)}, u32[]{:S(2)}) collective-permute-start(bf16[8,128,128]{2,1,0:T(8,128)(2,1)S(1)} %get-tuple-element.45), channel_id=1, source_target_pairs={{0,24},{8,0},{16,8},{24,16},{32,56},{40,32},{48,40},{56,48},{64,88... | collective-permute-start | bytes 786440 | tf_op jit(solution)/shard_map/ppermute | solution.py:201
  74.5 13.6 %collective-permute-start.16 = (bf16[2,128,128]{2,1,0:T(8,128)(2,1)S(1)}, bf16[2,128,128]{2,1,0:T(8,128)(2,1)S(1)}, u32[]{:S(2)}, u32[]{:S(2)}) collective-permute-start(bf16[2,128,128]{2,1,0:T(8,128)(2,1)S(1)} %get-tuple-element.56), channel_id=1, source_target_pairs={{0,32},{8,40},{16,48},{24,56},{32,64},{40,72},{48,80},{56,88},{64,... | collective-permute-start | bytes 196616 | tf_op jit(solution)/shard_map/ppermute | solution.py:201
  76.2 12.9 %collective-permute-start.17 = (bf16[2,128,128]{2,1,0:T(8,128)(2,1)S(1)}, bf16[2,128,128]{2,1,0:T(8,128)(2,1)S(1)}, u32[]{:S(2)}, u32[]{:S(2)}) collective-permute-start(bf16[2,128,128]{2,1,0:T(8,128)(2,1)S(1)} %get-tuple-element.57), channel_id=1, source_target_pairs={{0,64},{8,72},{16,80},{24,88},{32,96},{40,104},{48,112},{56,120},{... | collective-permute-start | bytes 196616 | tf_op jit(solution)/shard_map/ppermute | solution.py:201
  79.1 10.0 %collective-permute-start.18 = (bf16[2,128,128]{2,1,0:T(8,128)(2,1)S(1)}, bf16[2,128,128]{2,1,0:T(8,128)(2,1)S(1)}, u32[]{:S(2)}, u32[]{:S(2)}) collective-permute-start(bf16[2,128,128]{2,1,0:T(8,128)(2,1)S(1)} %get-tuple-element.58), channel_id=1, source_target_pairs={{0,96},{8,104},{16,112},{24,120},{32,0},{40,8},{48,16},{56,24},{64... | collective-permute-start | bytes 196616 | tf_op jit(solution)/shard_map/ppermute | solution.py:201
  83.8 13.5 %collective-permute-start.10 = (bf16[2,128,128]{2,1,0:T(8,128)(2,1)S(1)}, bf16[2,128,128]{2,1,0:T(8,128)(2,1)S(1)}, u32[]{:S(2)}, u32[]{:S(2)}) collective-permute-start(bf16[2,128,128]{2,1,0:T(8,128)(2,1)S(1)} %get-tuple-element.48), channel_id=1, source_target_pairs={{0,64},{8,72},{16,80},{24,88},{32,96},{40,104},{48,112},{56,120},{... | collective-permute-start | bytes 196616 | tf_op jit(solution)/shard_map/ppermute | solution.py:201
  87.1 10.3 %collective-permute-start.11 = (bf16[2,128,128]{2,1,0:T(8,128)(2,1)S(1)}, bf16[2,128,128]{2,1,0:T(8,128)(2,1)S(1)}, u32[]{:S(2)}, u32[]{:S(2)}) collective-permute-start(bf16[2,128,128]{2,1,0:T(8,128)(2,1)S(1)} %get-tuple-element.49), channel_id=1, source_target_pairs={{0,96},{8,104},{16,112},{24,120},{32,0},{40,8},{48,16},{56,24},{64... | collective-permute-start | bytes 196616 | tf_op jit(solution)/shard_map/ppermute | solution.py:201
  88.1 9.2 %collective-permute-start.9 = (bf16[2,128,128]{2,1,0:T(8,128)(2,1)S(1)}, bf16[2,128,128]{2,1,0:T(8,128)(2,1)S(1)}, u32[]{:S(2)}, u32[]{:S(2)}) collective-permute-start(bf16[2,128,128]{2,1,0:T(8,128)(2,1)S(1)} %get-tuple-element.47), channel_id=1, source_target_pairs={{0,32},{8,40},{16,48},{24,56},{32,64},{40,72},{48,80},{56,88},{64,... | collective-permute-start | bytes 196616 | tf_op jit(solution)/shard_map/ppermute | solution.py:201
  89.1 10.7 %collective-permute-start.19 = (f32[2,128,128]{2,1,0:T(8,128)S(1)}, f32[2,128,128]{2,1,0:T(8,128)S(1)}, u32[]{:S(2)}, u32[]{:S(2)}) collective-permute-start(f32[2,128,128]{2,1,0:T(8,128)S(1)} %convert_add_fusion), channel_id=1, source_target_pairs={{0,128},{8,136},{16,144},{24,152},{32,160},{40,168},{48,176},{56,1... | collective-permute-start | bytes 393224 | tf_op jit(solution)/shard_map/ppermute | solution.py:211
  97.4 10.8 %collective-permute-start.12 = (f32[2,128,128]{2,1,0:T(8,128)S(1)}, f32[2,128,128]{2,1,0:T(8,128)S(1)}, u32[]{:S(2)}, u32[]{:S(2)}) collective-permute-start(f32[2,128,128]{2,1,0:T(8,128)S(1)} %convert_add_fusion.1), channel_id=1, source_target_pairs={{64,192},{72,200},{80,208},{88,216},{96,224},{104,232},{112,240},{... | collective-permute-start | bytes 393224 | tf_op jit(solution)/shard_map/ppermute | solution.py:211

commit v2 on v1

v2 whole, which is shorter than its diff:
```python
import functools

import jax
import jax.numpy as jnp
from jax import lax
from jax.experimental import pallas as pl
from jax.experimental.pallas import tpu as pltpu
from jax.sharding import PartitionSpec as P

EY = 16
EXS = 4
EX = 32
NB = 128
HALF = NB // 2
NBAND = 4096
XS = 4
YS = 4
GROUP = 8
WIDE = GROUP * HALF + 16
THIN = 2 * HALF + 16

BF = jnp.bfloat16
F32 = jnp.float32
VMEM = pltpu.VMEM
LIMIT = 16 << 20
SMEM_SPEC = pl.BlockSpec(memory_space=pltpu.SMEM)
VMEM_SPEC = pl.BlockSpec(memory_space=VMEM)


def struct(shape, dtype):
    return jax.ShapeDtypeStruct(shape, dtype)


def call(kernel, name, outs, scalars, arrays, scratch=(), far=()):
    arrays = [pltpu.with_memory_space_constraint(a, VMEM) for a in arrays]
    arrays += [pltpu.with_memory_space_constraint(a, pltpu.HBM) for a in far]
    return pl.pallas_call(
        kernel,
        out_shape=outs,
        in_specs=[SMEM_SPEC] * len(scalars)
        + [VMEM_SPEC] * (len(arrays) - len(far))
        + [pl.BlockSpec(memory_space=pltpu.HBM)] * len(far),
        out_specs=[VMEM_SPEC] * len(outs),
        scratch_shapes=list(scratch),
        compiler_params=pltpu.CompilerParams(vmem_limit_bytes=LIMIT),
        name=name,
    )(*scalars, *arrays)


def dot(a, b):
    return jnp.dot(a, b, preferred_element_type=F32)


def gram(a, b):
    return lax.dot_general(a, b, (((1,), (1,)), ((), ())), preferred_element_type=F32)


def block_indices(adjacency, strip_index):
    local = jnp.arange(EXS * EY, dtype=jnp.int32)
    row = strip_index * EXS + local // EY
    col = local % EY
    wanted = jnp.stack(
        [
            row * EY + col,
            (row + 1) % EX * EY + col,
            (row + EX - 1) % EX * EY + col,
            row * EY + (col + 1) % EY,
            row * EY + (col + EY - 1) % EY,
        ],
        axis=1,
    )
    hit = adjacency[:, None, :] == wanted[:, :, None]
    slot = jnp.sum(jnp.where(hit, jnp.arange(5, dtype=jnp.int32), 0), axis=2)
    return (local[:, None] * 5 + slot).reshape(-1)


def element_at(x, j):
    return j // 2 * GROUP + 2 * x + j % 2


def pack_groups(me_ref, s_ref, outs):
    row = lax.broadcasted_iota(jnp.int32, (HALF, NB), 0)
    col = lax.broadcasted_iota(jnp.int32, (HALF, NB), 1) - HALF
    tile_row = lax.broadcasted_iota(jnp.int32, (16, NB), 0)
    for s in range(XS):
        x = lax.rem(me_ref[0] + s, XS)

        def element(j, diagonals):
            v = s_ref[element_at(x, j)]
            top, bottom = v[:HALF], v[HALF:]
            low = gram(bottom, v)
            high = gram(top, jnp.concatenate([bottom, top], axis=0))
            packed = jnp.where((col >= 0) & (col < row), high, low)
            outs[s][pl.ds(pl.multiple_of(j * HALF, HALF), HALF), :] = packed.astype(outs[s].dtype)
            diagonal = jnp.sum(jnp.where(col == row, high, 0.0), axis=0, keepdims=True)
            return jnp.where(tile_row == j, diagonal, diagonals)

        diagonals = lax.fori_loop(0, GROUP, element, jnp.zeros((16, NB), F32), unroll=GROUP)
        outs[s][GROUP * HALF :, :] = diagonals.astype(outs[s].dtype)


def group_structs(rows):
    return [struct((rows, NB), F32)] + [struct((rows, NB), BF)] * 3


def sweep_kernel(level, index_ref, *refs):
    if level == 1:
        me_ref, v_ref, root_ref, h_ref, mid_ref, part0, part3, h, sem = refs
        rows = [v_ref.at[pl.ds(r * EY, EY)] for r in range(EXS)]
        before = None
        spans = [pl.ds(r * 5 * EY, 5 * EY) for r in range(EXS)]
        copies = [
            pltpu.make_async_copy(h_ref.at[span], h.at[span], sem.at[r])
            for r, span in enumerate(spans)
        ]
        for copy in copies:
            copy.start()
    elif level == 2:
        v0, vm, v3, p_ref, h, mid_ref, part0, part3 = refs
        rows = [v0, vm.at[pl.ds(0, EY)], vm.at[pl.ds(EY, EY)], v3]
        before = [p_ref.at[pl.ds(r * EY, EY)] for r in range(EXS)]
    else:
        me_ref, root_ref, v0, vm, v3, p0, pm, p3, h, part0, part3, *outs, mid_ref = refs
        rows = [v0, vm.at[pl.ds(0, EY)], vm.at[pl.ds(EY, EY)], v3]
        before = [p0, pm.at[pl.ds(0, EY)], pm.at[pl.ds(EY, EY)], p3]
        root = root_ref[...]
    for r in range(EXS):
        if level == 1:
            copies[r].wait()

        def element(c, carry, r=r):
            at = (r * EY + c) * 5
            right = lax.rem(c + 1, EY)
            left = lax.rem(c + EY - 1, EY)
            terms = [(0, rows[r][c]), (3, rows[r][right]), (4, rows[r][left])]
            if r + 1 < EXS:
                terms.append((1, rows[r + 1][c]))
            if r > 0:
                terms.append((2, rows[r - 1][c]))
            a = jnp.concatenate([h[index_ref[at + k]] for k, _ in terms], axis=1)
            b = jnp.concatenate([v for _, v in terms], axis=0)
            total = dot(a, b)
            if before is not None:
                total = 2.0 * total - before[r][c].astype(F32)
            if r == 0:
                part0[c] = total
            elif r == EXS - 1:
                part3[c] = total
            elif level < 3:
                mid_ref[(r - 1) * EY + c] = total.astype(BF)
            else:
                mid_ref[(2 - r) * EY + c] = (total * root).astype(BF)
            return carry

        lax.fori_loop(0, EY, element, 0, unroll=8)
    if level == 3:
        pack_groups(me_ref, mid_ref, outs)


def sweep(level, scalars, arrays, far=()):
    row = struct((EY, NB, NB), F32)
    mid = (2 * EY, NB, NB)
    outs, scratch = [struct(mid, BF), row, row], []
    if level == 1:
        outs, scratch = outs + [struct(far[0].shape, BF)], [pltpu.SemaphoreType.DMA((EXS,))]
    elif level == 3:
        outs, scratch = [row, row] + group_structs(WIDE), [VMEM(mid, BF)]
    return call(
        functools.partial(sweep_kernel, level), f"sweep{level}", outs, scalars, arrays, scratch, far
    )


def far_term(row, index_ref, h, halo_ref, c):
    base, slot = (0, 2) if row == 0 else ((EXS - 1) * EY, 1)
    return dot(h[index_ref[(base + c) * 5 + slot]], halo_ref[c])


def edge_kernel(level, row, index_ref, part_ref, h, halo_ref, out_ref):
    scale = 1.0 if level == 1 else 2.0

    def element(c, carry):
        out_ref[c] = (part_ref[c] + scale * far_term(row, index_ref, h, halo_ref, c)).astype(BF)
        return carry

    lax.fori_loop(0, EY, element, 0, unroll=8)


def edge(level, row, index, part, h, halo):
    return call(
        functools.partial(edge_kernel, level, row),
        f"edge{level}_{row}",
        [struct((EY, NB, NB), BF)],
        [index],
        [part, h, halo],
    )[0]


def last_kernel(index_ref, me_ref, root_ref, part0, part3, h, low_ref, high_ref, *refs):
    outs, s_ref = refs[:-1], refs[-1]
    root = root_ref[...]
    for row, part, halo, at in ((0, part0, low_ref, 0), (3, part3, high_ref, EY)):

        def element(c, carry):
            value = part[c] + 2.0 * far_term(row, index_ref, h, halo, c)
            s_ref[at + c] = (value * root).astype(BF)
            return carry

        lax.fori_loop(0, EY, element, 0, unroll=8)
    pack_groups(me_ref, s_ref, outs)


def second_kernel(me_ref, *refs):
    pairs, outs = (refs[:XS], refs[XS : 2 * XS]), refs[2 * XS :]
    for n, srcs in enumerate(pairs):
        tail = sum(src[GROUP * HALF :, :].astype(F32) for src in srcs)
        for t in range(YS):
            y = lax.rem(me_ref[1] + t, YS)
            span = pl.ds(pl.multiple_of(y * NB, NB), NB)
            total = sum(src[span, :].astype(F32) for src in srcs)
            at = n * THIN
            outs[t][at : at + NB, :] = total.astype(outs[t].dtype)
            turned = pltpu.roll(tail, lax.rem(16 - 2 * y, 16), 0)
            outs[t][at + NB : at + THIN, :] = turned.astype(outs[t].dtype)


def third_kernel(me_ref, *refs):
    srcs, (own_ref, sent_ref) = refs[:YS], refs[YS:]
    own = pl.ds(pl.multiple_of(me_ref[2] * THIN, 16), THIN)
    other = pl.ds(pl.multiple_of((1 - me_ref[2]) * THIN, 16), THIN)
    own_ref[...] = sum(src[own, :].astype(F32) for src in srcs)
    sent_ref[...] = sum(src[other, :].astype(F32) for src in srcs).astype(BF)


def final_kernel(own_ref, received_ref, out_ref):
    row = lax.broadcasted_iota(jnp.int32, (HALF, HALF), 0)
    col = lax.broadcasted_iota(jnp.int32, (HALF, HALF), 1)
    total = (own_ref[...] + received_ref[...].astype(F32)) * (1.0 / NBAND)
    for k in range(2):
        u = total[k * HALF : (k + 1) * HALF]
        b, w = u[:, :HALF], u[:, HALF:]
        turned = u.T
        b_t, w_t = turned[:HALF], turned[HALF:]
        diagonal = total[NB + k : NB + k + 1, HALF:]
        a = jnp.where(col < row, w, w_t)
        a = jnp.where(col == row, diagonal, a)
        c = jnp.where(col >= row, w, w_t)
        out_ref[k, :HALF, :] = jnp.concatenate([a, b_t], axis=1)
        out_ref[k, HALF:, :] = jnp.concatenate([b, c], axis=1)


def shifted(array, along, shift):
    step, size = (1, XS) if along == "x" else (XS, YS)
    pairs = []
    for b in range(2 * XS * YS):
        at = b // step % size
        pairs.append((b, b + ((at + shift) % size - at) * step))
    return lax.ppermute(array, "band", pairs)


def exchanged(pieces, along):
    return [pieces[0]] + [shifted(pieces[s], along, s) for s in (1, 2, 3)]


def across(array):
    half = XS * YS
    return lax.ppermute(array, "band", [(b, (b + half) % (2 * half)) for b in range(2 * half)])


def local(coeffs, hamiltonian, adjacency, occupation):
    strip_index = lax.axis_index("strip")
    band_index = lax.axis_index("band")
    count = lax.axis_size("strip")
    ahead = [(i, (i + 1) % count) for i in range(count)]
    back = [(j, i) for i, j in ahead]
    send_up = lambda a: lax.ppermute(a, "strip", ahead)
    send_down = lambda a: lax.ppermute(a, "strip", back)

    low = send_up(coeffs[3 * EY :])
    high = send_down(coeffs[:EY])
    index = block_indices(adjacency, strip_index)
    h = hamiltonian.reshape(-1, NB, NB)
    outer_owner = 1 - ((band_index >> 4) ^ (band_index >> 3 & 1))
    me = jnp.stack([band_index & 3, band_index >> 2 & 3, outer_owner])
    root = jnp.sqrt(occupation).reshape(1, NB)

    m1, part0, part3, h = sweep(1, [index, me], [coeffs, root], [h])
    u0 = edge(1, 0, index, part0, h, low)
    high1 = send_down(u0)
    u3 = edge(1, 3, index, part3, h, high)
    low1 = send_up(u3)
    m2, part0, part3 = sweep(2, [index], [u0, m1, u3, coeffs, h])
    w3 = edge(2, 3, index, part3, h, high1)
    low2 = send_up(w3)
    w0 = edge(2, 0, index, part0, h, low1)
    high2 = send_down(w0)
    part0, part3, *inner = sweep(3, [index, me], [root, w0, m2, w3, u0, m1, u3, h])
    inner = exchanged(inner, "x")
    outer = call(
        last_kernel,
        "last",
        group_structs(WIDE),
        [index, me],
        [root, part0, part3, h, low2, high2],
        [VMEM((2 * EY, NB, NB), BF)],
    )
    outer = exchanged(outer, "x")
    both = call(second_kernel, "second", group_structs(2 * THIN), [me], [*inner, *outer])
    own, sent = call(
        third_kernel,
        "third",
        [struct((THIN, NB), F32), struct((THIN, NB), BF)],
        [me],
        exchanged(both, "y"),
    )
    return call(final_kernel, "final", [struct((2, NB, NB), F32)], [], [own, across(sent)])[0]


def solution(mesh):
    return jax.shard_map(
        local,
        mesh=mesh,
        in_specs=(
            P("strip", None, "band"),
            P("strip", None, None, None),
            P("strip", None),
            P("band"),
        ),
        out_specs=P(("strip", "band"), None, None),
        check_vma=False,
    )
```

time: 109 us -> 78.6 us (0.72)
  Pallas kernels: 44.9 us -> 25.6 us
  starting transfers between devices: 36.8 us -> 28.5 us
  local copies, waits for them, and re-layouts: 6.23 us -> 3.78 us
    pallas_call x13 -> x11, Pallas kernels: 44.9 us -> 25.6 us  [call(): pl.pallas_call(kernel, out_shape=outs, in_specs=[SMEM_SPEC] * len(scalars...]
    ppermute x2 -> x1, waiting for transfers between devices: 9.45 us -> 1.94 us  [across(): lax.ppermute(array, 'band', [(b, (b + half) % (2 * half)) for b in range(...]
    ppermute x3, waiting for transfers between devices: 0.55 us -> 7.64 us  [local(): send_up = lambda a: lax.ppermute(a, 'strip', ahead)]
    ppermute x12 -> x9, starting transfers between devices: 19.6 us -> 15.1 us  [shifted(): return lax.ppermute(array, 'band', pairs)]
    ppermute x2 -> x1, starting transfers between devices: 9.46 us -> 7.05 us  [across(): lax.ppermute(array, 'band', [(b, (b + half) % (2 * half)) for b in range(...]
    ppermute x3, starting transfers between devices: 7.63 us -> 5.68 us  [local(): send_down = lambda a: lax.ppermute(a, 'strip', back)]
    slice x1, local copies, waits for them, and re-layouts: 2.46 us -> 1.27 us  [local(): high = send_down(coeffs[:EY])]
    unnamed x12 -> x4, local copies, waits for them, and re-layouts: 2.47 us -> 1.6 us
  transfers between devices with their start and end apart: 20 -> 16, of which waited for: 6 -> 10; matrix products, arithmetic and copies ran while one was open for 1% -> 2% of each run, Pallas kernels for 41% -> 30%
where the time goes in v2:
time: 78.6 us; the launch traced here: 78.2 us
  starting transfers between devices  28.5 us (36%)
  Pallas kernels  25.6 us (33%)
  waiting for transfers between devices  19.3 us (25%)
  local copies, waits for them, and re-layouts  3.78 us (5%)
  other arithmetic  0.83 us (1%)
    pallas_call x11, Pallas kernels, call(): pl.pallas_call(kernel, out_shape=outs, in_specs=[SMEM_SPEC] * len(scalars...  25.6 us
    ppermute x9, starting transfers between devices, shifted(): return lax.ppermute(array, 'band', pairs)  15.1 us
    ppermute x9, waiting for transfers between devices, shifted(): return lax.ppermute(array, 'band', pairs)  9.45 us
    ppermute x3, waiting for transfers between devices, local(): send_up = lambda a: lax.ppermute(a, 'strip', ahead)  7.64 us
    ppermute x1, starting transfers between devices, across(): lax.ppermute(array, 'band', [(b, (b + half) % (2 * half)) for b in range(...  7.05 us
    ppermute x3, starting transfers between devices, local(): send_down = lambda a: lax.ppermute(a, 'strip', back)  5.68 us
    ppermute x1, waiting for transfers between devices, across(): lax.ppermute(array, 'band', [(b, (b + half) % (2 * half)) for b in range(...  1.94 us
    unnamed x4, local copies, waits for them, and re-layouts  1.6 us
  transfers between devices with their start and end apart: 16, of which 10 were waited for; matrix products, arithmetic and copies ran while one was open for 2% of the time, Pallas kernels for 30%

profile of v2, /device:TPU:2, one launch (start us, length us, event | category | flops | bytes accessed | tf_op | source)
XLA Modules:
  0.0 78.2 jit_solution(16367843570251045229)
XLA Ops:
  0.0 1.3 %fusion.12 = (bf16[16,128,128]{2,1,0:T(8,128)(2,1)S(1)}, bf16[16,128,128]{2,1,0:T(8,128)(2,1)S(1)}) fusion(bf16[64,128,128]{2,1,0:T(8,128)(2,1)} %refs_3_.1), kind=kLoop, calls=%fused_computation.35 | loop fusion | bytes 2097152 | tf_op jit(solution)/shard_map/slice | solution.py:279
  1.3 4.1 %collective-permute-start.1 = (bf16[16,128,128]{2,1,0:T(8,128)(2,1)S(1)}, bf16[16,128,128]{2,1,0:T(8,128)(2,1)S(1)}, u32[]{:S(2)}, u32[]{:S(2)}) collective-permute-start(bf16[16,128,128]{2,1,0:T(8,128)(2,1)S(1)} %get-tuple-element.51), channel_id=1, source_target_pairs={{1,0},{2,1},{3,2},{4,3},{5,4},{6,5},{7,6},{0,7},{9,8},{10,9},{11,1... | collective-permute-start | bytes 1572872 | tf_op jit(solution)/shard_map/ppermute | solution.py:276
  5.4 0.0 collective-permute-start
  5.5 0.7 select_reduce_fusion
  6.2 0.1 copy.9
  6.3 0.1 add.257.index_ref
  6.5 0.1 pad_add_fusion.refs_0_.me_ref
  6.5 0.7 sqrt_bitcast_fusion.refs_2_.refs_1_.root_ref
  7.2 0.0 copy-start
  7.2 1.6 %copy-done = bf16[64,128,128]{2,1,0:T(8,128)(2,1)S(1)} copy-done((bf16[64,128,128]{2,1,0:T(8,128)(2,1)S(1)}, bf16[64,128,128]{2,1,0:T(8,128)(2,1)}, u32[]{:S(2)}) %copy-start) | copy-done | bytes 2097176
  8.8 6.2 %sweep1.1 = (bf16[32,128,128]{2,1,0:T(8,128)(2,1)S(1)}, f32[16,128,128]{2,1,0:T(8,128)S(1)}, f32[16,128,128]{2,1,0:T(8,128)S(1)}, bf16[320,128,128]{2,1,0:T(8,128)(2,1)S(1)}) custom-call(s32[320]{0:T(512)S(1)} %add.257.index_ref, s32[3]{0:T(128)S(1)} %pad_add_fusion.refs_0_.me_ref, bf16[64,128,128]{2,1,0:T(8,128)(2,1)S(1)} %copy-done, ...), custom_call_target="tpu_custom_call" | custom-call | tf_op jit(solution)/shard_map/sweep1/pallas_call | solution.py:37
  15.0 0.3 collective-permute-done.1.halo_ref
  15.3 0.0 copy-start.1
  15.3 1.0 %edge1_3.1.refs_2_.refs_7_ = bf16[16,128,128]{2,1,0:T(8,128)(2,1)S(1)} custom-call(s32[320]{0:T(512)S(1)} %add.257.index_ref, f32[16,128,128]{2,1,0:T(8,128)S(1)} %get-tuple-element.31.part_ref, bf16[320,128,128]{2,1,0:T(8,128)(2,1)S(1)} %get-tuple-element.29.h.refs_4_.refs_8_, bf16[16,128,128]{2,1,0:T(8,128)(2,1)S(1)} %collective-permute-done.1.halo_ref), custom_call_target="tpu_custom_call" | custom-call | tf_op jit(solution)/shard_map/edge1_3/pallas_call | solution.py:37
  16.3 0.1 collective-permute-start.2
  16.4 2.3 %collective-permute-done.halo_ref = bf16[16,128,128]{2,1,0:T(8,128)(2,1)S(1)} collective-permute-done((bf16[16,128,128]{2,1,0:T(8,128)(2,1)S(1)}, bf16[16,128,128]{2,1,0:T(8,128)(2,1)S(1)}, u32[]{:S(2)}, u32[]{:S(2)}) %collective-permute-start) | collective-permute-done | bytes 524320 | tf_op jit(solution)/shard_map/ppermute | solution.py:275
  18.8 1.0 %edge1_0.1.refs_0_.refs_5_ = bf16[16,128,128]{2,1,0:T(8,128)(2,1)S(1)} custom-call(s32[320]{0:T(512)S(1)} %add.257.index_ref, f32[16,128,128]{2,1,0:T(8,128)S(1)} %get-tuple-element.28.part_ref, bf16[320,128,128]{2,1,0:T(8,128)(2,1)S(1)} %get-tuple-element.29.h.refs_4_.refs_8_, bf16[16,128,128]{2,1,0:T(8,128)(2,1)S(1)} %collective-permute-done.halo_ref), custom_call_target="tpu_custom_call" | custom-call | tf_op jit(solution)/shard_map/edge1_0/pallas_call | solution.py:37
  19.8 1.5 %collective-permute-start.3 = (bf16[16,128,128]{2,1,0:T(8,128)(2,1)S(1)}, bf16[16,128,128]{2,1,0:T(8,128)(2,1)S(1)}, u32[]{:S(2)}, u32[]{:S(2)}) collective-permute-start(bf16[16,128,128]{2,1,0:T(8,128)(2,1)S(1)} %edge1_0.1.refs_0_.refs_5_), channel_id=1, source_target_pairs={{1,0},{2,1},{3,2},{4,3},{5,4},{6,5},{7,6},{0,7},{9,8},{10,9},{11,1... | collective-permute-start | bytes 1572872 | tf_op jit(solution)/shard_map/ppermute | solution.py:276
  21.2 0.0 copy-done.1
  21.2 4.3 %sweep2.1 = (bf16[32,128,128]{2,1,0:T(8,128)(2,1)S(1)}, f32[16,128,128]{2,1,0:T(8,128)S(1)}, f32[16,128,128]{2,1,0:T(8,128)S(1)}) custom-call(s32[320]{0:T(512)S(1)} %add.257.index_ref, bf16[16,128,128]{2,1,0:T(8,128)(2,1)S(1)} %edge1_0.1.refs_0_.refs_5_, bf16[32,128,128]{2,1,0:T(8,128)(2,1)S(1)} %get-tuple-element.30.refs_1_.refs_6_, ...), custom_call_target="tpu_custom_call" | custom-call | tf_op jit(solution)/shard_map/sweep2/pallas_call | solution.py:37
  25.5 5.3 %collective-permute-done.2.halo_ref = bf16[16,128,128]{2,1,0:T(8,128)(2,1)S(1)} collective-permute-done((bf16[16,128,128]{2,1,0:T(8,128)(2,1)S(1)}, bf16[16,128,128]{2,1,0:T(8,128)(2,1)S(1)}, u32[]{:S(2)}, u32[]{:S(2)}) %collective-permute-start.2) | collective-permute-done | bytes 524320 | tf_op jit(solution)/shard_map/ppermute | solution.py:275
  30.8 1.0 %edge2_0.1.refs_2_ = bf16[16,128,128]{2,1,0:T(8,128)(2,1)S(1)} custom-call(s32[320]{0:T(512)S(1)} %add.257.index_ref, f32[16,128,128]{2,1,0:T(8,128)S(1)} %get-tuple-element.32.part_ref, bf16[320,128,128]{2,1,0:T(8,128)(2,1)S(1)} %get-tuple-element.29.h.refs_4_.refs_8_, bf16[16,128,128]{2,1,0:T(8,128)(2,1)S(1)} %collective-permute-done.2.halo_ref), custom_call_target="tpu_custom_call" | custom-call | tf_op jit(solution)/shard_map/edge2_0/pallas_call | solution.py:37
  31.9 0.1 collective-permute-start.8
  31.9 0.0 collective-permute-done.3.halo_ref
  32.0 1.0 %edge2_3.1.refs_4_ = bf16[16,128,128]{2,1,0:T(8,128)(2,1)S(1)} custom-call(s32[320]{0:T(512)S(1)} %add.257.index_ref, f32[16,128,128]{2,1,0:T(8,128)S(1)} %get-tuple-element.34.part_ref, bf16[320,128,128]{2,1,0:T(8,128)(2,1)S(1)} %get-tuple-element.29.h.refs_4_.refs_8_, bf16[16,128,128]{2,1,0:T(8,128)(2,1)S(1)} %collective-permute-done.3.halo_ref), custom_call_target="tpu_custom_call" | custom-call | tf_op jit(solution)/shard_map/edge2_3/pallas_call | solution.py:37
  33.0 0.6 collective-permute-start.7
  33.5 5.9 %sweep3.1 = (f32[16,128,128]{2,1,0:T(8,128)S(1)}, f32[16,128,128]{2,1,0:T(8,128)S(1)}, f32[528,128]{1,0:T(8,128)S(1)}, bf16[528,128]{1,0:T(8,128)(2,1)S(1)}, bf1...) custom-call(s32[320]{0:T(512)S(1)} %add.257.index_ref, s32[3]{0:T(128)S(1)} %pad_add_fusion.refs_0_.me_ref, ...), custom_call_target="tpu_custom_call" | custom-call | tf_op jit(solution)/shard_map/sweep3/pallas_call | solution.py:37
  39.5 1.7 %collective-permute-start.4 = (bf16[528,128]{1,0:T(8,128)(2,1)S(1)}, bf16[528,128]{1,0:T(8,128)(2,1)S(1)}, u32[]{:S(2)}, u32[]{:S(2)}) collective-permute-start(bf16[528,128]{1,0:T(8,128)(2,1)S(1)} %get-tuple-element.36), channel_id=1, source_target_pairs={{0,8},{8,16},{16,24},{24,0},{32,40},{40,48},{48,56},{56,32},{64,72... | collective-permute-start | bytes 405512 | tf_op jit(solution)/shard_map/ppermute | solution.py:257
  41.2 1.3 %collective-permute-start.5 = (bf16[528,128]{1,0:T(8,128)(2,1)S(1)}, bf16[528,128]{1,0:T(8,128)(2,1)S(1)}, u32[]{:S(2)}, u32[]{:S(2)}) collective-permute-start(bf16[528,128]{1,0:T(8,128)(2,1)S(1)} %get-tuple-element.37), channel_id=1, source_target_pairs={{0,16},{8,24},{16,0},{24,8},{32,48},{40,56},{48,32},{56,40},{64,80... | collective-permute-start | bytes 405512 | tf_op jit(solution)/shard_map/ppermute | solution.py:257
  42.5 1.9 %collective-permute-start.6 = (bf16[528,128]{1,0:T(8,128)(2,1)S(1)}, bf16[528,128]{1,0:T(8,128)(2,1)S(1)}, u32[]{:S(2)}, u32[]{:S(2)}) collective-permute-start(bf16[528,128]{1,0:T(8,128)(2,1)S(1)} %get-tuple-element.38), channel_id=1, source_target_pairs={{0,24},{8,0},{16,8},{24,16},{32,56},{40,32},{48,40},{56,48},{64,88... | collective-permute-start | bytes 405512 | tf_op jit(solution)/shard_map/ppermute | solution.py:257
  44.5 0.0 collective-permute-done.8.high_ref
  44.5 0.0 collective-permute-done.7.low_ref
  44.5 3.0 %last.1 = (f32[528,128]{1,0:T(8,128)S(1)}, bf16[528,128]{1,0:T(8,128)(2,1)S(1)}, bf16[528,128]{1,0:T(8,128)(2,1)S(1)}, bf16[528,128]{1,0:T(8,128)(2,1)S(1)}) custom-call(s32[320]{0:T(512)S(1)} %add.257.index_ref, s32[3]{0:T(128)S(1)} %pad_add_fusion.refs_0_.me_ref, f32[1,128]{1,0:T(1,128)S(1)} %sqrt_bitcast_fusion.refs_2_.refs_1_.root_ref, ...), custom_call_target="tpu_custom_call" | custom-call | tf_op jit(solution)/shard_map/last/pallas_call | solution.py:37
  47.5 0.9 %collective-permute-start.9 = (bf16[528,128]{1,0:T(8,128)(2,1)S(1)}, bf16[528,128]{1,0:T(8,128)(2,1)S(1)}, u32[]{:S(2)}, u32[]{:S(2)}) collective-permute-start(bf16[528,128]{1,0:T(8,128)(2,1)S(1)} %get-tuple-element.42), channel_id=1, source_target_pairs={{0,8},{8,16},{16,24},{24,0},{32,40},{40,48},{48,56},{56,32},{64,72... | collective-permute-start | bytes 405512 | tf_op jit(solution)/shard_map/ppermute | solution.py:257
  48.4 2.7 %collective-permute-start.10 = (bf16[528,128]{1,0:T(8,128)(2,1)S(1)}, bf16[528,128]{1,0:T(8,128)(2,1)S(1)}, u32[]{:S(2)}, u32[]{:S(2)}) collective-permute-start(bf16[528,128]{1,0:T(8,128)(2,1)S(1)} %get-tuple-element.43), channel_id=1, source_target_pairs={{0,16},{8,24},{16,0},{24,8},{32,48},{40,56},{48,32},{56,40},{64,80... | collective-permute-start | bytes 405512 | tf_op jit(solution)/shard_map/ppermute | solution.py:257
  51.1 0.0 collective-permute-done.4.refs_1_
  51.1 0.6 collective-permute-start.11
  51.7 0.0 collective-permute-done.5.refs_2_
  51.7 0.0 collective-permute-done.6.refs_3_
  51.7 1.7 %collective-permute-done.9.refs_5_ = bf16[528,128]{1,0:T(8,128)(2,1)S(1)} collective-permute-done((bf16[528,128]{1,0:T(8,128)(2,1)S(1)}, bf16[528,128]{1,0:T(8,128)(2,1)S(1)}, u32[]{:S(2)}, u32[]{:S(2)}) %collective-permute-start.9) | collective-permute-done | bytes 135200 | tf_op jit(solution)/shard_map/ppermute | solution.py:257
  53.4 3.0 %collective-permute-done.10.refs_6_ = bf16[528,128]{1,0:T(8,128)(2,1)S(1)} collective-permute-done((bf16[528,128]{1,0:T(8,128)(2,1)S(1)}, bf16[528,128]{1,0:T(8,128)(2,1)S(1)}, u32[]{:S(2)}, u32[]{:S(2)}) %collective-permute-start.10) | collective-permute-done | bytes 135200 | tf_op jit(solution)/shard_map/ppermute | solution.py:257
  56.4 1.7 %collective-permute-done.11.refs_7_ = bf16[528,128]{1,0:T(8,128)(2,1)S(1)} collective-permute-done((bf16[528,128]{1,0:T(8,128)(2,1)S(1)}, bf16[528,128]{1,0:T(8,128)(2,1)S(1)}, u32[]{:S(2)}, u32[]{:S(2)}) %collective-permute-start.11) | collective-permute-done | bytes 135200 | tf_op jit(solution)/shard_map/ppermute | solution.py:257
  58.1 0.7 second.1
  58.8 1.6 %collective-permute-start.12 = (bf16[288,128]{1,0:T(8,128)(2,1)S(1)}, bf16[288,128]{1,0:T(8,128)(2,1)S(1)}, u32[]{:S(2)}, u32[]{:S(2)}) collective-permute-start(bf16[288,128]{1,0:T(8,128)(2,1)S(1)} %get-tuple-element.46), channel_id=1, source_target_pairs={{0,32},{8,40},{16,48},{24,56},{32,64},{40,72},{48,80},{56,88},{64,... | collective-permute-start | bytes 221192 | tf_op jit(solution)/shard_map/ppermute | solution.py:257
  60.4 2.9 %collective-permute-start.13 = (bf16[288,128]{1,0:T(8,128)(2,1)S(1)}, bf16[288,128]{1,0:T(8,128)(2,1)S(1)}, u32[]{:S(2)}, u32[]{:S(2)}) collective-permute-start(bf16[288,128]{1,0:T(8,128)(2,1)S(1)} %get-tuple-element.47), channel_id=1, source_target_pairs={{0,64},{8,72},{16,80},{24,88},{32,96},{40,104},{48,112},{56,120},{... | collective-permute-start | bytes 221192 | tf_op jit(solution)/shard_map/ppermute | solution.py:257
  63.4 1.3 %collective-permute-start.14 = (bf16[288,128]{1,0:T(8,128)(2,1)S(1)}, bf16[288,128]{1,0:T(8,128)(2,1)S(1)}, u32[]{:S(2)}, u32[]{:S(2)}) collective-permute-start(bf16[288,128]{1,0:T(8,128)(2,1)S(1)} %get-tuple-element.48), channel_id=1, source_target_pairs={{0,96},{8,104},{16,112},{24,120},{32,0},{40,8},{48,16},{56,24},{64... | collective-permute-start | bytes 221192 | tf_op jit(solution)/shard_map/ppermute | solution.py:257
  64.7 0.6 collective-permute-done.12.refs_1_
  65.3 1.4 %collective-permute-done.13.refs_2_ = bf16[288,128]{1,0:T(8,128)(2,1)S(1)} collective-permute-done((bf16[288,128]{1,0:T(8,128)(2,1)S(1)}, bf16[288,128]{1,0:T(8,128)(2,1)S(1)}, u32[]{:S(2)}, u32[]{:S(2)}) %collective-permute-start.13) | collective-permute-done | bytes 73760 | tf_op jit(solution)/shard_map/ppermute | solution.py:257
  66.6 1.1 %collective-permute-done.14.refs_3_ = bf16[288,128]{1,0:T(8,128)(2,1)S(1)} collective-permute-done((bf16[288,128]{1,0:T(8,128)(2,1)S(1)}, bf16[288,128]{1,0:T(8,128)(2,1)S(1)}, u32[]{:S(2)}, u32[]{:S(2)}) %collective-permute-start.14) | collective-permute-done | bytes 73760 | tf_op jit(solution)/shard_map/ppermute | solution.py:257
  67.7 0.6 third.1
  68.3 7.1 %collective-permute-start.15 = (bf16[144,128]{1,0:T(8,128)(2,1)S(1)}, bf16[144,128]{1,0:T(8,128)(2,1)S(1)}, u32[]{:S(2)}, u32[]{:S(2)}) collective-permute-start(bf16[144,128]{1,0:T(8,128)(2,1)S(1)} %get-tuple-element.50), channel_id=1, source_target_pairs={{0,128},{8,136},{16,144},{24,152},{32,160},{40,168},{48,176},{56,1... | collective-permute-start | bytes 110600 | tf_op jit(solution)/shard_map/ppermute | solution.py:266
  75.3 1.9 %collective-permute-done.15.received_ref = bf16[144,128]{1,0:T(8,128)(2,1)S(1)} collective-permute-done((bf16[144,128]{1,0:T(8,128)(2,1)S(1)}, bf16[144,128]{1,0:T(8,128)(2,1)S(1)}, u32[]{:S(2)}, u32[]{:S(2)}) %collective-permute-start.15) | collective-permute-done | bytes 36896 | tf_op jit(solution)/shard_map/ppermute | solution.py:266
  77.3 0.9 %final.1 = f32[2,128,128]{2,1,0:T(8,128)} custom-call(f32[144,128]{1,0:T(8,128)S(1)} %get-tuple-element.49.own_ref, bf16[144,128]{1,0:T(8,128)(2,1)S(1)} %collective-permute-done.15.received_ref), custom_call_target="tpu_custom_call" | custom-call | tf_op jit(solution)/shard_map/final/pallas_call | solution.py:37
  (6 shorter events, 0.1 us)
Async XLA Ops:
  1.3 14.0 %collective-permute-start.1 = (bf16[16,128,128]{2,1,0:T(8,128)(2,1)S(1)}, bf16[16,128,128]{2,1,0:T(8,128)(2,1)S(1)}, u32[]{:S(2)}, u32[]{:S(2)}) collective-permute-start(bf16[16,128,128]{2,1,0:T(8,128)(2,1)S(1)} %get-tuple-element.51), channel_id=1, source_target_pairs={{1,0},{2,1},{3,2},{4,3},{5,4},{6,5},{7,6},{0,7},{9,8},{10,9},{11,1... | collective-permute-start | bytes 1572872 | tf_op jit(solution)/shard_map/ppermute | solution.py:276
  5.4 13.3 %collective-permute-start = (bf16[16,128,128]{2,1,0:T(8,128)(2,1)S(1)}, bf16[16,128,128]{2,1,0:T(8,128)(2,1)S(1)}, u32[]{:S(2)}, u32[]{:S(2)}) collective-permute-start(bf16[16,128,128]{2,1,0:T(8,128)(2,1)S(1)} %get-tuple-element.52), channel_id=1, source_target_pairs={{0,1},{1,2},{2,3},{3,4},{4,5},{5,6},{6,7},{7,0},{8,9},{9,10},{10,1... | collective-permute-start | bytes 1572872 | tf_op jit(solution)/shard_map/ppermute | solution.py:275
  7.2 1.6 %copy-start = (bf16[64,128,128]{2,1,0:T(8,128)(2,1)S(1)}, bf16[64,128,128]{2,1,0:T(8,128)(2,1)}, u32[]{:S(2)}) copy-start(bf16[64,128,128]{2,1,0:T(8,128)(2,1)} %refs_3_.1) | copy-start | bytes 6291460
  15.3 5.9 %copy-start.1 = (bf16[64,128,128]{2,1,0:T(8,128)(2,1)S(1)}, bf16[64,128,128]{2,1,0:T(8,128)(2,1)}, u32[]{:S(2)}) copy-start(bf16[64,128,128]{2,1,0:T(8,128)(2,1)} %refs_3_.1) | copy-start | bytes 6291460
  16.3 14.5 %collective-permute-start.2 = (bf16[16,128,128]{2,1,0:T(8,128)(2,1)S(1)}, bf16[16,128,128]{2,1,0:T(8,128)(2,1)S(1)}, u32[]{:S(2)}, u32[]{:S(2)}) collective-permute-start(bf16[16,128,128]{2,1,0:T(8,128)(2,1)S(1)} %edge1_3.1.refs_2_.refs_7_), channel_id=1, source_target_pairs={{0,1},{1,2},{2,3},{3,4},{4,5},{5,6},{6,7},{7,0},{8,9},{9,10},{10,1... | collective-permute-start | bytes 1572872 | tf_op jit(solution)/shard_map/ppermute | solution.py:275
  19.8 12.2 %collective-permute-start.3 = (bf16[16,128,128]{2,1,0:T(8,128)(2,1)S(1)}, bf16[16,128,128]{2,1,0:T(8,128)(2,1)S(1)}, u32[]{:S(2)}, u32[]{:S(2)}) collective-permute-start(bf16[16,128,128]{2,1,0:T(8,128)(2,1)S(1)} %edge1_0.1.refs_0_.refs_5_), channel_id=1, source_target_pairs={{1,0},{2,1},{3,2},{4,3},{5,4},{6,5},{7,6},{0,7},{9,8},{10,9},{11,1... | collective-permute-start | bytes 1572872 | tf_op jit(solution)/shard_map/ppermute | solution.py:276
  31.9 12.6 %collective-permute-start.8 = (bf16[16,128,128]{2,1,0:T(8,128)(2,1)S(1)}, bf16[16,128,128]{2,1,0:T(8,128)(2,1)S(1)}, u32[]{:S(2)}, u32[]{:S(2)}) collective-permute-start(bf16[16,128,128]{2,1,0:T(8,128)(2,1)S(1)} %edge2_0.1.refs_2_), channel_id=1, source_target_pairs={{1,0},{2,1},{3,2},{4,3},{5,4},{6,5},{7,6},{0,7},{9,8},{10,9},{11,1... | collective-permute-start | bytes 1572872 | tf_op jit(solution)/shard_map/ppermute | solution.py:276
  33.0 11.5 %collective-permute-start.7 = (bf16[16,128,128]{2,1,0:T(8,128)(2,1)S(1)}, bf16[16,128,128]{2,1,0:T(8,128)(2,1)S(1)}, u32[]{:S(2)}, u32[]{:S(2)}) collective-permute-start(bf16[16,128,128]{2,1,0:T(8,128)(2,1)S(1)} %edge2_3.1.refs_4_), channel_id=1, source_target_pairs={{0,1},{1,2},{2,3},{3,4},{4,5},{5,6},{6,7},{7,0},{8,9},{9,10},{10,1... | collective-permute-start | bytes 1572872 | tf_op jit(solution)/shard_map/ppermute | solution.py:275
  39.5 11.6 %collective-permute-start.4 = (bf16[528,128]{1,0:T(8,128)(2,1)S(1)}, bf16[528,128]{1,0:T(8,128)(2,1)S(1)}, u32[]{:S(2)}, u32[]{:S(2)}) collective-permute-start(bf16[528,128]{1,0:T(8,128)(2,1)S(1)} %get-tuple-element.36), channel_id=1, source_target_pairs={{0,8},{8,16},{16,24},{24,0},{32,40},{40,48},{48,56},{56,32},{64,72... | collective-permute-start | bytes 405512 | tf_op jit(solution)/shard_map/ppermute | solution.py:257
  41.2 10.5 %collective-permute-start.5 = (bf16[528,128]{1,0:T(8,128)(2,1)S(1)}, bf16[528,128]{1,0:T(8,128)(2,1)S(1)}, u32[]{:S(2)}, u32[]{:S(2)}) collective-permute-start(bf16[528,128]{1,0:T(8,128)(2,1)S(1)} %get-tuple-element.37), channel_id=1, source_target_pairs={{0,16},{8,24},{16,0},{24,8},{32,48},{40,56},{48,32},{56,40},{64,80... | collective-permute-start | bytes 405512 | tf_op jit(solution)/shard_map/ppermute | solution.py:257
  42.5 9.1 %collective-permute-start.6 = (bf16[528,128]{1,0:T(8,128)(2,1)S(1)}, bf16[528,128]{1,0:T(8,128)(2,1)S(1)}, u32[]{:S(2)}, u32[]{:S(2)}) collective-permute-start(bf16[528,128]{1,0:T(8,128)(2,1)S(1)} %get-tuple-element.38), channel_id=1, source_target_pairs={{0,24},{8,0},{16,8},{24,16},{32,56},{40,32},{48,40},{56,48},{64,88... | collective-permute-start | bytes 405512 | tf_op jit(solution)/shard_map/ppermute | solution.py:257
  47.5 5.9 %collective-permute-start.9 = (bf16[528,128]{1,0:T(8,128)(2,1)S(1)}, bf16[528,128]{1,0:T(8,128)(2,1)S(1)}, u32[]{:S(2)}, u32[]{:S(2)}) collective-permute-start(bf16[528,128]{1,0:T(8,128)(2,1)S(1)} %get-tuple-element.42), channel_id=1, source_target_pairs={{0,8},{8,16},{16,24},{24,0},{32,40},{40,48},{48,56},{56,32},{64,72... | collective-permute-start | bytes 405512 | tf_op jit(solution)/shard_map/ppermute | solution.py:257
  48.4 8.0 %collective-permute-start.10 = (bf16[528,128]{1,0:T(8,128)(2,1)S(1)}, bf16[528,128]{1,0:T(8,128)(2,1)S(1)}, u32[]{:S(2)}, u32[]{:S(2)}) collective-permute-start(bf16[528,128]{1,0:T(8,128)(2,1)S(1)} %get-tuple-element.43), channel_id=1, source_target_pairs={{0,16},{8,24},{16,0},{24,8},{32,48},{40,56},{48,32},{56,40},{64,80... | collective-permute-start | bytes 405512 | tf_op jit(solution)/shard_map/ppermute | solution.py:257
  51.1 7.0 %collective-permute-start.11 = (bf16[528,128]{1,0:T(8,128)(2,1)S(1)}, bf16[528,128]{1,0:T(8,128)(2,1)S(1)}, u32[]{:S(2)}, u32[]{:S(2)}) collective-permute-start(bf16[528,128]{1,0:T(8,128)(2,1)S(1)} %get-tuple-element.44), channel_id=1, source_target_pairs={{0,24},{8,0},{16,8},{24,16},{32,56},{40,32},{48,40},{56,48},{64,88... | collective-permute-start | bytes 405512 | tf_op jit(solution)/shard_map/ppermute | solution.py:257
  58.8 6.4 %collective-permute-start.12 = (bf16[288,128]{1,0:T(8,128)(2,1)S(1)}, bf16[288,128]{1,0:T(8,128)(2,1)S(1)}, u32[]{:S(2)}, u32[]{:S(2)}) collective-permute-start(bf16[288,128]{1,0:T(8,128)(2,1)S(1)} %get-tuple-element.46), channel_id=1, source_target_pairs={{0,32},{8,40},{16,48},{24,56},{32,64},{40,72},{48,80},{56,88},{64,... | collective-permute-start | bytes 221192 | tf_op jit(solution)/shard_map/ppermute | solution.py:257
  60.4 6.2 %collective-permute-start.13 = (bf16[288,128]{1,0:T(8,128)(2,1)S(1)}, bf16[288,128]{1,0:T(8,128)(2,1)S(1)}, u32[]{:S(2)}, u32[]{:S(2)}) collective-permute-start(bf16[288,128]{1,0:T(8,128)(2,1)S(1)} %get-tuple-element.47), channel_id=1, source_target_pairs={{0,64},{8,72},{16,80},{24,88},{32,96},{40,104},{48,112},{56,120},{... | collective-permute-start | bytes 221192 | tf_op jit(solution)/shard_map/ppermute | solution.py:257
  63.4 4.4 %collective-permute-start.14 = (bf16[288,128]{1,0:T(8,128)(2,1)S(1)}, bf16[288,128]{1,0:T(8,128)(2,1)S(1)}, u32[]{:S(2)}, u32[]{:S(2)}) collective-permute-start(bf16[288,128]{1,0:T(8,128)(2,1)S(1)} %get-tuple-element.48), channel_id=1, source_target_pairs={{0,96},{8,104},{16,112},{24,120},{32,0},{40,8},{48,16},{56,24},{64... | collective-permute-start | bytes 221192 | tf_op jit(solution)/shard_map/ppermute | solution.py:257
  68.3 9.0 %collective-permute-start.15 = (bf16[144,128]{1,0:T(8,128)(2,1)S(1)}, bf16[144,128]{1,0:T(8,128)(2,1)S(1)}, u32[]{:S(2)}, u32[]{:S(2)}) collective-permute-start(bf16[144,128]{1,0:T(8,128)(2,1)S(1)} %get-tuple-element.50), channel_id=1, source_target_pairs={{0,128},{8,136},{16,144},{24,152},{32,160},{40,168},{48,176},{56,1... | collective-permute-start | bytes 110600 | tf_op jit(solution)/shard_map/ppermute | solution.py:266

commit v3 on v0

v3 whole, which is shorter than its diff:
```python
import functools

import jax
import jax.numpy as jnp
from jax import lax
from jax.experimental import pallas as pl
from jax.experimental.pallas import tpu as pltpu
from jax.sharding import PartitionSpec as P


EY = 16
EXS = 4
EX = 32
NB = 128
HALF = NB // 2
NBAND = 4096
XS = 4
YS = 4
PART = EY // 2
PAIR = 2 * HALF
WIDE = 8 * HALF + 16
THIN = PAIR + 16

BF = jnp.bfloat16
F32 = jnp.float32
VMEM = pltpu.VMEM
LIMIT = 16 << 20
RUN = PART * 5
SMEM_SPEC = pl.BlockSpec(memory_space=pltpu.SMEM)
VMEM_SPEC = pl.BlockSpec(memory_space=VMEM)

FAR, NEAR = 0, 3
SELF, INWARD, OUTWARD, RIGHT, LEFT = range(5)


def struct(shape, dtype):
    return jax.ShapeDtypeStruct(shape, dtype)


def call(kernel, outs, scalars, arrays, scratch=(), out_specs=None, hbm=()):
    arrays = [pltpu.with_memory_space_constraint(a, VMEM) for a in arrays]
    return pl.pallas_call(
        kernel,
        out_shape=outs,
        in_specs=[SMEM_SPEC] * len(scalars)
        + [VMEM_SPEC] * len(arrays)
        + [pl.BlockSpec(memory_space=pltpu.HBM)] * len(hbm),
        out_specs=out_specs or [VMEM_SPEC] * len(outs),
        scratch_shapes=list(scratch),
        compiler_params=pltpu.CompilerParams(vmem_limit_bytes=LIMIT),
    )(*scalars, *arrays, *[pltpu.with_memory_space_constraint(a, pltpu.HBM) for a in hbm])


def dot(a, b):
    return jnp.dot(a, b, preferred_element_type=F32)


def gram(a, b):
    return lax.dot_general(a, b, (((1,), (1,)), ((), ())), preferred_element_type=F32)


def odd():
    return lax.axis_index("strip") & 1


def place(stage):
    band = lax.axis_index("band")
    x, y = band & 3, band >> 2 & 3
    return jnp.where(odd() == stage, x, y)


def row_base(row):
    return (row + odd() * (EXS - 1 - 2 * row)) * EY


def start_kernel(c_ref, fa_ref, fb_ref, near_ref, sem):
    far, near = row_base(FAR), row_base(NEAR)
    copies = [
        pltpu.make_async_copy(c_ref.at[pl.ds(at, size)], ref, sem.at[n])
        for n, (at, size, ref) in enumerate(
            ((far, PART, fa_ref), (far + PART, PART, fb_ref), (near, EY, near_ref))
        )
    ]
    for copy in copies:
        copy.start()
    for copy in copies:
        copy.wait()


def fill_places(adj_ref, table):
    local = lax.broadcasted_iota(jnp.int32, (1, EXS * EY), 1)
    row = lax.axis_index("strip") * EXS + (local >> 4)
    col = local & (EY - 1)
    inward = 1 - 2 * odd()
    wanted = {
        SELF: (row, col),
        INWARD: (row + inward & EX - 1, col),
        OUTWARD: (row - inward & EX - 1, col),
        RIGHT: (row, col + 1 & EY - 1),
        LEFT: (row, col - 1 & EY - 1),
    }
    for k, (r, c) in wanted.items():
        slot = sum(jnp.where(adj_ref[j : j + 1, :] == r * EY + c, j, 0) for j in range(1, 5))
        table[k : k + 1, : EXS * EY] = local * 5 + slot


def pack(v, ref, at):
    row = lax.broadcasted_iota(jnp.int32, (HALF, NB), 0)
    col = lax.broadcasted_iota(jnp.int32, (HALF, NB), 1) - HALF
    top, bottom = v[:HALF], v[HALF:]
    low = gram(bottom, v)
    high = gram(top, jnp.concatenate([bottom, top], axis=0))
    packed = jnp.where((col >= 0) & (col < row), high, low)
    ref[at * HALF : (at + 1) * HALF, :] = packed.astype(ref.dtype)
    return jnp.sum(jnp.where(col == row, high, 0.0), axis=0, keepdims=True)


def pack_groups(s_ref, outs):
    tile_row = lax.broadcasted_iota(jnp.int32, (16, NB), 0)
    turn, me = odd(), place(0)
    for s in range(XS):
        to = me ^ s
        diagonals = jnp.zeros((16, NB), F32)
        for j in range(8):
            at = jnp.where(turn == 1, to * 8 + j, j // 2 * 8 + 2 * to + j % 2)
            diagonals = jnp.where(tile_row == j, pack(s_ref[at], outs[s], j), diagonals)
        outs[s][8 * HALF :, :] = diagonals.astype(outs[s].dtype)


def group_structs(rows):
    return [struct((rows, NB), F32)] + [struct((rows, NB), BF)] * 3


def apply_row(row, first, count, index_ref, h, value, past, halo, put):
    base = row_base(row)

    def element(n, carry):
        c = first + n
        terms = [
            (SELF, value(row, c)),
            (RIGHT, value(row, c + 1 & EY - 1)),
            (LEFT, value(row, c - 1 & EY - 1)),
        ]
        if row < NEAR:
            terms.append((INWARD, value(row + 1, c)))
        elif halo is not None:
            terms.append((INWARD, halo[c]))
        if row > FAR:
            terms.append((OUTWARD, value(row - 1, c)))
        a = jnp.concatenate([h[index_ref[k, base + c]] for k, _ in terms], axis=1)
        b = jnp.concatenate([v for _, v in terms], axis=0)
        total = dot(a, b)
        if past is not None:
            total = 2.0 * total - past(row, c).astype(F32)
        put(c, total)
        return carry

    lax.fori_loop(0, count, element, 0, unroll=PART)


def putter(ref, root=None):
    def put(c, total):
        ref[c] = (total if root is None else total * root).astype(ref.dtype)

    return put


def first_kernel(adj_hbm, occ_hbm, c_ref, h_ref, *refs):
    index_ref, root_ref, part_ref, x_ref, y_ref, near_ref, v_ref, h, adj, occ, table, sem = refs
    small = [
        pltpu.make_async_copy(adj_hbm, adj, sem.at[0]),
        pltpu.make_async_copy(occ_hbm, occ, sem.at[1]),
    ]
    place = pltpu.make_async_copy(table, index_ref, sem.at[2])
    fields, runs = [], []
    for row in range(EXS):
        span = pl.ds(row_base(row), EY)
        fields.append(pltpu.make_async_copy(c_ref.at[span], v_ref.at[span], sem.at[3 + row]))
        for n in range(2):
            span = pl.ds(row_base(row) * 5 + n * RUN, RUN)
            at = 3 + EXS + len(runs)
            runs.append(pltpu.make_async_copy(h_ref.at[span], h.at[span], sem.at[at]))
    order = small + fields[:2] + runs[:2]
    for row in range(1, EXS):
        order += fields[row + 1 : row + 2] + runs[2 * row : 2 * row + 2]
    for copy in order:
        copy.start()
    for copy in small:
        copy.wait()
    fill_places(adj, table)
    place.start()
    root_ref[...] = jnp.sqrt(occ[...])
    place.wait()
    fields[0].wait()
    value = lambda row, c: v_ref[row_base(row) + c]
    for row, out in enumerate((part_ref, x_ref, y_ref, near_ref)):
        if row < NEAR:
            fields[row + 1].wait()
        for n in range(2):
            runs[2 * row + n].wait()
            apply_row(row, n * PART, PART, index_ref, h, value, None, None, putter(out))


def inner_kernel(rows, index_ref, x, y, near, halo, h, *refs):
    past_ref, *outs = refs
    value = lambda row, c: (None, x, y, near)[row][c]
    past = lambda row, c: past_ref[row_base(row) + c]
    for row, out in zip(rows, outs):
        apply_row(row, 0, EY, index_ref, h, value, past, halo, putter(out))


def second_sweep_kernel(index_ref, fa, fb, x, y, near, h, past_ref, part_ref, x_out, y_out, far):
    far[:PART] = fa[...]
    far[PART:] = fb[...]
    value = lambda row, c: (far, x, y, near)[row][c]
    past = lambda row, c: past_ref[row_base(row) + c]
    for row, out in enumerate((part_ref, x_out, y_out)):
        apply_row(row, 0, EY, index_ref, h, value, past, None, putter(out))


def early_kernel(index_ref, root_ref, x, y, near, halo, h, past_y, past_near, *refs):
    outs, s_ref = refs[:-1], refs[-1]
    root = root_ref[...]
    value = lambda row, c: (None, x, y, near)[row][c]
    past = lambda row, c: (None, None, past_y, past_near)[row][c]
    for row, at in ((2, odd()), (NEAR, 1 - odd())):
        put = putter(s_ref.at[pl.ds(at * EY, EY)], root)
        apply_row(row, 0, EY, index_ref, h, value, past, halo, put)
    pack_groups(s_ref, outs)


def third_sweep_kernel(index_ref, root_ref, fa, fb, x, y, h, pa, pb, px, part_ref, x_out, far, pfar):
    far[:PART] = fa[...]
    far[PART:] = fb[...]
    pfar[:PART] = pa[...]
    pfar[PART:] = pb[...]
    root = root_ref[...]
    value = lambda row, c: (far, x, y)[row][c]
    past = lambda row, c: (pfar, px)[row][c]
    for row, out in ((FAR, putter(part_ref)), (1, putter(x_out, root))):
        apply_row(row, 0, EY, index_ref, h, value, past, None, out)


def last_kernel(index_ref, root_ref, part_ref, h, halo_a, halo_b, x, *refs):
    outs, s_ref = refs[:-1], refs[-1]
    root = root_ref[...]
    base = row_base(FAR)
    at = odd() * EY
    s_ref[pl.ds(EY - at, EY)] = x[...]
    for first, halo in ((0, halo_a), (PART, halo_b)):
        for c in range(PART):
            term = dot(h[index_ref[OUTWARD, base + first + c]], halo[c])
            s_ref[at + first + c] = ((part_ref[first + c] + 2.0 * term) * root).astype(BF)
    pack_groups(s_ref, outs)


def edge_kernel(level, row, first, index_ref, part_ref, h, halo_ref, out_ref):
    scale = 1.0 if level == 1 else 2.0
    way = OUTWARD if row == FAR else INWARD
    base = row_base(row) + first
    for c in range(out_ref.shape[0]):
        term = dot(h[index_ref[way, base + c]], halo_ref[c])
        out_ref[c] = (part_ref[first + c] + scale * term).astype(BF)


def edge(level, row, first, index, part, h, halo):
    return call(
        functools.partial(edge_kernel, level, row, first),
        [struct(halo.shape, BF)],
        [index],
        [part, h, halo],
    )[0]


def second_kernel(*refs):
    pairs, outs = (refs[:XS], refs[XS : 2 * XS]), refs[2 * XS :]
    me = place(1)
    for n, srcs in enumerate(pairs):
        tail = sum(src[8 * HALF :, :].astype(F32) for src in srcs)
        at = n * THIN
        for t in range(YS):
            to = me ^ t
            span = pl.ds(pl.multiple_of(to * PAIR, PAIR), PAIR)
            total = sum(src[span, :].astype(F32) for src in srcs)
            outs[t][at : at + PAIR, :] = total.astype(outs[t].dtype)
            turned = pltpu.roll(tail, lax.rem(16 - 2 * to, 16), 0)
            outs[t][at + PAIR : at + THIN, :] = turned.astype(outs[t].dtype)


def third_kernel(*refs):
    srcs, (own_ref, sent_ref) = refs[:YS], refs[YS:]
    own_late = 1 - (lax.axis_index("band") >> 4 ^ odd())
    own = pl.ds(pl.multiple_of(own_late * THIN, 16), THIN)
    other = pl.ds(pl.multiple_of((1 - own_late) * THIN, 16), THIN)
    own_ref[...] = sum(src[own, :].astype(F32) for src in srcs)
    sent_ref[...] = sum(src[other, :].astype(F32) for src in srcs).astype(BF)


def final_kernel(own_ref, received_ref, out_ref):
    row = lax.broadcasted_iota(jnp.int32, (HALF, HALF), 0)
    col = lax.broadcasted_iota(jnp.int32, (HALF, HALF), 1)
    total = (own_ref[...] + received_ref[...].astype(F32)) * (1.0 / NBAND)
    for k in range(2):
        u = total[k * HALF : (k + 1) * HALF]
        b, w = u[:, :HALF], u[:, HALF:]
        turned = u.T
        b_t, w_t = turned[:HALF], turned[HALF:]
        diagonal = total[PAIR + k : PAIR + k + 1, HALF:]
        a = jnp.where(col < row, w, w_t)
        a = jnp.where(col == row, diagonal, a)
        c = jnp.where(col >= row, w, w_t)
        out_ref[k, :HALF, :] = jnp.concatenate([a, b_t], axis=1)
        out_ref[k, HALF:, :] = jnp.concatenate([b, c], axis=1)


def exchanged(pieces, stage):
    bands, strips = lax.axis_size("band"), lax.axis_size("strip")
    arrived = [pieces[0]]
    for s in (2, 1, 3):
        pairs = []
        for strip in range(strips):
            step = 1 if strip % 2 == stage else XS
            pairs += [(b * strips + strip, (b ^ s * step) * strips + strip) for b in range(bands)]
        arrived.append(lax.ppermute(pieces[s], ("band", "strip"), pairs))
    return arrived


def across(array):
    half = XS * YS
    return lax.ppermute(array, "band", [(b, (b + half) % (2 * half)) for b in range(2 * half)])


def swapped(array, first):
    count = lax.axis_size("strip")
    pairs = []
    for i in range(first, first + count, 2):
        a, b = i % count, (i + 1) % count
        pairs += [(a, b), (b, a)]
    return lax.ppermute(array, "strip", pairs)


def stage(kernel, outs, scalars, arrays, *more, **options):
    return call(kernel, outs, scalars, arrays, *more, **options)


def program(coeffs, hamiltonian, adjacency, occupation):
    h = hamiltonian.reshape(-1, NB, NB)
    row, part = struct((EY, NB, NB), BF), struct((PART, NB, NB), BF)
    wide = struct((EY, NB, NB), F32)
    scratch = VMEM(row.shape, BF)
    fa, fb, near = stage(
        start_kernel, [part, part, row], [], [], [pltpu.SemaphoreType.DMA((3,))], hbm=[coeffs]
    )
    fa_in, fb_in = swapped(fa, 1), swapped(fb, 1)
    near_in = swapped(near, 0)
    table = struct((8, NB), jnp.int32)
    outs = [table, struct((1, NB), F32), wide, row, row, wide, struct(coeffs.shape, BF)]
    index, root, far, x1, y1, near, field, h = stage(
        first_kernel,
        outs + [struct(h.shape, BF)],
        [],
        [],
        [
            VMEM((5, EXS * EY), jnp.int32),
            VMEM((1, NB), F32),
            VMEM(table.shape, jnp.int32),
            pltpu.SemaphoreType.DMA((3 + 3 * EXS,)),
        ],
        [SMEM_SPEC] + [VMEM_SPEC] * len(outs),
        hbm=[adjacency.T, occupation.reshape(1, NB), coeffs, h],
    )
    near1 = edge(1, NEAR, 0, index, near, h, near_in)
    near_in = swapped(near1, 0)
    fa1 = edge(1, FAR, 0, index, far, h, fa_in)
    fa_in = swapped(fa1, 1)
    fb1 = edge(1, FAR, PART, index, far, h, fb_in)
    fb_in = swapped(fb1, 1)
    inner = functools.partial(inner_kernel, (NEAR,))
    (near2,) = stage(inner, [row], [index], [x1, y1, near1, near_in, h, field])
    near_in = swapped(near2, 0)
    far, x2, y2 = stage(
        second_sweep_kernel,
        [wide, row, row],
        [index],
        [fa1, fb1, x1, y1, near1, h, field],
        [scratch],
    )
    fa2 = edge(2, FAR, 0, index, far, h, fa_in)
    fa_in = swapped(fa2, 1)
    early = stage(
        early_kernel,
        group_structs(WIDE),
        [index],
        [root, x2, y2, near2, near_in, h, y1, near1],
        [VMEM((2 * EY, NB, NB), BF)],
    )
    fb2 = edge(2, FAR, PART, index, far, h, fb_in)
    fb_in = swapped(fb2, 1)
    early = exchanged(early, 0)
    far, x = stage(
        third_sweep_kernel,
        [wide, row],
        [index],
        [root, fa2, fb2, x2, y2, h, fa1, fb1, x1],
        [scratch, scratch],
    )
    late = stage(
        last_kernel,
        group_structs(WIDE),
        [index],
        [root, far, h, fa_in, fb_in, x],
        [VMEM((2 * EY, NB, NB), BF)],
    )
    late = exchanged(late, 0)
    both = stage(second_kernel, group_structs(2 * THIN), [], [*early, *late])
    thin = [struct((THIN, NB), F32), struct((THIN, NB), BF)]
    own, sent = stage(third_kernel, thin, [], exchanged(both, 1))
    return stage(final_kernel, [struct((2, NB, NB), F32)], [], [own, across(sent)])[0]


def solution(mesh):
    return jax.shard_map(
        program,
        mesh=mesh,
        in_specs=(
            P("strip", None, "band"),
            P("strip", None, None, None),
            P("strip", None),
            P("band"),
        ),
        out_specs=P(("strip", "band"), None, None),
        check_vma=False,
    )
```

time: 207 us -> 89.1 us (0.43)
  local copies, waits for them, and re-layouts: 62.5 us -> 0 us
  waiting for transfers between devices: 55.8 us -> 25.8 us
  matrix products: 29.1 us -> 0 us
  Pallas kernels: 0 us -> 26.7 us
  starting transfers between devices: 50.3 us -> 35.2 us
  other arithmetic: 7.99 us -> 0 us
    gather x4 -> x0, local copies, waits for them, and re-layouts: 46.7 us -> none  [apply_operator(): picked = jnp.take(padded, local_index, axis=0)]
    all_to_all x3 -> x0, waiting for transfers between devices: 40.1 us -> none  [the longest x2 40.1 us: items_in_groups(): lax.all_to_all(group, axis, split_axis=split_dim, concat_axis=concat_dim,...]
    all_to_all x3 -> x0, starting transfers between devices: 38.9 us -> none  [the longest x2 22 us: items_in_groups(): lax.all_to_all(group, axis, split_axis=split_dim, concat_axis=concat_dim,...]
    dot_general x5 -> x0, matrix products: 29.1 us -> none  [the longest x3 28.2 us: apply_operator(): jnp.einsum('ejik,ejkb->eib', hamiltonian, picked, preferred_element_type=...]
    pallas_call x0 -> x15, Pallas kernels: none -> 26.7 us  [call(): pl.pallas_call(kernel, out_shape=outs, in_specs=[SMEM_SPEC] * len(scalars...]
    ppermute x6 -> x19, starting transfers between devices: 11.3 us -> 35.2 us  [the longest x9 16.1 us: swapped(): return lax.ppermute(array, 'strip', pairs)]
    unnamed x23 -> x0, local copies, waits for them, and re-layouts: 11.3 us -> none
    ppermute x6 -> x19, waiting for transfers between devices: 15.7 us -> 25.8 us  [the longest x9 14.2 us: swapped(): return lax.ppermute(array, 'strip', pairs)]
  transfers between devices with their start and end apart: 9 -> 19, of which waited for: 5 -> 12; matrix products, arithmetic and copies ran while one was open for 15% -> 0% of each run, Pallas kernels for 0% -> 27%
where the time goes in v3:
time: 89.1 us; the launch traced here: 87.8 us
  starting transfers between devices  35.2 us (40%)
  Pallas kernels  26.7 us (30%)
  waiting for transfers between devices  25.8 us (29%)
    pallas_call x15, Pallas kernels, call(): pl.pallas_call(kernel, out_shape=outs, in_specs=[SMEM_SPEC] * len(scalars...  26.7 us
    ppermute x9, starting transfers between devices, swapped(): return lax.ppermute(array, 'strip', pairs)  16.1 us
    ppermute x9, waiting for transfers between devices, swapped(): return lax.ppermute(array, 'strip', pairs)  14.2 us
    ppermute x9, starting transfers between devices, exchanged(): arrived.append(lax.ppermute(pieces[s], ('band', 'strip'), pairs))  12.7 us
    ppermute x9, waiting for transfers between devices, exchanged(): arrived.append(lax.ppermute(pieces[s], ('band', 'strip'), pairs))  9.65 us
    ppermute x1, starting transfers between devices, across(): lax.ppermute(array, 'band', [(b, (b + half) % (2 * half)) for b in range(...  6.41 us
    ppermute x1, waiting for transfers between devices, across(): lax.ppermute(array, 'band', [(b, (b + half) % (2 * half)) for b in range(...  1.94 us
  transfers between devices with their start and end apart: 19, of which 12 were waited for; matrix products, arithmetic and copies ran while one was open for 0% of the time, Pallas kernels for 27%

profile of v3, /device:TPU:2, one launch (start us, length us, event | category | flops | bytes accessed | tf_op | source)
XLA Modules:
  0.0 87.8 jit_solution(11665078001916216712)
XLA Ops:
  0.0 1.2 %shard_map.47 = (bf16[8,128,128]{2,1,0:T(8,128)(2,1)S(1)}, bf16[8,128,128]{2,1,0:T(8,128)(2,1)S(1)}, bf16[16,128,128]{2,1,0:T(8,128)(2,1)S(1)}) custom-call(bf16[64,128,128]{2,1,0:T(8,128)(2,1)} %c_ref.3), custom_call_target="tpu_custom_call" | custom-call | tf_op jit(solution)/shard_map/pallas_call | solution.py:42
  1.2 0.1 collective-permute-start.2
  1.3 6.1 %shard_map.46 = (s32[8,128]{1,0:T(8,128)S(1)}, f32[1,128]{1,0:T(1,128)S(1)}, f32[16,128,128]{2,1,0:T(8,128)S(1)}, bf16[16,128,128]{2,1,0:T(8,128)(2,1)S(1)}, bf1...) custom-call(s32[5,64]{1,0:T(8,128)} %bitcast.4, ...), custom_call_target="tpu_custom_call" | custom-call | tf_op jit(solution)/shard_map/pallas_call | solution.py:42
  7.4 0.0 collective-permute-done.2.halo_ref
  7.4 0.9 %shard_map.50.near.past_near = bf16[16,128,128]{2,1,0:T(8,128)(2,1)S(1)} custom-call(s32[8,128]{1,0:T(8,128)S(1)} %get-tuple-element.35.index_ref, f32[16,128,128]{2,1,0:T(8,128)S(1)} %get-tuple-element.43.part_ref, bf16[320,128,128]{2,1,0:T(8,128)(2,1)S(1)} %get-tuple-element.38.h, bf16[16,128,128]{2,1,0:T(8,128)(2,1)S(1)} %collective-permute-done.2.halo_ref), custom_call_target="tpu_custom_call" | custom-call | tf_op jit(solution)/shard_map/pallas_call | solution.py:42
  8.3 0.6 collective-permute-start.3
  8.9 4.3 %collective-permute-start = (bf16[8,128,128]{2,1,0:T(8,128)(2,1)S(1)}, bf16[8,128,128]{2,1,0:T(8,128)(2,1)S(1)}, u32[]{:S(2)}, u32[]{:S(2)}) collective-permute-start(bf16[8,128,128]{2,1,0:T(8,128)(2,1)S(1)} %get-tuple-element.39), channel_id=1, source_target_pairs={{1,2},{2,1},{3,4},{4,3},{5,6},{6,5},{7,0},{0,7},{9,10},{10,9},{11,... | collective-permute-start | bytes 786440 | tf_op jit(solution)/shard_map/ppermute | solution.py:339
  13.2 0.1 collective-permute-start.1
  13.3 6.6 %collective-permute-done.halo_ref = bf16[8,128,128]{2,1,0:T(8,128)(2,1)S(1)} collective-permute-done((bf16[8,128,128]{2,1,0:T(8,128)(2,1)S(1)}, bf16[8,128,128]{2,1,0:T(8,128)(2,1)S(1)}, u32[]{:S(2)}, u32[]{:S(2)}) %collective-permute-start) | collective-permute-done | bytes 262176 | tf_op jit(solution)/shard_map/ppermute | solution.py:339
  19.9 0.8 shard_map.48.fa.pa
  20.8 3.8 %collective-permute-start.8 = (bf16[8,128,128]{2,1,0:T(8,128)(2,1)S(1)}, bf16[8,128,128]{2,1,0:T(8,128)(2,1)S(1)}, u32[]{:S(2)}, u32[]{:S(2)}) collective-permute-start(bf16[8,128,128]{2,1,0:T(8,128)(2,1)S(1)} %shard_map.48.fa.pa), channel_id=1, source_target_pairs={{1,2},{2,1},{3,4},{4,3},{5,6},{6,5},{7,0},{0,7},{9,10},{10,9},{11,... | collective-permute-start | bytes 786440 | tf_op jit(solution)/shard_map/ppermute | solution.py:339
  24.6 1.0 %collective-permute-done.1.halo_ref = bf16[8,128,128]{2,1,0:T(8,128)(2,1)S(1)} collective-permute-done((bf16[8,128,128]{2,1,0:T(8,128)(2,1)S(1)}, bf16[8,128,128]{2,1,0:T(8,128)(2,1)S(1)}, u32[]{:S(2)}, u32[]{:S(2)}) %collective-permute-start.1) | collective-permute-done | bytes 262176 | tf_op jit(solution)/shard_map/ppermute | solution.py:339
  25.6 0.8 shard_map.49.fb.pb
  26.4 3.8 %collective-permute-start.9 = (bf16[8,128,128]{2,1,0:T(8,128)(2,1)S(1)}, bf16[8,128,128]{2,1,0:T(8,128)(2,1)S(1)}, u32[]{:S(2)}, u32[]{:S(2)}) collective-permute-start(bf16[8,128,128]{2,1,0:T(8,128)(2,1)S(1)} %shard_map.49.fb.pb), channel_id=1, source_target_pairs={{1,2},{2,1},{3,4},{4,3},{5,6},{6,5},{7,0},{0,7},{9,10},{10,9},{11,... | collective-permute-start | bytes 786440 | tf_op jit(solution)/shard_map/ppermute | solution.py:339
  30.2 0.0 collective-permute-done.3.halo
  30.2 1.6 %shard_map.52.near = bf16[16,128,128]{2,1,0:T(8,128)(2,1)S(1)} custom-call(s32[8,128]{1,0:T(8,128)S(1)} %get-tuple-element.35.index_ref, bf16[16,128,128]{2,1,0:T(8,128)(2,1)S(1)} %get-tuple-element.41.x.px, bf16[16,128,128]{2,1,0:T(8,128)(2,1)S(1)} %get-tuple-element.42.y.past_y, bf16[16,128,128]{2,1,0:T(8,128)(2,1)S(1)} %shard_map.50.near.past_near, ...), custom_call_target="tpu_custom_call" | custom-call | tf_op jit(solution)/shard_map/pallas_call | solution.py:42
  31.8 0.1 collective-permute-start.4
  31.9 3.6 %shard_map.51 = (f32[16,128,128]{2,1,0:T(8,128)S(1)}, bf16[16,128,128]{2,1,0:T(8,128)(2,1)S(1)}, bf16[16,128,128]{2,1,0:T(8,128)(2,1)S(1)}) custom-call(s32[8,128]{1,0:T(8,128)S(1)} %get-tuple-element.35.index_ref, bf16[8,128,128]{2,1,0:T(8,128)(2,1)S(1)} %shard_map.48.fa.pa, bf16[8,128,128]{2,1,0:T(8,128)(2,1)S(1)} %shard_map.49.fb.pb, ...), custom_call_target="tpu_custom_call" | custom-call | tf_op jit(solution)/shard_map/pallas_call | solution.py:42
  35.5 0.0 collective-permute-done.8.halo_ref
  35.5 0.8 shard_map.54.fa
  36.4 0.1 collective-permute-start.10
  36.5 0.6 collective-permute-done.9.halo_ref
  37.1 0.8 shard_map.55.fb
  37.9 3.2 %collective-permute-start.11 = (bf16[8,128,128]{2,1,0:T(8,128)(2,1)S(1)}, bf16[8,128,128]{2,1,0:T(8,128)(2,1)S(1)}, u32[]{:S(2)}, u32[]{:S(2)}) collective-permute-start(bf16[8,128,128]{2,1,0:T(8,128)(2,1)S(1)} %shard_map.55.fb), channel_id=1, source_target_pairs={{1,2},{2,1},{3,4},{4,3},{5,6},{6,5},{7,0},{0,7},{9,10},{10,9},{11,... | collective-permute-start | bytes 786440 | tf_op jit(solution)/shard_map/ppermute | solution.py:339
  41.1 2.6 %shard_map.56 = (f32[16,128,128]{2,1,0:T(8,128)S(1)}, bf16[16,128,128]{2,1,0:T(8,128)(2,1)S(1)}) custom-call(s32[8,128]{1,0:T(8,128)S(1)} %get-tuple-element.35.index_ref, f32[1,128]{1,0:T(1,128)S(1)} %get-tuple-element.36.root_ref, bf16[8,128,128]{2,1,0:T(8,128)(2,1)S(1)} %shard_map.54.fa, bf16[8,128,128]{2,1,0:T(8,128)(2,1)S(1)} %shard_map.55.fb, ...), custom_call_target="tpu_custom_call" | custom-call | tf_op jit(solution)/shard_map/pallas_call | solution.py:42
  43.7 2.8 %collective-permute-done.10.halo_a = bf16[8,128,128]{2,1,0:T(8,128)(2,1)S(1)} collective-permute-done((bf16[8,128,128]{2,1,0:T(8,128)(2,1)S(1)}, bf16[8,128,128]{2,1,0:T(8,128)(2,1)S(1)}, u32[]{:S(2)}, u32[]{:S(2)}) %collective-permute-start.10) | collective-permute-done | bytes 262176 | tf_op jit(solution)/shard_map/ppermute | solution.py:339
  46.4 3.2 %collective-permute-done.11.halo_b = bf16[8,128,128]{2,1,0:T(8,128)(2,1)S(1)} collective-permute-done((bf16[8,128,128]{2,1,0:T(8,128)(2,1)S(1)}, bf16[8,128,128]{2,1,0:T(8,128)(2,1)S(1)}, u32[]{:S(2)}, u32[]{:S(2)}) %collective-permute-start.11) | collective-permute-done | bytes 262176 | tf_op jit(solution)/shard_map/ppermute | solution.py:339
  49.7 2.1 %shard_map.57 = (f32[528,128]{1,0:T(8,128)S(1)}, bf16[528,128]{1,0:T(8,128)(2,1)S(1)}, bf16[528,128]{1,0:T(8,128)(2,1)S(1)}, bf16[528,128]{1,0:T(8,128)(2,1)S(1)}) custom-call(s32[8,128]{1,0:T(8,128)S(1)} %get-tuple-element.35.index_ref, f32[1,128]{1,0:T(1,128)S(1)} %get-tuple-element.36.root_ref, f32[16,128,128]{2,1,0:T(8,128)S(1)} %get-tuple-element.53.part_ref, ...), custom_call_target="tpu_custom_call" | custom-call | tf_op jit(solution)/shard_map/pallas_call | solution.py:42
  51.8 2.2 %collective-permute-start.12 = (bf16[528,128]{1,0:T(8,128)(2,1)S(1)}, bf16[528,128]{1,0:T(8,128)(2,1)S(1)}, u32[]{:S(2)}, u32[]{:S(2)}) collective-permute-start(bf16[528,128]{1,0:T(8,128)(2,1)S(1)} %get-tuple-element.56), channel_id=1, source_target_pairs={{0,16},{8,24},{16,0},{24,8},{32,48},{40,56},{48,32},{56,40},{64,80... | collective-permute-start | bytes 405512 | tf_op jit(solution)/shard_map/ppermute | solution.py:324
  54.0 1.4 %collective-permute-start.13 = (bf16[528,128]{1,0:T(8,128)(2,1)S(1)}, bf16[528,128]{1,0:T(8,128)(2,1)S(1)}, u32[]{:S(2)}, u32[]{:S(2)}) collective-permute-start(bf16[528,128]{1,0:T(8,128)(2,1)S(1)} %get-tuple-element.57), channel_id=1, source_target_pairs={{0,8},{8,0},{16,24},{24,16},{32,40},{40,32},{48,56},{56,48},{64,72... | collective-permute-start | bytes 405512 | tf_op jit(solution)/shard_map/ppermute | solution.py:324
  55.4 0.5 collective-permute-start.14
  56.0 0.0 collective-permute-done.4.halo
  56.0 4.2 %shard_map.53 = (f32[528,128]{1,0:T(8,128)S(1)}, bf16[528,128]{1,0:T(8,128)(2,1)S(1)}, bf16[528,128]{1,0:T(8,128)(2,1)S(1)}, bf16[528,128]{1,0:T(8,128)(2,1)S(1)}) custom-call(s32[8,128]{1,0:T(8,128)S(1)} %get-tuple-element.35.index_ref, f32[1,128]{1,0:T(1,128)S(1)} %get-tuple-element.36.root_ref, bf16[16,128,128]{2,1,0:T(8,128)(2,1)S(1)} %get-tuple-element.46.x, ...), custom_call_target="tpu_custom_call" | custom-call | tf_op jit(solution)/shard_map/pallas_call | solution.py:42
  60.2 2.2 %collective-permute-start.5 = (bf16[528,128]{1,0:T(8,128)(2,1)S(1)}, bf16[528,128]{1,0:T(8,128)(2,1)S(1)}, u32[]{:S(2)}, u32[]{:S(2)}) collective-permute-start(bf16[528,128]{1,0:T(8,128)(2,1)S(1)} %get-tuple-element.49), channel_id=1, source_target_pairs={{0,16},{8,24},{16,0},{24,8},{32,48},{40,56},{48,32},{56,40},{64,80... | collective-permute-start | bytes 405512 | tf_op jit(solution)/shard_map/ppermute | solution.py:324
  62.4 1.4 %collective-permute-start.6 = (bf16[528,128]{1,0:T(8,128)(2,1)S(1)}, bf16[528,128]{1,0:T(8,128)(2,1)S(1)}, u32[]{:S(2)}, u32[]{:S(2)}) collective-permute-start(bf16[528,128]{1,0:T(8,128)(2,1)S(1)} %get-tuple-element.50), channel_id=1, source_target_pairs={{0,8},{8,0},{16,24},{24,16},{32,40},{40,32},{48,56},{56,48},{64,72... | collective-permute-start | bytes 405512 | tf_op jit(solution)/shard_map/ppermute | solution.py:324
  63.8 0.0 collective-permute-done.12.refs_5_
  63.8 0.5 collective-permute-start.7
  64.4 0.0 collective-permute-done.13.refs_6_
  64.4 0.0 collective-permute-done.14.refs_7_
  64.4 2.4 %collective-permute-done.5.refs_1_ = bf16[528,128]{1,0:T(8,128)(2,1)S(1)} collective-permute-done((bf16[528,128]{1,0:T(8,128)(2,1)S(1)}, bf16[528,128]{1,0:T(8,128)(2,1)S(1)}, u32[]{:S(2)}, u32[]{:S(2)}) %collective-permute-start.5) | collective-permute-done | bytes 135200 | tf_op jit(solution)/shard_map/ppermute | solution.py:324
  66.8 1.5 %collective-permute-done.6.refs_2_ = bf16[528,128]{1,0:T(8,128)(2,1)S(1)} collective-permute-done((bf16[528,128]{1,0:T(8,128)(2,1)S(1)}, bf16[528,128]{1,0:T(8,128)(2,1)S(1)}, u32[]{:S(2)}, u32[]{:S(2)}) %collective-permute-start.6) | collective-permute-done | bytes 135200 | tf_op jit(solution)/shard_map/ppermute | solution.py:324
  68.3 0.6 collective-permute-done.7.refs_3_
  68.8 0.2 shard_map.58
  69.0 3.3 %collective-permute-start.15 = (bf16[288,128]{1,0:T(8,128)(2,1)S(1)}, bf16[288,128]{1,0:T(8,128)(2,1)S(1)}, u32[]{:S(2)}, u32[]{:S(2)}) collective-permute-start(bf16[288,128]{1,0:T(8,128)(2,1)S(1)} %get-tuple-element.60), channel_id=1, source_target_pairs={{0,64},{8,72},{16,80},{24,88},{32,96},{40,104},{48,112},{56,120},{... | collective-permute-start | bytes 221192 | tf_op jit(solution)/shard_map/ppermute | solution.py:324
  72.3 0.7 collective-permute-start.16
  73.0 0.4 collective-permute-start.17
  73.3 1.6 %collective-permute-done.15.refs_1_ = bf16[288,128]{1,0:T(8,128)(2,1)S(1)} collective-permute-done((bf16[288,128]{1,0:T(8,128)(2,1)S(1)}, bf16[288,128]{1,0:T(8,128)(2,1)S(1)}, u32[]{:S(2)}, u32[]{:S(2)}) %collective-permute-start.15) | collective-permute-done | bytes 73760 | tf_op jit(solution)/shard_map/ppermute | solution.py:324
  74.9 1.7 %collective-permute-done.16.refs_2_ = bf16[288,128]{1,0:T(8,128)(2,1)S(1)} collective-permute-done((bf16[288,128]{1,0:T(8,128)(2,1)S(1)}, bf16[288,128]{1,0:T(8,128)(2,1)S(1)}, u32[]{:S(2)}, u32[]{:S(2)}) %collective-permute-start.16) | collective-permute-done | bytes 73760 | tf_op jit(solution)/shard_map/ppermute | solution.py:324
  76.6 1.9 %collective-permute-done.17.refs_3_ = bf16[288,128]{1,0:T(8,128)(2,1)S(1)} collective-permute-done((bf16[288,128]{1,0:T(8,128)(2,1)S(1)}, bf16[288,128]{1,0:T(8,128)(2,1)S(1)}, u32[]{:S(2)}, u32[]{:S(2)}) %collective-permute-start.17) | collective-permute-done | bytes 73760 | tf_op jit(solution)/shard_map/ppermute | solution.py:324
  78.6 6.4 %collective-permute-start.18 = (bf16[144,128]{1,0:T(8,128)(2,1)S(1)}, bf16[144,128]{1,0:T(8,128)(2,1)S(1)}, u32[]{:S(2)}, u32[]{:S(2)}) collective-permute-start(bf16[144,128]{1,0:T(8,128)(2,1)S(1)} %get-tuple-element.64), channel_id=1, source_target_pairs={{0,128},{8,136},{16,144},{24,152},{32,160},{40,168},{48,176},{56,1... | collective-permute-start | bytes 110600 | tf_op jit(solution)/shard_map/ppermute | solution.py:330
  85.0 1.9 %collective-permute-done.18.received_ref = bf16[144,128]{1,0:T(8,128)(2,1)S(1)} collective-permute-done((bf16[144,128]{1,0:T(8,128)(2,1)S(1)}, bf16[144,128]{1,0:T(8,128)(2,1)S(1)}, u32[]{:S(2)}, u32[]{:S(2)}) %collective-permute-start.18) | collective-permute-done | bytes 36896 | tf_op jit(solution)/shard_map/ppermute | solution.py:330
  86.9 0.9 %shard_map.60 = f32[2,128,128]{2,1,0:T(8,128)} custom-call(f32[144,128]{1,0:T(8,128)S(1)} %get-tuple-element.63.own_ref, bf16[144,128]{1,0:T(8,128)(2,1)S(1)} %collective-permute-done.18.received_ref), custom_call_target="tpu_custom_call" | custom-call | tf_op jit(solution)/shard_map/pallas_call | solution.py:42
  (1 shorter events, 0.0 us)
Async XLA Ops:
  1.2 6.2 %collective-permute-start.2 = (bf16[16,128,128]{2,1,0:T(8,128)(2,1)S(1)}, bf16[16,128,128]{2,1,0:T(8,128)(2,1)S(1)}, u32[]{:S(2)}, u32[]{:S(2)}) collective-permute-start(bf16[16,128,128]{2,1,0:T(8,128)(2,1)S(1)} %get-tuple-element.44), channel_id=1, source_target_pairs={{0,1},{1,0},{2,3},{3,2},{4,5},{5,4},{6,7},{7,6},{8,9},{9,8},{10,11... | collective-permute-start | bytes 1572872 | tf_op jit(solution)/shard_map/ppermute | solution.py:339
  8.3 21.8 %collective-permute-start.3 = (bf16[16,128,128]{2,1,0:T(8,128)(2,1)S(1)}, bf16[16,128,128]{2,1,0:T(8,128)(2,1)S(1)}, u32[]{:S(2)}, u32[]{:S(2)}) collective-permute-start(bf16[16,128,128]{2,1,0:T(8,128)(2,1)S(1)} %shard_map.50.near.past_near), channel_id=1, source_target_pairs={{0,1},{1,0},{2,3},{3,2},{4,5},{5,4},{6,7},{7,6},{8,9},{9,8},{10,11... | collective-permute-start | bytes 1572872 | tf_op jit(solution)/shard_map/ppermute | solution.py:339
  8.9 11.0 %collective-permute-start = (bf16[8,128,128]{2,1,0:T(8,128)(2,1)S(1)}, bf16[8,128,128]{2,1,0:T(8,128)(2,1)S(1)}, u32[]{:S(2)}, u32[]{:S(2)}) collective-permute-start(bf16[8,128,128]{2,1,0:T(8,128)(2,1)S(1)} %get-tuple-element.39), channel_id=1, source_target_pairs={{1,2},{2,1},{3,4},{4,3},{5,6},{6,5},{7,0},{0,7},{9,10},{10,9},{11,... | collective-permute-start | bytes 786440 | tf_op jit(solution)/shard_map/ppermute | solution.py:339
  13.2 12.3 %collective-permute-start.1 = (bf16[8,128,128]{2,1,0:T(8,128)(2,1)S(1)}, bf16[8,128,128]{2,1,0:T(8,128)(2,1)S(1)}, u32[]{:S(2)}, u32[]{:S(2)}) collective-permute-start(bf16[8,128,128]{2,1,0:T(8,128)(2,1)S(1)} %get-tuple-element.40), channel_id=1, source_target_pairs={{1,2},{2,1},{3,4},{4,3},{5,6},{6,5},{7,0},{0,7},{9,10},{10,9},{11,... | collective-permute-start | bytes 786440 | tf_op jit(solution)/shard_map/ppermute | solution.py:339
  20.8 14.7 %collective-permute-start.8 = (bf16[8,128,128]{2,1,0:T(8,128)(2,1)S(1)}, bf16[8,128,128]{2,1,0:T(8,128)(2,1)S(1)}, u32[]{:S(2)}, u32[]{:S(2)}) collective-permute-start(bf16[8,128,128]{2,1,0:T(8,128)(2,1)S(1)} %shard_map.48.fa.pa), channel_id=1, source_target_pairs={{1,2},{2,1},{3,4},{4,3},{5,6},{6,5},{7,0},{0,7},{9,10},{10,9},{11,... | collective-permute-start | bytes 786440 | tf_op jit(solution)/shard_map/ppermute | solution.py:339
  26.4 10.7 %collective-permute-start.9 = (bf16[8,128,128]{2,1,0:T(8,128)(2,1)S(1)}, bf16[8,128,128]{2,1,0:T(8,128)(2,1)S(1)}, u32[]{:S(2)}, u32[]{:S(2)}) collective-permute-start(bf16[8,128,128]{2,1,0:T(8,128)(2,1)S(1)} %shard_map.49.fb.pb), channel_id=1, source_target_pairs={{1,2},{2,1},{3,4},{4,3},{5,6},{6,5},{7,0},{0,7},{9,10},{10,9},{11,... | collective-permute-start | bytes 786440 | tf_op jit(solution)/shard_map/ppermute | solution.py:339
  31.8 24.1 %collective-permute-start.4 = (bf16[16,128,128]{2,1,0:T(8,128)(2,1)S(1)}, bf16[16,128,128]{2,1,0:T(8,128)(2,1)S(1)}, u32[]{:S(2)}, u32[]{:S(2)}) collective-permute-start(bf16[16,128,128]{2,1,0:T(8,128)(2,1)S(1)} %shard_map.52.near), channel_id=1, source_target_pairs={{0,1},{1,0},{2,3},{3,2},{4,5},{5,4},{6,7},{7,6},{8,9},{9,8},{10,11... | collective-permute-start | bytes 1572872 | tf_op jit(solution)/shard_map/ppermute | solution.py:339
  36.4 10.1 %collective-permute-start.10 = (bf16[8,128,128]{2,1,0:T(8,128)(2,1)S(1)}, bf16[8,128,128]{2,1,0:T(8,128)(2,1)S(1)}, u32[]{:S(2)}, u32[]{:S(2)}) collective-permute-start(bf16[8,128,128]{2,1,0:T(8,128)(2,1)S(1)} %shard_map.54.fa), channel_id=1, source_target_pairs={{1,2},{2,1},{3,4},{4,3},{5,6},{6,5},{7,0},{0,7},{9,10},{10,9},{11,... | collective-permute-start | bytes 786440 | tf_op jit(solution)/shard_map/ppermute | solution.py:339
  37.9 11.8 %collective-permute-start.11 = (bf16[8,128,128]{2,1,0:T(8,128)(2,1)S(1)}, bf16[8,128,128]{2,1,0:T(8,128)(2,1)S(1)}, u32[]{:S(2)}, u32[]{:S(2)}) collective-permute-start(bf16[8,128,128]{2,1,0:T(8,128)(2,1)S(1)} %shard_map.55.fb), channel_id=1, source_target_pairs={{1,2},{2,1},{3,4},{4,3},{5,6},{6,5},{7,0},{0,7},{9,10},{10,9},{11,... | collective-permute-start | bytes 786440 | tf_op jit(solution)/shard_map/ppermute | solution.py:339
  51.8 12.1 %collective-permute-start.12 = (bf16[528,128]{1,0:T(8,128)(2,1)S(1)}, bf16[528,128]{1,0:T(8,128)(2,1)S(1)}, u32[]{:S(2)}, u32[]{:S(2)}) collective-permute-start(bf16[528,128]{1,0:T(8,128)(2,1)S(1)} %get-tuple-element.56), channel_id=1, source_target_pairs={{0,16},{8,24},{16,0},{24,8},{32,48},{40,56},{48,32},{56,40},{64,80... | collective-permute-start | bytes 405512 | tf_op jit(solution)/shard_map/ppermute | solution.py:324
  54.0 10.4 %collective-permute-start.13 = (bf16[528,128]{1,0:T(8,128)(2,1)S(1)}, bf16[528,128]{1,0:T(8,128)(2,1)S(1)}, u32[]{:S(2)}, u32[]{:S(2)}) collective-permute-start(bf16[528,128]{1,0:T(8,128)(2,1)S(1)} %get-tuple-element.57), channel_id=1, source_target_pairs={{0,8},{8,0},{16,24},{24,16},{32,40},{40,32},{48,56},{56,48},{64,72... | collective-permute-start | bytes 405512 | tf_op jit(solution)/shard_map/ppermute | solution.py:324
  55.4 9.0 %collective-permute-start.14 = (bf16[528,128]{1,0:T(8,128)(2,1)S(1)}, bf16[528,128]{1,0:T(8,128)(2,1)S(1)}, u32[]{:S(2)}, u32[]{:S(2)}) collective-permute-start(bf16[528,128]{1,0:T(8,128)(2,1)S(1)} %get-tuple-element.58), channel_id=1, source_target_pairs={{0,24},{8,16},{16,8},{24,0},{32,56},{40,48},{48,40},{56,32},{64,88... | collective-permute-start | bytes 405512 | tf_op jit(solution)/shard_map/ppermute | solution.py:324
  60.2 6.6 %collective-permute-start.5 = (bf16[528,128]{1,0:T(8,128)(2,1)S(1)}, bf16[528,128]{1,0:T(8,128)(2,1)S(1)}, u32[]{:S(2)}, u32[]{:S(2)}) collective-permute-start(bf16[528,128]{1,0:T(8,128)(2,1)S(1)} %get-tuple-element.49), channel_id=1, source_target_pairs={{0,16},{8,24},{16,0},{24,8},{32,48},{40,56},{48,32},{56,40},{64,80... | collective-permute-start | bytes 405512 | tf_op jit(solution)/shard_map/ppermute | solution.py:324
  62.4 5.9 %collective-permute-start.6 = (bf16[528,128]{1,0:T(8,128)(2,1)S(1)}, bf16[528,128]{1,0:T(8,128)(2,1)S(1)}, u32[]{:S(2)}, u32[]{:S(2)}) collective-permute-start(bf16[528,128]{1,0:T(8,128)(2,1)S(1)} %get-tuple-element.50), channel_id=1, source_target_pairs={{0,8},{8,0},{16,24},{24,16},{32,40},{40,32},{48,56},{56,48},{64,72... | collective-permute-start | bytes 405512 | tf_op jit(solution)/shard_map/ppermute | solution.py:324
  63.8 5.0 %collective-permute-start.7 = (bf16[528,128]{1,0:T(8,128)(2,1)S(1)}, bf16[528,128]{1,0:T(8,128)(2,1)S(1)}, u32[]{:S(2)}, u32[]{:S(2)}) collective-permute-start(bf16[528,128]{1,0:T(8,128)(2,1)S(1)} %get-tuple-element.51), channel_id=1, source_target_pairs={{0,24},{8,16},{16,8},{24,0},{32,56},{40,48},{48,40},{56,32},{64,88... | collective-permute-start | bytes 405512 | tf_op jit(solution)/shard_map/ppermute | solution.py:324
  69.0 5.9 %collective-permute-start.15 = (bf16[288,128]{1,0:T(8,128)(2,1)S(1)}, bf16[288,128]{1,0:T(8,128)(2,1)S(1)}, u32[]{:S(2)}, u32[]{:S(2)}) collective-permute-start(bf16[288,128]{1,0:T(8,128)(2,1)S(1)} %get-tuple-element.60), channel_id=1, source_target_pairs={{0,64},{8,72},{16,80},{24,88},{32,96},{40,104},{48,112},{56,120},{... | collective-permute-start | bytes 221192 | tf_op jit(solution)/shard_map/ppermute | solution.py:324
  72.3 4.4 %collective-permute-start.16 = (bf16[288,128]{1,0:T(8,128)(2,1)S(1)}, bf16[288,128]{1,0:T(8,128)(2,1)S(1)}, u32[]{:S(2)}, u32[]{:S(2)}) collective-permute-start(bf16[288,128]{1,0:T(8,128)(2,1)S(1)} %get-tuple-element.61), channel_id=1, source_target_pairs={{0,32},{8,40},{16,48},{24,56},{32,0},{40,8},{48,16},{56,24},{64,96... | collective-permute-start | bytes 221192 | tf_op jit(solution)/shard_map/ppermute | solution.py:324
  73.0 5.6 %collective-permute-start.17 = (bf16[288,128]{1,0:T(8,128)(2,1)S(1)}, bf16[288,128]{1,0:T(8,128)(2,1)S(1)}, u32[]{:S(2)}, u32[]{:S(2)}) collective-permute-start(bf16[288,128]{1,0:T(8,128)(2,1)S(1)} %get-tuple-element.62), channel_id=1, source_target_pairs={{0,96},{8,104},{16,112},{24,120},{32,64},{40,72},{48,80},{56,88},{... | collective-permute-start | bytes 221192 | tf_op jit(solution)/shard_map/ppermute | solution.py:324
  78.6 8.4 %collective-permute-start.18 = (bf16[144,128]{1,0:T(8,128)(2,1)S(1)}, bf16[144,128]{1,0:T(8,128)(2,1)S(1)}, u32[]{:S(2)}, u32[]{:S(2)}) collective-permute-start(bf16[144,128]{1,0:T(8,128)(2,1)S(1)} %get-tuple-element.64), channel_id=1, source_target_pairs={{0,128},{8,136},{16,144},{24,152},{32,160},{40,168},{48,176},{56,1... | collective-permute-start | bytes 110600 | tf_op jit(solution)/shard_map/ppermute | solution.py:330

commit v4 on v3

--- a/solution.py
+++ b/solution.py
@@ -37,7 +37,7 @@
     return jax.ShapeDtypeStruct(shape, dtype)
 
 
-def call(kernel, outs, scalars, arrays, scratch=(), out_specs=None, hbm=()):
+def call(kernel, outs, scalars, arrays, scratch=(), hbm=(), limit=LIMIT):
     arrays = [pltpu.with_memory_space_constraint(a, VMEM) for a in arrays]
     return pl.pallas_call(
         kernel,
@@ -45,9 +45,9 @@
         in_specs=[SMEM_SPEC] * len(scalars)
         + [VMEM_SPEC] * len(arrays)
         + [pl.BlockSpec(memory_space=pltpu.HBM)] * len(hbm),
-        out_specs=out_specs or [VMEM_SPEC] * len(outs),
+        out_specs=[VMEM_SPEC] * len(outs),
         scratch_shapes=list(scratch),
-        compiler_params=pltpu.CompilerParams(vmem_limit_bytes=LIMIT),
+        compiler_params=pltpu.CompilerParams(vmem_limit_bytes=limit),
     )(*scalars, *arrays, *[pltpu.with_memory_space_constraint(a, pltpu.HBM) for a in hbm])
 
 
@@ -107,9 +107,8 @@
 def pack(v, ref, at):
     row = lax.broadcasted_iota(jnp.int32, (HALF, NB), 0)
     col = lax.broadcasted_iota(jnp.int32, (HALF, NB), 1) - HALF
-    top, bottom = v[:HALF], v[HALF:]
-    low = gram(bottom, v)
-    high = gram(top, jnp.concatenate([bottom, top], axis=0))
+    product = gram(v, v)
+    low, high = product[HALF:], pltpu.roll(product[:HALF], HALF, 1)
     packed = jnp.where((col >= 0) & (col < row), high, low)
     ref[at * HALF : (at + 1) * HALF, :] = packed.astype(ref.dtype)
     return jnp.sum(jnp.where(col == row, high, 0.0), axis=0, keepdims=True)
@@ -131,7 +130,7 @@
     return [struct((rows, NB), F32)] + [struct((rows, NB), BF)] * 3
 
 
-def apply_row(row, first, count, index_ref, h, value, past, halo, put):
+def apply_row(row, first, count, block, value, past, halo, put):
     base = row_base(row)
 
     def element(n, carry):
@@ -147,7 +146,7 @@
             terms.append((INWARD, halo[c]))
         if row > FAR:
             terms.append((OUTWARD, value(row - 1, c)))
-        a = jnp.concatenate([h[index_ref[k, base + c]] for k, _ in terms], axis=1)
+        a = jnp.concatenate([block(base + c, k) for k, _ in terms], axis=1)
         b = jnp.concatenate([v for _, v in terms], axis=0)
         total = dot(a, b)
         if past is not None:
@@ -158,6 +157,10 @@
     lax.fori_loop(0, count, element, 0, unroll=PART)
 
 
+def sorted_block(h):
+    return lambda e, k: h[e * 5 + k]
+
+
 def putter(ref, root=None):
     def put(c, total):
         ref[c] = (total if root is None else total * root).astype(ref.dtype)
@@ -166,7 +169,8 @@
 
 
 def first_kernel(adj_hbm, occ_hbm, c_ref, h_ref, *refs):
-    index_ref, root_ref, part_ref, x_ref, y_ref, near_ref, v_ref, h, adj, occ, table, sem = refs
+    root_ref, part_ref, x_ref, y_ref, near_ref, v_ref, sorted_ref, *refs = refs
+    h, index_ref, adj, occ, table, sem = refs
     small = [
         pltpu.make_async_copy(adj_hbm, adj, sem.at[0]),
         pltpu.make_async_copy(occ_hbm, occ, sem.at[1]),
@@ -193,43 +197,54 @@
     place.wait()
     fields[0].wait()
     value = lambda row, c: v_ref[row_base(row) + c]
+
+    def block(e, k):
+        found = h[index_ref[k, e]]
+        sorted_ref[e * 5 + k] = found
+        return found
+
     for row, out in enumerate((part_ref, x_ref, y_ref, near_ref)):
         if row < NEAR:
             fields[row + 1].wait()
         for n in range(2):
             runs[2 * row + n].wait()
-            apply_row(row, n * PART, PART, index_ref, h, value, None, None, putter(out))
-
-
-def inner_kernel(rows, index_ref, x, y, near, halo, h, *refs):
+            apply_row(row, n * PART, PART, block, value, None, None, putter(out))
+            for c in range(n * PART, (n + 1) * PART):
+                if row == FAR:
+                    block(row_base(row) + c, OUTWARD)
+                if row == NEAR:
+                    block(row_base(row) + c, INWARD)
+
+
+def inner_kernel(rows, x, y, near, halo, h, *refs):
     past_ref, *outs = refs
     value = lambda row, c: (None, x, y, near)[row][c]
     past = lambda row, c: past_ref[row_base(row) + c]
     for row, out in zip(rows, outs):
-        apply_row(row, 0, EY, index_ref, h, value, past, halo, putter(out))
-
-
-def second_sweep_kernel(index_ref, fa, fb, x, y, near, h, past_ref, part_ref, x_out, y_out, far):
+        apply_row(row, 0, EY, sorted_block(h), value, past, halo, putter(out))
+
+
+def second_sweep_kernel(fa, fb, x, y, near, h, past_ref, part_ref, x_out, y_out, far):
     far[:PART] = fa[...]
     far[PART:] = fb[...]
     value = lambda row, c: (far, x, y, near)[row][c]
     past = lambda row, c: past_ref[row_base(row) + c]
     for row, out in enumerate((part_ref, x_out, y_out)):
-        apply_row(row, 0, EY, index_ref, h, value, past, None, putter(out))
-
-
-def early_kernel(index_ref, root_ref, x, y, near, halo, h, past_y, past_near, *refs):
+        apply_row(row, 0, EY, sorted_block(h), value, past, None, putter(out))
+
+
+def early_kernel(root_ref, x, y, near, halo, h, past_y, past_near, *refs):
     outs, s_ref = refs[:-1], refs[-1]
     root = root_ref[...]
     value = lambda row, c: (None, x, y, near)[row][c]
     past = lambda row, c: (None, None, past_y, past_near)[row][c]
     for row, at in ((2, odd()), (NEAR, 1 - odd())):
         put = putter(s_ref.at[pl.ds(at * EY, EY)], root)
-        apply_row(row, 0, EY, index_ref, h, value, past, halo, put)
+        apply_row(row, 0, EY, sorted_block(h), value, past, halo, put)
     pack_groups(s_ref, outs)
 
 
-def third_sweep_kernel(index_ref, root_ref, fa, fb, x, y, h, pa, pb, px, part_ref, x_out, far, pfar):
+def third_sweep_kernel(root_ref, fa, fb, x, y, h, pa, pb, px, part_ref, x_out, far, pfar):
     far[:PART] = fa[...]
     far[PART:] = fb[...]
     pfar[:PART] = pa[...]
@@ -238,10 +253,10 @@
     value = lambda row, c: (far, x, y)[row][c]
     past = lambda row, c: (pfar, px)[row][c]
     for row, out in ((FAR, putter(part_ref)), (1, putter(x_out, root))):
-        apply_row(row, 0, EY, index_ref, h, value, past, None, out)
-
-
-def last_kernel(index_ref, root_ref, part_ref, h, halo_a, halo_b, x, *refs):
+        apply_row(row, 0, EY, sorted_block(h), value, past, None, out)
+
+
+def last_kernel(root_ref, part_ref, h, halo_a, halo_b, x, *refs):
     outs, s_ref = refs[:-1], refs[-1]
     root = root_ref[...]
     base = row_base(FAR)
@@ -249,25 +264,25 @@
     s_ref[pl.ds(EY - at, EY)] = x[...]
     for first, halo in ((0, halo_a), (PART, halo_b)):
         for c in range(PART):
-            term = dot(h[index_ref[OUTWARD, base + first + c]], halo[c])
+            term = dot(h[(base + first + c) * 5 + OUTWARD], halo[c])
             s_ref[at + first + c] = ((part_ref[first + c] + 2.0 * term) * root).astype(BF)
     pack_groups(s_ref, outs)
 
 
-def edge_kernel(level, row, first, index_ref, part_ref, h, halo_ref, out_ref):
+def edge_kernel(level, row, first, part_ref, h, halo_ref, out_ref):
     scale = 1.0 if level == 1 else 2.0
     way = OUTWARD if row == FAR else INWARD
     base = row_base(row) + first
     for c in range(out_ref.shape[0]):
-        term = dot(h[index_ref[way, base + c]], halo_ref[c])
+        term = dot(h[(base + c) * 5 + way], halo_ref[c])
         out_ref[c] = (part_ref[first + c] + scale * term).astype(BF)
 
 
-def edge(level, row, first, index, part, h, halo):
+def edge(level, row, first, part, h, halo):
     return call(
         functools.partial(edge_kernel, level, row, first),
         [struct(halo.shape, BF)],
-        [index],
+        [],
         [part, h, halo],
     )[0]
 
@@ -354,60 +369,58 @@
     fa_in, fb_in = swapped(fa, 1), swapped(fb, 1)
     near_in = swapped(near, 0)
     table = struct((8, NB), jnp.int32)
-    outs = [table, struct((1, NB), F32), wide, row, row, wide, struct(coeffs.shape, BF)]
-    index, root, far, x1, y1, near, field, h = stage(
+    outs = [struct((1, NB), F32), wide, row, row, wide, struct(coeffs.shape, BF)]
+    root, far, x1, y1, near, field, h = stage(
         first_kernel,
         outs + [struct(h.shape, BF)],
         [],
         [],
         [
+            VMEM(h.shape, BF),
+            pltpu.SMEM(table.shape, jnp.int32),
             VMEM((5, EXS * EY), jnp.int32),
             VMEM((1, NB), F32),
             VMEM(table.shape, jnp.int32),
             pltpu.SemaphoreType.DMA((3 + 3 * EXS,)),
         ],
-        [SMEM_SPEC] + [VMEM_SPEC] * len(outs),
+        limit=32 << 20,
         hbm=[adjacency.T, occupation.reshape(1, NB), coeffs, h],
     )
-    near1 = edge(1, NEAR, 0, index, near, h, near_in)
+    near1 = edge(1, NEAR, 0, near, h, near_in)
     near_in = swapped(near1, 0)
-    fa1 = edge(1, FAR, 0, index, far, h, fa_in)
+    fa1 = edge(1, FAR, 0, far, h, fa_in)
     fa_in = swapped(fa1, 1)
-    fb1 = edge(1, FAR, PART, index, far, h, fb_in)
+    fb1 = edge(1, FAR, PART, far, h, fb_in)
     fb_in = swapped(fb1, 1)
     inner = functools.partial(inner_kernel, (NEAR,))
-    (near2,) = stage(inner, [row], [index], [x1, y1, near1, near_in, h, field])
+    (near2,) = stage(inner, [row], [], [x1, y1, near1, near_in, h, field])
     near_in = swapped(near2, 0)
     far, x2, y2 = stage(
-        second_sweep_kernel,
-        [wide, row, row],
-        [index],
-        [fa1, fb1, x1, y1, near1, h, field],
-        [scratch],
-    )
-    fa2 = edge(2, FAR, 0, index, far, h, fa_in)
+        second_sweep_kernel, [wide, row, row], [], [fa1, fb1, x1, y1, near1, h, field], [scratch]
+    )
+    fa2 = edge(2, FAR, 0, far, h, fa_in)
     fa_in = swapped(fa2, 1)
     early = stage(
         early_kernel,
         group_structs(WIDE),
-        [index],
+        [],
         [root, x2, y2, near2, near_in, h, y1, near1],
         [VMEM((2 * EY, NB, NB), BF)],
     )
-    fb2 = edge(2, FAR, PART, index, far, h, fb_in)
+    fb2 = edge(2, FAR, PART, far, h, fb_in)
     fb_in = swapped(fb2, 1)
     early = exchanged(early, 0)
     far, x = stage(
         third_sweep_kernel,
         [wide, row],
-        [index],
+        [],
         [root, fa2, fb2, x2, y2, h, fa1, fb1, x1],
         [scratch, scratch],
     )
     late = stage(
         last_kernel,
         group_structs(WIDE),
-        [index],
+        [],
         [root, far, h, fa_in, fb_in, x],
         [VMEM((2 * EY, NB, NB), BF)],
     )

time: 89.1 us -> 83.8 us (0.941)
  Pallas kernels: 26.7 us -> 19.7 us
  waiting for transfers between devices: 25.8 us -> 29.4 us
  starting transfers between devices: 35.2 us -> 34 us
    pallas_call x15, Pallas kernels: 26.7 us -> 19.7 us  [call(): pl.pallas_call(kernel, out_shape=outs, in_specs=[SMEM_SPEC] * len(scalars...]
    ppermute x9, waiting for transfers between devices: 14.2 us -> 17.7 us  [swapped(): return lax.ppermute(array, 'strip', pairs)]
  transfers between devices with their start and end apart: 19 -> 19, of which waited for: 12 -> 12; matrix products, arithmetic and copies ran while one was open for 0% -> 0% of each run, Pallas kernels for 27% -> 21%
where the time goes in v4:
time: 83.8 us; the launch traced here: 83.3 us
  starting transfers between devices  34 us (41%)
  waiting for transfers between devices  29.4 us (35%)
  Pallas kernels  19.7 us (24%)
    pallas_call x15, Pallas kernels, call(): pl.pallas_call(kernel, out_shape=outs, in_specs=[SMEM_SPEC] * len(scalars...  19.7 us
    ppermute x9, waiting for transfers between devices, swapped(): return lax.ppermute(array, 'strip', pairs)  17.7 us
    ppermute x9, starting transfers between devices, swapped(): return lax.ppermute(array, 'strip', pairs)  15.4 us
    ppermute x9, starting transfers between devices, exchanged(): arrived.append(lax.ppermute(pieces[s], ('band', 'strip'), pairs))  12.7 us
    ppermute x9, waiting for transfers between devices, exchanged(): arrived.append(lax.ppermute(pieces[s], ('band', 'strip'), pairs))  9.66 us
    ppermute x1, starting transfers between devices, across(): lax.ppermute(array, 'band', [(b, (b + half) % (2 * half)) for b in range(...  5.88 us
    ppermute x1, waiting for transfers between devices, across(): lax.ppermute(array, 'band', [(b, (b + half) % (2 * half)) for b in range(...  2.07 us
  transfers between devices with their start and end apart: 19, of which 12 were waited for; matrix products, arithmetic and copies ran while one was open for 0% of the time, Pallas kernels for 21%

profile of v4, /device:TPU:2, one launch (start us, length us, event | category | flops | bytes accessed | tf_op | source)
XLA Modules:
  0.0 83.3 jit_solution(5782205701567342993)
XLA Ops:
  0.0 1.2 %shard_map.47 = (bf16[8,128,128]{2,1,0:T(8,128)(2,1)S(1)}, bf16[8,128,128]{2,1,0:T(8,128)(2,1)S(1)}, bf16[16,128,128]{2,1,0:T(8,128)(2,1)S(1)}) custom-call(bf16[64,128,128]{2,1,0:T(8,128)(2,1)} %c_ref.3), custom_call_target="tpu_custom_call" | custom-call | tf_op jit(solution)/shard_map/pallas_call | solution.py:42
  1.2 0.1 collective-permute-start.2
  1.3 6.2 %shard_map.46 = (f32[1,128]{1,0:T(1,128)S(1)}, f32[16,128,128]{2,1,0:T(8,128)S(1)}, bf16[16,128,128]{2,1,0:T(8,128)(2,1)S(1)}, bf16[16,128,128]{2,1,0:T(8,128)(2...) custom-call(s32[5,64]{1,0:T(8,128)} %bitcast.4, ...), custom_call_target="tpu_custom_call" | custom-call | tf_op jit(solution)/shard_map/pallas_call | solution.py:42
  7.5 0.0 collective-permute-done.2.halo_ref
  7.5 0.3 shard_map.50.near.past_near
  7.8 0.6 collective-permute-start.3
  8.4 4.3 %collective-permute-start = (bf16[8,128,128]{2,1,0:T(8,128)(2,1)S(1)}, bf16[8,128,128]{2,1,0:T(8,128)(2,1)S(1)}, u32[]{:S(2)}, u32[]{:S(2)}) collective-permute-start(bf16[8,128,128]{2,1,0:T(8,128)(2,1)S(1)} %get-tuple-element.37), channel_id=1, source_target_pairs={{1,2},{2,1},{3,4},{4,3},{5,6},{6,5},{7,0},{0,7},{9,10},{10,9},{11,... | collective-permute-start | bytes 786440 | tf_op jit(solution)/shard_map/ppermute | solution.py:354
  12.7 0.1 collective-permute-start.1
  12.8 6.6 %collective-permute-done.halo_ref = bf16[8,128,128]{2,1,0:T(8,128)(2,1)S(1)} collective-permute-done((bf16[8,128,128]{2,1,0:T(8,128)(2,1)S(1)}, bf16[8,128,128]{2,1,0:T(8,128)(2,1)S(1)}, u32[]{:S(2)}, u32[]{:S(2)}) %collective-permute-start) | collective-permute-done | bytes 262176 | tf_op jit(solution)/shard_map/ppermute | solution.py:354
  19.4 0.2 shard_map.48.fa.pa
  19.6 3.8 %collective-permute-start.8 = (bf16[8,128,128]{2,1,0:T(8,128)(2,1)S(1)}, bf16[8,128,128]{2,1,0:T(8,128)(2,1)S(1)}, u32[]{:S(2)}, u32[]{:S(2)}) collective-permute-start(bf16[8,128,128]{2,1,0:T(8,128)(2,1)S(1)} %shard_map.48.fa.pa), channel_id=1, source_target_pairs={{1,2},{2,1},{3,4},{4,3},{5,6},{6,5},{7,0},{0,7},{9,10},{10,9},{11,... | collective-permute-start | bytes 786440 | tf_op jit(solution)/shard_map/ppermute | solution.py:354
  23.4 1.6 %collective-permute-done.1.halo_ref = bf16[8,128,128]{2,1,0:T(8,128)(2,1)S(1)} collective-permute-done((bf16[8,128,128]{2,1,0:T(8,128)(2,1)S(1)}, bf16[8,128,128]{2,1,0:T(8,128)(2,1)S(1)}, u32[]{:S(2)}, u32[]{:S(2)}) %collective-permute-start.1) | collective-permute-done | bytes 262176 | tf_op jit(solution)/shard_map/ppermute | solution.py:354
  25.0 0.2 shard_map.49.fb.pb
  25.3 3.8 %collective-permute-start.9 = (bf16[8,128,128]{2,1,0:T(8,128)(2,1)S(1)}, bf16[8,128,128]{2,1,0:T(8,128)(2,1)S(1)}, u32[]{:S(2)}, u32[]{:S(2)}) collective-permute-start(bf16[8,128,128]{2,1,0:T(8,128)(2,1)S(1)} %shard_map.49.fb.pb), channel_id=1, source_target_pairs={{1,2},{2,1},{3,4},{4,3},{5,6},{6,5},{7,0},{0,7},{9,10},{10,9},{11,... | collective-permute-start | bytes 786440 | tf_op jit(solution)/shard_map/ppermute | solution.py:354
  29.0 0.0 collective-permute-done.3.halo
  29.1 1.0 %shard_map.52.near = bf16[16,128,128]{2,1,0:T(8,128)(2,1)S(1)} custom-call(bf16[16,128,128]{2,1,0:T(8,128)(2,1)S(1)} %get-tuple-element.39.x.px, bf16[16,128,128]{2,1,0:T(8,128)(2,1)S(1)} %get-tuple-element.40.y.past_y, bf16[16,128,128]{2,1,0:T(8,128)(2,1)S(1)} %shard_map.50.near.past_near, bf16[16,128,128]{2,1,0:T(8,128)(2,1)S(1)} %collective-permute-done.3.halo, ...), custom_call_target="tpu_custom_call" | custom-call | tf_op jit(solution)/shard_map/pallas_call | solution.py:42
  30.1 0.1 collective-permute-start.4
  30.2 2.9 %shard_map.51 = (f32[16,128,128]{2,1,0:T(8,128)S(1)}, bf16[16,128,128]{2,1,0:T(8,128)(2,1)S(1)}, bf16[16,128,128]{2,1,0:T(8,128)(2,1)S(1)}) custom-call(bf16[8,128,128]{2,1,0:T(8,128)(2,1)S(1)} %shard_map.48.fa.pa, bf16[8,128,128]{2,1,0:T(8,128)(2,1)S(1)} %shard_map.49.fb.pb, bf16[16,128,128]{2,1,0:T(8,128)(2,1)S(1)} %get-tuple-element.39.x.px, ...), custom_call_target="tpu_custom_call" | custom-call | tf_op jit(solution)/shard_map/pallas_call | solution.py:42
  33.2 0.0 collective-permute-done.8.halo_ref
  33.2 0.2 shard_map.54.fa
  33.4 1.2 %collective-permute-start.10 = (bf16[8,128,128]{2,1,0:T(8,128)(2,1)S(1)}, bf16[8,128,128]{2,1,0:T(8,128)(2,1)S(1)}, u32[]{:S(2)}, u32[]{:S(2)}) collective-permute-start(bf16[8,128,128]{2,1,0:T(8,128)(2,1)S(1)} %shard_map.54.fa), channel_id=1, source_target_pairs={{1,2},{2,1},{3,4},{4,3},{5,6},{6,5},{7,0},{0,7},{9,10},{10,9},{11,... | collective-permute-start | bytes 786440 | tf_op jit(solution)/shard_map/ppermute | solution.py:354
  34.6 1.3 %collective-permute-done.9.halo_ref = bf16[8,128,128]{2,1,0:T(8,128)(2,1)S(1)} collective-permute-done((bf16[8,128,128]{2,1,0:T(8,128)(2,1)S(1)}, bf16[8,128,128]{2,1,0:T(8,128)(2,1)S(1)}, u32[]{:S(2)}, u32[]{:S(2)}) %collective-permute-start.9) | collective-permute-done | bytes 262176 | tf_op jit(solution)/shard_map/ppermute | solution.py:354
  35.9 0.2 shard_map.55.fb
  36.1 1.4 %collective-permute-start.11 = (bf16[8,128,128]{2,1,0:T(8,128)(2,1)S(1)}, bf16[8,128,128]{2,1,0:T(8,128)(2,1)S(1)}, u32[]{:S(2)}, u32[]{:S(2)}) collective-permute-start(bf16[8,128,128]{2,1,0:T(8,128)(2,1)S(1)} %shard_map.55.fb), channel_id=1, source_target_pairs={{1,2},{2,1},{3,4},{4,3},{5,6},{6,5},{7,0},{0,7},{9,10},{10,9},{11,... | collective-permute-start | bytes 786440 | tf_op jit(solution)/shard_map/ppermute | solution.py:354
  37.6 2.0 %shard_map.56 = (f32[16,128,128]{2,1,0:T(8,128)S(1)}, bf16[16,128,128]{2,1,0:T(8,128)(2,1)S(1)}) custom-call(f32[1,128]{1,0:T(1,128)S(1)} %get-tuple-element.34.root_ref, bf16[8,128,128]{2,1,0:T(8,128)(2,1)S(1)} %shard_map.54.fa, bf16[8,128,128]{2,1,0:T(8,128)(2,1)S(1)} %shard_map.55.fb, bf16[16,128,128]{2,1,0:T(8,128)(2,1)S(1)} %get-tuple-element.44.x, ...), custom_call_target="tpu_custom_call" | custom-call | tf_op jit(solution)/shard_map/pallas_call | solution.py:42
  39.5 4.1 %collective-permute-done.10.halo_a = bf16[8,128,128]{2,1,0:T(8,128)(2,1)S(1)} collective-permute-done((bf16[8,128,128]{2,1,0:T(8,128)(2,1)S(1)}, bf16[8,128,128]{2,1,0:T(8,128)(2,1)S(1)}, u32[]{:S(2)}, u32[]{:S(2)}) %collective-permute-start.10) | collective-permute-done | bytes 262176 | tf_op jit(solution)/shard_map/ppermute | solution.py:354
  43.6 4.1 %collective-permute-done.11.halo_b = bf16[8,128,128]{2,1,0:T(8,128)(2,1)S(1)} collective-permute-done((bf16[8,128,128]{2,1,0:T(8,128)(2,1)S(1)}, bf16[8,128,128]{2,1,0:T(8,128)(2,1)S(1)}, u32[]{:S(2)}, u32[]{:S(2)}) %collective-permute-start.11) | collective-permute-done | bytes 262176 | tf_op jit(solution)/shard_map/ppermute | solution.py:354
  47.7 1.2 %shard_map.57 = (f32[528,128]{1,0:T(8,128)S(1)}, bf16[528,128]{1,0:T(8,128)(2,1)S(1)}, bf16[528,128]{1,0:T(8,128)(2,1)S(1)}, bf16[528,128]{1,0:T(8,128)(2,1)S(1)}) custom-call(f32[1,128]{1,0:T(1,128)S(1)} %get-tuple-element.34.root_ref, f32[16,128,128]{2,1,0:T(8,128)S(1)} %get-tuple-element.51.part_ref, bf16[320,128,128]{2,1,0:T(8,128)(2,1)S(1)} %get-tuple-element.36.h, ...), custom_call_target="tpu_custom_call" | custom-call | tf_op jit(solution)/shard_map/pallas_call | solution.py:42
  48.9 2.2 %collective-permute-start.12 = (bf16[528,128]{1,0:T(8,128)(2,1)S(1)}, bf16[528,128]{1,0:T(8,128)(2,1)S(1)}, u32[]{:S(2)}, u32[]{:S(2)}) collective-permute-start(bf16[528,128]{1,0:T(8,128)(2,1)S(1)} %get-tuple-element.54), channel_id=1, source_target_pairs={{0,16},{8,24},{16,0},{24,8},{32,48},{40,56},{48,32},{56,40},{64,80... | collective-permute-start | bytes 405512 | tf_op jit(solution)/shard_map/ppermute | solution.py:339
  51.1 1.4 %collective-permute-start.13 = (bf16[528,128]{1,0:T(8,128)(2,1)S(1)}, bf16[528,128]{1,0:T(8,128)(2,1)S(1)}, u32[]{:S(2)}, u32[]{:S(2)}) collective-permute-start(bf16[528,128]{1,0:T(8,128)(2,1)S(1)} %get-tuple-element.55), channel_id=1, source_target_pairs={{0,8},{8,0},{16,24},{24,16},{32,40},{40,32},{48,56},{56,48},{64,72... | collective-permute-start | bytes 405512 | tf_op jit(solution)/shard_map/ppermute | solution.py:339
  52.5 0.5 collective-permute-start.14
  53.1 0.0 collective-permute-done.4.halo
  53.1 3.0 %shard_map.53 = (f32[528,128]{1,0:T(8,128)S(1)}, bf16[528,128]{1,0:T(8,128)(2,1)S(1)}, bf16[528,128]{1,0:T(8,128)(2,1)S(1)}, bf16[528,128]{1,0:T(8,128)(2,1)S(1)}) custom-call(f32[1,128]{1,0:T(1,128)S(1)} %get-tuple-element.34.root_ref, bf16[16,128,128]{2,1,0:T(8,128)(2,1)S(1)} %get-tuple-element.44.x, bf16[16,128,128]{2,1,0:T(8,128)(2,1)S(1)} %get-tuple-element.45.y, ...), custom_call_target="tpu_custom_call" | custom-call | tf_op jit(solution)/shard_map/pallas_call | solution.py:42
  56.1 2.2 %collective-permute-start.5 = (bf16[528,128]{1,0:T(8,128)(2,1)S(1)}, bf16[528,128]{1,0:T(8,128)(2,1)S(1)}, u32[]{:S(2)}, u32[]{:S(2)}) collective-permute-start(bf16[528,128]{1,0:T(8,128)(2,1)S(1)} %get-tuple-element.47), channel_id=1, source_target_pairs={{0,16},{8,24},{16,0},{24,8},{32,48},{40,56},{48,32},{56,40},{64,80... | collective-permute-start | bytes 405512 | tf_op jit(solution)/shard_map/ppermute | solution.py:339
  58.3 1.4 %collective-permute-start.6 = (bf16[528,128]{1,0:T(8,128)(2,1)S(1)}, bf16[528,128]{1,0:T(8,128)(2,1)S(1)}, u32[]{:S(2)}, u32[]{:S(2)}) collective-permute-start(bf16[528,128]{1,0:T(8,128)(2,1)S(1)} %get-tuple-element.48), channel_id=1, source_target_pairs={{0,8},{8,0},{16,24},{24,16},{32,40},{40,32},{48,56},{56,48},{64,72... | collective-permute-start | bytes 405512 | tf_op jit(solution)/shard_map/ppermute | solution.py:339
  59.7 0.0 collective-permute-done.12.refs_5_
  59.7 0.5 collective-permute-start.7
  60.2 0.0 collective-permute-done.13.refs_6_
  60.2 0.0 collective-permute-done.14.refs_7_
  60.2 2.4 %collective-permute-done.5.refs_1_ = bf16[528,128]{1,0:T(8,128)(2,1)S(1)} collective-permute-done((bf16[528,128]{1,0:T(8,128)(2,1)S(1)}, bf16[528,128]{1,0:T(8,128)(2,1)S(1)}, u32[]{:S(2)}, u32[]{:S(2)}) %collective-permute-start.5) | collective-permute-done | bytes 135200 | tf_op jit(solution)/shard_map/ppermute | solution.py:339
  62.7 1.5 %collective-permute-done.6.refs_2_ = bf16[528,128]{1,0:T(8,128)(2,1)S(1)} collective-permute-done((bf16[528,128]{1,0:T(8,128)(2,1)S(1)}, bf16[528,128]{1,0:T(8,128)(2,1)S(1)}, u32[]{:S(2)}, u32[]{:S(2)}) %collective-permute-start.6) | collective-permute-done | bytes 135200 | tf_op jit(solution)/shard_map/ppermute | solution.py:339
  64.1 0.6 collective-permute-done.7.refs_3_
  64.7 0.1 shard_map.58
  64.9 3.3 %collective-permute-start.15 = (bf16[288,128]{1,0:T(8,128)(2,1)S(1)}, bf16[288,128]{1,0:T(8,128)(2,1)S(1)}, u32[]{:S(2)}, u32[]{:S(2)}) collective-permute-start(bf16[288,128]{1,0:T(8,128)(2,1)S(1)} %get-tuple-element.58), channel_id=1, source_target_pairs={{0,64},{8,72},{16,80},{24,88},{32,96},{40,104},{48,112},{56,120},{... | collective-permute-start | bytes 221192 | tf_op jit(solution)/shard_map/ppermute | solution.py:339
  68.1 0.7 collective-permute-start.16
  68.8 0.4 collective-permute-start.17
  69.2 1.6 %collective-permute-done.15.refs_1_ = bf16[288,128]{1,0:T(8,128)(2,1)S(1)} collective-permute-done((bf16[288,128]{1,0:T(8,128)(2,1)S(1)}, bf16[288,128]{1,0:T(8,128)(2,1)S(1)}, u32[]{:S(2)}, u32[]{:S(2)}) %collective-permute-start.15) | collective-permute-done | bytes 73760 | tf_op jit(solution)/shard_map/ppermute | solution.py:339
  70.8 1.7 %collective-permute-done.16.refs_2_ = bf16[288,128]{1,0:T(8,128)(2,1)S(1)} collective-permute-done((bf16[288,128]{1,0:T(8,128)(2,1)S(1)}, bf16[288,128]{1,0:T(8,128)(2,1)S(1)}, u32[]{:S(2)}, u32[]{:S(2)}) %collective-permute-start.16) | collective-permute-done | bytes 73760 | tf_op jit(solution)/shard_map/ppermute | solution.py:339
  72.5 1.9 %collective-permute-done.17.refs_3_ = bf16[288,128]{1,0:T(8,128)(2,1)S(1)} collective-permute-done((bf16[288,128]{1,0:T(8,128)(2,1)S(1)}, bf16[288,128]{1,0:T(8,128)(2,1)S(1)}, u32[]{:S(2)}, u32[]{:S(2)}) %collective-permute-start.17) | collective-permute-done | bytes 73760 | tf_op jit(solution)/shard_map/ppermute | solution.py:339
  74.4 5.9 %collective-permute-start.18 = (bf16[144,128]{1,0:T(8,128)(2,1)S(1)}, bf16[144,128]{1,0:T(8,128)(2,1)S(1)}, u32[]{:S(2)}, u32[]{:S(2)}) collective-permute-start(bf16[144,128]{1,0:T(8,128)(2,1)S(1)} %get-tuple-element.62), channel_id=1, source_target_pairs={{0,128},{8,136},{16,144},{24,152},{32,160},{40,168},{48,176},{56,1... | collective-permute-start | bytes 110600 | tf_op jit(solution)/shard_map/ppermute | solution.py:345
  80.3 2.1 %collective-permute-done.18.received_ref = bf16[144,128]{1,0:T(8,128)(2,1)S(1)} collective-permute-done((bf16[144,128]{1,0:T(8,128)(2,1)S(1)}, bf16[144,128]{1,0:T(8,128)(2,1)S(1)}, u32[]{:S(2)}, u32[]{:S(2)}) %collective-permute-start.18) | collective-permute-done | bytes 36896 | tf_op jit(solution)/shard_map/ppermute | solution.py:345
  82.4 0.9 %shard_map.60 = f32[2,128,128]{2,1,0:T(8,128)} custom-call(f32[144,128]{1,0:T(8,128)S(1)} %get-tuple-element.61.own_ref, bf16[144,128]{1,0:T(8,128)(2,1)S(1)} %collective-permute-done.18.received_ref), custom_call_target="tpu_custom_call" | custom-call | tf_op jit(solution)/shard_map/pallas_call | solution.py:42
  (1 shorter events, 0.0 us)
Async XLA Ops:
  1.2 6.3 %collective-permute-start.2 = (bf16[16,128,128]{2,1,0:T(8,128)(2,1)S(1)}, bf16[16,128,128]{2,1,0:T(8,128)(2,1)S(1)}, u32[]{:S(2)}, u32[]{:S(2)}) collective-permute-start(bf16[16,128,128]{2,1,0:T(8,128)(2,1)S(1)} %get-tuple-element.42), channel_id=1, source_target_pairs={{0,1},{1,0},{2,3},{3,2},{4,5},{5,4},{6,7},{7,6},{8,9},{9,8},{10,11... | collective-permute-start | bytes 1572872 | tf_op jit(solution)/shard_map/ppermute | solution.py:354
  7.8 21.2 %collective-permute-start.3 = (bf16[16,128,128]{2,1,0:T(8,128)(2,1)S(1)}, bf16[16,128,128]{2,1,0:T(8,128)(2,1)S(1)}, u32[]{:S(2)}, u32[]{:S(2)}) collective-permute-start(bf16[16,128,128]{2,1,0:T(8,128)(2,1)S(1)} %shard_map.50.near.past_near), channel_id=1, source_target_pairs={{0,1},{1,0},{2,3},{3,2},{4,5},{5,4},{6,7},{7,6},{8,9},{9,8},{10,11... | collective-permute-start | bytes 1572872 | tf_op jit(solution)/shard_map/ppermute | solution.py:354
  8.4 11.0 %collective-permute-start = (bf16[8,128,128]{2,1,0:T(8,128)(2,1)S(1)}, bf16[8,128,128]{2,1,0:T(8,128)(2,1)S(1)}, u32[]{:S(2)}, u32[]{:S(2)}) collective-permute-start(bf16[8,128,128]{2,1,0:T(8,128)(2,1)S(1)} %get-tuple-element.37), channel_id=1, source_target_pairs={{1,2},{2,1},{3,4},{4,3},{5,6},{6,5},{7,0},{0,7},{9,10},{10,9},{11,... | collective-permute-start | bytes 786440 | tf_op jit(solution)/shard_map/ppermute | solution.py:354
  12.7 12.3 %collective-permute-start.1 = (bf16[8,128,128]{2,1,0:T(8,128)(2,1)S(1)}, bf16[8,128,128]{2,1,0:T(8,128)(2,1)S(1)}, u32[]{:S(2)}, u32[]{:S(2)}) collective-permute-start(bf16[8,128,128]{2,1,0:T(8,128)(2,1)S(1)} %get-tuple-element.38), channel_id=1, source_target_pairs={{1,2},{2,1},{3,4},{4,3},{5,6},{6,5},{7,0},{0,7},{9,10},{10,9},{11,... | collective-permute-start | bytes 786440 | tf_op jit(solution)/shard_map/ppermute | solution.py:354
  19.6 13.5 %collective-permute-start.8 = (bf16[8,128,128]{2,1,0:T(8,128)(2,1)S(1)}, bf16[8,128,128]{2,1,0:T(8,128)(2,1)S(1)}, u32[]{:S(2)}, u32[]{:S(2)}) collective-permute-start(bf16[8,128,128]{2,1,0:T(8,128)(2,1)S(1)} %shard_map.48.fa.pa), channel_id=1, source_target_pairs={{1,2},{2,1},{3,4},{4,3},{5,6},{6,5},{7,0},{0,7},{9,10},{10,9},{11,... | collective-permute-start | bytes 786440 | tf_op jit(solution)/shard_map/ppermute | solution.py:354
  25.3 10.7 %collective-permute-start.9 = (bf16[8,128,128]{2,1,0:T(8,128)(2,1)S(1)}, bf16[8,128,128]{2,1,0:T(8,128)(2,1)S(1)}, u32[]{:S(2)}, u32[]{:S(2)}) collective-permute-start(bf16[8,128,128]{2,1,0:T(8,128)(2,1)S(1)} %shard_map.49.fb.pb), channel_id=1, source_target_pairs={{1,2},{2,1},{3,4},{4,3},{5,6},{6,5},{7,0},{0,7},{9,10},{10,9},{11,... | collective-permute-start | bytes 786440 | tf_op jit(solution)/shard_map/ppermute | solution.py:354
  30.1 23.0 %collective-permute-start.4 = (bf16[16,128,128]{2,1,0:T(8,128)(2,1)S(1)}, bf16[16,128,128]{2,1,0:T(8,128)(2,1)S(1)}, u32[]{:S(2)}, u32[]{:S(2)}) collective-permute-start(bf16[16,128,128]{2,1,0:T(8,128)(2,1)S(1)} %shard_map.52.near), channel_id=1, source_target_pairs={{0,1},{1,0},{2,3},{3,2},{4,5},{5,4},{6,7},{7,6},{8,9},{9,8},{10,11... | collective-permute-start | bytes 1572872 | tf_op jit(solution)/shard_map/ppermute | solution.py:354
  33.4 10.2 %collective-permute-start.10 = (bf16[8,128,128]{2,1,0:T(8,128)(2,1)S(1)}, bf16[8,128,128]{2,1,0:T(8,128)(2,1)S(1)}, u32[]{:S(2)}, u32[]{:S(2)}) collective-permute-start(bf16[8,128,128]{2,1,0:T(8,128)(2,1)S(1)} %shard_map.54.fa), channel_id=1, source_target_pairs={{1,2},{2,1},{3,4},{4,3},{5,6},{6,5},{7,0},{0,7},{9,10},{10,9},{11,... | collective-permute-start | bytes 786440 | tf_op jit(solution)/shard_map/ppermute | solution.py:354
  36.1 11.5 %collective-permute-start.11 = (bf16[8,128,128]{2,1,0:T(8,128)(2,1)S(1)}, bf16[8,128,128]{2,1,0:T(8,128)(2,1)S(1)}, u32[]{:S(2)}, u32[]{:S(2)}) collective-permute-start(bf16[8,128,128]{2,1,0:T(8,128)(2,1)S(1)} %shard_map.55.fb), channel_id=1, source_target_pairs={{1,2},{2,1},{3,4},{4,3},{5,6},{6,5},{7,0},{0,7},{9,10},{10,9},{11,... | collective-permute-start | bytes 786440 | tf_op jit(solution)/shard_map/ppermute | solution.py:354
  48.9 10.8 %collective-permute-start.12 = (bf16[528,128]{1,0:T(8,128)(2,1)S(1)}, bf16[528,128]{1,0:T(8,128)(2,1)S(1)}, u32[]{:S(2)}, u32[]{:S(2)}) collective-permute-start(bf16[528,128]{1,0:T(8,128)(2,1)S(1)} %get-tuple-element.54), channel_id=1, source_target_pairs={{0,16},{8,24},{16,0},{24,8},{32,48},{40,56},{48,32},{56,40},{64,80... | collective-permute-start | bytes 405512 | tf_op jit(solution)/shard_map/ppermute | solution.py:339
  51.1 9.1 %collective-permute-start.13 = (bf16[528,128]{1,0:T(8,128)(2,1)S(1)}, bf16[528,128]{1,0:T(8,128)(2,1)S(1)}, u32[]{:S(2)}, u32[]{:S(2)}) collective-permute-start(bf16[528,128]{1,0:T(8,128)(2,1)S(1)} %get-tuple-element.55), channel_id=1, source_target_pairs={{0,8},{8,0},{16,24},{24,16},{32,40},{40,32},{48,56},{56,48},{64,72... | collective-permute-start | bytes 405512 | tf_op jit(solution)/shard_map/ppermute | solution.py:339
  52.5 7.7 %collective-permute-start.14 = (bf16[528,128]{1,0:T(8,128)(2,1)S(1)}, bf16[528,128]{1,0:T(8,128)(2,1)S(1)}, u32[]{:S(2)}, u32[]{:S(2)}) collective-permute-start(bf16[528,128]{1,0:T(8,128)(2,1)S(1)} %get-tuple-element.56), channel_id=1, source_target_pairs={{0,24},{8,16},{16,8},{24,0},{32,56},{40,48},{48,40},{56,32},{64,88... | collective-permute-start | bytes 405512 | tf_op jit(solution)/shard_map/ppermute | solution.py:339
  56.1 6.6 %collective-permute-start.5 = (bf16[528,128]{1,0:T(8,128)(2,1)S(1)}, bf16[528,128]{1,0:T(8,128)(2,1)S(1)}, u32[]{:S(2)}, u32[]{:S(2)}) collective-permute-start(bf16[528,128]{1,0:T(8,128)(2,1)S(1)} %get-tuple-element.47), channel_id=1, source_target_pairs={{0,16},{8,24},{16,0},{24,8},{32,48},{40,56},{48,32},{56,40},{64,80... | collective-permute-start | bytes 405512 | tf_op jit(solution)/shard_map/ppermute | solution.py:339
  58.3 5.9 %collective-permute-start.6 = (bf16[528,128]{1,0:T(8,128)(2,1)S(1)}, bf16[528,128]{1,0:T(8,128)(2,1)S(1)}, u32[]{:S(2)}, u32[]{:S(2)}) collective-permute-start(bf16[528,128]{1,0:T(8,128)(2,1)S(1)} %get-tuple-element.48), channel_id=1, source_target_pairs={{0,8},{8,0},{16,24},{24,16},{32,40},{40,32},{48,56},{56,48},{64,72... | collective-permute-start | bytes 405512 | tf_op jit(solution)/shard_map/ppermute | solution.py:339
  59.7 5.0 %collective-permute-start.7 = (bf16[528,128]{1,0:T(8,128)(2,1)S(1)}, bf16[528,128]{1,0:T(8,128)(2,1)S(1)}, u32[]{:S(2)}, u32[]{:S(2)}) collective-permute-start(bf16[528,128]{1,0:T(8,128)(2,1)S(1)} %get-tuple-element.49), channel_id=1, source_target_pairs={{0,24},{8,16},{16,8},{24,0},{32,56},{40,48},{48,40},{56,32},{64,88... | collective-permute-start | bytes 405512 | tf_op jit(solution)/shard_map/ppermute | solution.py:339
  64.9 5.9 %collective-permute-start.15 = (bf16[288,128]{1,0:T(8,128)(2,1)S(1)}, bf16[288,128]{1,0:T(8,128)(2,1)S(1)}, u32[]{:S(2)}, u32[]{:S(2)}) collective-permute-start(bf16[288,128]{1,0:T(8,128)(2,1)S(1)} %get-tuple-element.58), channel_id=1, source_target_pairs={{0,64},{8,72},{16,80},{24,88},{32,96},{40,104},{48,112},{56,120},{... | collective-permute-start | bytes 221192 | tf_op jit(solution)/shard_map/ppermute | solution.py:339
  68.1 4.4 %collective-permute-start.16 = (bf16[288,128]{1,0:T(8,128)(2,1)S(1)}, bf16[288,128]{1,0:T(8,128)(2,1)S(1)}, u32[]{:S(2)}, u32[]{:S(2)}) collective-permute-start(bf16[288,128]{1,0:T(8,128)(2,1)S(1)} %get-tuple-element.59), channel_id=1, source_target_pairs={{0,32},{8,40},{16,48},{24,56},{32,0},{40,8},{48,16},{56,24},{64,96... | collective-permute-start | bytes 221192 | tf_op jit(solution)/shard_map/ppermute | solution.py:339
  68.8 5.6 %collective-permute-start.17 = (bf16[288,128]{1,0:T(8,128)(2,1)S(1)}, bf16[288,128]{1,0:T(8,128)(2,1)S(1)}, u32[]{:S(2)}, u32[]{:S(2)}) collective-permute-start(bf16[288,128]{1,0:T(8,128)(2,1)S(1)} %get-tuple-element.60), channel_id=1, source_target_pairs={{0,96},{8,104},{16,112},{24,120},{32,64},{40,72},{48,80},{56,88},{... | collective-permute-start | bytes 221192 | tf_op jit(solution)/shard_map/ppermute | solution.py:339
  74.4 8.0 %collective-permute-start.18 = (bf16[144,128]{1,0:T(8,128)(2,1)S(1)}, bf16[144,128]{1,0:T(8,128)(2,1)S(1)}, u32[]{:S(2)}, u32[]{:S(2)}) collective-permute-start(bf16[144,128]{1,0:T(8,128)(2,1)S(1)} %get-tuple-element.62), channel_id=1, source_target_pairs={{0,128},{8,136},{16,144},{24,152},{32,160},{40,168},{48,176},{56,1... | collective-permute-start | bytes 110600 | tf_op jit(solution)/shard_map/ppermute | solution.py:345
